TPU v7x, 32 devices: a whole 2x2x4 slice. The times are simulated.
32 devices in a mesh: gx: 8 (over z, x), gy: 4 (over y, core).
Axes of the slice: x: 2, y: 2, z: 4, core: 2. Of those that a mesh axis runs over, the one named last changes fastest.
Arguments:
- coarse_state: float32 [5, 256, 1024], P(None, 'gx', 'gy'), may hold values from -6 to 6
- fine_state: float32 [32, 5, 32, 512], P(('gx', 'gy')), may hold values from -6 to 6
- slot_site: int32 [32, 2], P(('gx', 'gy')), may hold values from 0 to 3, as said below
- box_live: int32 [32], P(('gx', 'gy')), may hold values 0 or 1
Outputs:
- coarse_out: float32 [5, 256, 1024], P(None, 'gx', 'gy')
- fine_out: float32 [32, 5, 32, 512], P(('gx', 'gy'))
Inputs may be any that keep to these rules, and one draw needn't show every extreme that they name: `slot_site`: within each group of 4 devices that share a gx index, slots of the group and box positions of the group's coarse blocks are matched one to one; column 0 is the gy index of the block, column 1 the position number, 0 to 0.
All inputs are finite; a program needn't handle non-finite values. No bound on the sum of `box_live` on one device may be relied on, other than what follows from the above.
Results may differ from a plain program's by a relative error of at most 0.000088.
Values sent between devices are 32-bit elements; how exact they have to be, the bound alone decides.
No kernel may reach another device: no remote copies, remote signals or barrier semaphores. Data moves between devices by JAX's collectives and lax.ppermute only.
A program may use at most 64 MiB of HBM per device.

v0:
```python
from functools import partial

import jax
import jax.numpy as jnp
from jax import lax
from jax.experimental import pallas as pl
from jax.experimental.pallas import tpu as pltpu
from jax.sharding import PartitionSpec as P

LANES = 128
SUB = 8
PAD = 8

courant = 0.2
drift = (0.5, 0.3, 0.2)
signal = (1.5, 1.3, 1.2)
PLUS = tuple(0.5 * (a + s) for a, s in zip(drift, signal))
MINUS = tuple(0.5 * (a - s) for a, s in zip(drift, signal))

NVAR = 5
VMEM = pltpu.VMEM


def minmod(first, second):
    return jnp.maximum(jnp.minimum(first, second), jnp.minimum(jnp.maximum(first, second), 0.0))


def lanes_of(rows=SUB):
    return lax.broadcasted_iota(jnp.int32, (rows, LANES), 1)


def roll(values, step):
    step = step % LANES
    return values if step == 0 else pltpu.roll(values, step, 1)


def take(values, index):
    return jnp.take_along_axis(values, index, axis=1, mode="promise_in_bounds")


def coupled(direction):
    return {0: 1 + direction, 1 + direction: 4, 4: 1 + direction}


def add_jumps(acc, direction, jumps):
    couples = coupled(direction)
    for v in range(NVAR):
        left, right = jumps(v)
        for t in range(len(left)):
            term = (courant * PLUS[direction]) * left[t] + (courant * MINUS[direction]) * right[t]
            acc[v][t] = term if acc[v][t] is None else acc[v][t] + term
        targets = [w for w in couples if couples[w] == v]
        if targets:
            for t in range(len(left)):
                shared = (0.5 * courant) * (left[t] + right[t])
                for w in targets:
                    acc[w][t] = shared if acc[w][t] is None else acc[w][t] + shared


def flux_of(left, right, direction):
    couples = coupled(direction)
    out = []
    for v in range(NVAR):
        flux = PLUS[direction] * left[v] + MINUS[direction] * right[v]
        if v in couples:
            w = couples[v]
            flux = flux + 0.5 * (left[w] + right[w])
        out.append(flux)
    return out


class Level:
    def __init__(self, q, slopes, count, rows, depth):
        self.q, self.slopes, self.count, self.rows, self.depth = q, slopes, count, rows, depth
        lane = lanes_of()
        self.first = lane < depth
        self.last = lane >= LANES - depth
        place = lane % depth
        self.behind = jnp.where(place == 0, lane + depth - 1, lane - 1)
        self.ahead = jnp.where(place == depth - 1, lane - depth + 1, lane + 1)

    def x_slopes(self):
        q = self.q
        for v in range(NVAR):
            for t in range(self.count):
                for b in range((self.rows + 2 + SUB - 1) // SUB):
                    row = PAD - 1 + SUB * b
                    here = q[v, t + 1, row : row + SUB]
                    low = here - q[v, t + 1, row - 1 : row - 1 + SUB]
                    high = q[v, t + 1, row + 1 : row + 1 + SUB] - here
                    self.slopes[v, t, SUB * b : SUB * (b + 1)] = 0.5 * minmod(low, high)

    def x_jumps(self, s, v):
        left, right = [], []
        row = PAD + SUB * s
        for t in range(self.count):
            here = self.q[v, t + 1, row : row + SUB]
            low = here - self.q[v, t + 1, row - 1 : row - 1 + SUB]
            high = self.q[v, t + 1, row + 1 : row + 1 + SUB] - here
            before = self.slopes[v, t, SUB * s : SUB * s + SUB]
            slope = self.slopes[v, t, SUB * s + 1 : SUB * s + 1 + SUB]
            after = self.slopes[v, t, SUB * s + 2 : SUB * s + 2 + SUB]
            left.append(low + (slope - before))
            right.append(high - (after - slope))
        return left, right

    def from_low(self, tiles):
        rolled = [roll(tile, self.depth) for tile in tiles]
        return [
            rolled[i] if i == 0 else jnp.where(self.first, rolled[i - 1], rolled[i])
            for i in range(len(tiles))
        ]

    def from_high(self, tiles):
        rolled = [roll(tile, -self.depth) for tile in tiles]
        top = len(tiles) - 1
        return [
            rolled[i] if i == top else jnp.where(self.last, rolled[i + 1], rolled[i])
            for i in range(len(tiles))
        ]

    def y_parts(self, s, v):
        row = PAD + SUB * s
        tiles = [self.q[v, t, row : row + SUB] for t in range(self.count + 2)]
        low = [tile - near for tile, near in zip(tiles, self.from_low(tiles))]
        slopes = [0.5 * minmod(a, b) for a, b in zip(low, self.from_high(low))]
        return tiles, low, slopes

    def y_jumps(self, parts):
        tiles, low, slopes = parts
        rise = [slope - near for slope, near in zip(slopes, self.from_low(slopes))]
        left = [a + b for a, b in zip(low, rise)]
        right = self.from_high([a - b for a, b in zip(low, rise)])
        return left[1:-1], right[1:-1]

    def z_jumps(self, s, v):
        left, right = [], []
        row = PAD + SUB * s
        for t in range(self.count):
            here = self.q[v, t + 1, row : row + SUB]
            low = here - take(here, self.behind)
            slope = 0.5 * minmod(low, take(low, self.ahead))
            rise = slope - take(slope, self.behind)
            left.append(low + rise)
            right.append(take(low - rise, self.ahead))
        return left, right

    def block(self, s, seen=None):
        acc = [[None] * self.count for _ in range(NVAR)]
        add_jumps(acc, 0, partial(self.x_jumps, s))
        parts = {}

        def jumps(v):
            parts[v] = self.y_parts(s, v)
            return self.y_jumps(parts[v])

        add_jumps(acc, 1, jumps)
        if seen is not None:
            seen(parts)
        add_jumps(acc, 2, partial(self.z_jumps, s))
        row = PAD + SUB * s
        return [
            [self.q[v, t + 1, row : row + SUB] - acc[v][t] for t in range(self.count)]
            for v in range(NVAR)
        ]


class Plan:
    def __init__(self, coarse, fine, size):
        self.rows = coarse[1]
        self.depth = 8
        self.count = coarse[2] // LANES
        self.fine_rows = fine[2]
        self.fine_depth = 2 * self.depth
        self.fine_count = fine[3] // LANES
        self.patch = self.fine_rows // 2
        self.start = (self.rows - self.patch) // 2
        self.end = self.start + self.patch
        self.size = size
        self.line_rows = 24
        self.ring_rows = 48
        self.sent_rows = 72
        self.average_rows = NVAR * self.patch
        self.side_at = self.average_rows
        self.face_at = self.side_at + self.patch
        self.owner_at = self.face_at + 10
        self.payload_rows = self.owner_at + 6


def split(plan, c_ref, q):
    for v in range(NVAR):
        for t in range(plan.count):
            q[v, t + 1, PAD : PAD + plan.rows] = c_ref[v, :, LANES * t : LANES * (t + 1)]


def window_row(plan, tiles, lane):
    low, high = (roll(tile, LANES // 2) for tile in tiles)
    return jnp.where(lane < LANES // 2, low, high)


def coarse_kernel(plan, c_ref, up_ref, down_ref, mid_ref, xup_ref, xdown_ref, q, slopes, fresh):
    split(plan, c_ref, q)
    for v in range(NVAR):
        for t in range(plan.count):
            for edge in (0, PAD + plan.rows):
                q[v, t + 1, edge : edge + PAD] = jnp.zeros((PAD, LANES), jnp.float32)
        for t in (0, plan.count + 1):
            q[v, t, PAD : PAD + plan.rows] = jnp.zeros((plan.rows, LANES), jnp.float32)
    level = Level(q, slopes, plan.count, plan.rows, plan.depth)
    level.x_slopes()
    for s in range(plan.rows // SUB):
        new = level.block(s)
        row = PAD + SUB * s
        for v in range(NVAR):
            for t in range(plan.count):
                here = q[v, t + 1, row : row + SUB]
                fresh[v, t, SUB * s : SUB * (s + 1)] = 0.5 * (here + new[v][t])
    lane, single = lanes_of(), lanes_of(1)
    sent = (up_ref, down_ref, mid_ref)
    blank = jnp.zeros((SUB, LANES), jnp.float32)
    for ref in sent:
        ref[16:24] = blank
    for level_id in range(2):
        for side, x in enumerate((plan.start - 1, plan.end)):
            for v in range(NVAR):
                if level_id == 0:
                    tiles = [q[v, t + 1, PAD + x : PAD + x + 1] for t in range(2)]
                else:
                    tiles = [fresh[v, t, x : x + 1] for t in range(2)]
                line = window_row(plan, tiles, single)
                at = 10 * level_id + 5 * side + v
                for ref in sent:
                    ref[at : at + 1] = line
    depth = plan.depth
    low_lane = (plan.start - 1) * depth
    high_lane = plan.end * depth - LANES
    packed = [None] * 3
    for level_id in range(2):
        for side, (t, at) in enumerate(((0, low_lane), (1, high_lane))):
            for v in range(NVAR):
                for half in range(plan.patch // SUB):
                    x = plan.start + SUB * half
                    if level_id == 0:
                        tile = q[v, t + 1, PAD + x : PAD + x + SUB]
                    else:
                        tile = fresh[v, t, x : x + SUB]
                    piece = ((level_id * 2 + side) * NVAR + v) * 2 + half
                    slot = piece % 16
                    moved = roll(tile, slot * depth - at)
                    where, old = piece // 16, packed[piece // 16]
                    packed[where] = moved if old is None else jnp.where(lane // depth == slot, moved, old)
    for index, tile in enumerate(packed):
        for ref in sent:
            ref[plan.line_rows + SUB * index : plan.line_rows + SUB * (index + 1)] = tile
    wide = 2 * depth
    for ref, t, at in ((up_ref, plan.count - 1, LANES - wide), (down_ref, 0, 0)):
        packed = [None] * 3
        for v in range(NVAR):
            for s in range(plan.rows // SUB):
                piece = v * (plan.rows // SUB) + s
                slot = piece % 8
                moved = roll(q[v, t + 1, PAD + SUB * s : PAD + SUB * (s + 1)], slot * wide - at)
                where, old = piece // 8, packed[piece // 8]
                packed[where] = moved if old is None else jnp.where(lane // wide == slot, moved, old)
        for index, tile in enumerate(packed):
            ref[plan.ring_rows + SUB * index : plan.ring_rows + SUB * (index + 1)] = tile
    for ref, x in ((xup_ref, plan.rows - 2), (xdown_ref, 0)):
        ref[16:24] = blank
        for v in range(NVAR):
            for t in range(plan.count):
                at = (v * plan.count + t) * 2
                ref[at : at + 2] = q[v, t + 1, PAD + x : PAD + x + 2]


def fine_kernel(plan, others, site_ref, me_ref, f_ref, *refs):
    rings = refs[: others + 1]
    out_ref, pay_ref, q, slopes, lines, faces, sides = refs[others + 1 :]
    turn = (me_ref[0] - site_ref[0, 0] + plan.size) % plan.size
    count, depth, rows = plan.fine_count, plan.fine_depth, plan.fine_rows
    lane = lanes_of()
    ring = []
    for at in range(0, plan.ring_rows, SUB):
        chosen = rings[0][at : at + SUB]
        for k in range(1, others + 1):
            chosen = jnp.where(turn == k, rings[k][at : at + SUB], chosen)
        ring.append(chosen)
    for t in range(count):
        cells = (lane // depth + t * (LANES // depth)) // 2
        index = cells * plan.depth + (lane % depth) // 2
        for at in range(plan.line_rows // SUB):
            lines[t, SUB * at : SUB * (at + 1)] = take(ring[at], index)
    spread = (lane % depth) // 2

    def ghosts(level_id):
        for v in range(NVAR):
            for side, row in enumerate((PAD - 2, PAD + rows)):
                at = 10 * level_id + 5 * side + v
                for t in range(count):
                    q[v, t + 1, row : row + 2] = jnp.broadcast_to(lines[t, at : at + 1], (2, LANES))
            for side, t in enumerate((0, count + 1)):
                for half in range(plan.patch // SUB):
                    piece = ((level_id * 2 + side) * NVAR + v) * 2 + half
                    tile = ring[plan.line_rows // SUB + piece // 16]
                    column = take(tile, spread + (piece % 16) * plan.depth)
                    row = PAD + 2 * SUB * half
                    q[v, t, pl.ds(row, SUB, stride=2)] = column
                    q[v, t, pl.ds(row + 1, SUB, stride=2)] = column

    for v in range(NVAR):
        for t in range(count):
            q[v, t + 1, PAD : PAD + rows] = f_ref[0, v, :, LANES * t : LANES * (t + 1)]
    level = Level(q, slopes, count, rows, depth)
    for step in range(2):
        ghosts(step)
        level.x_slopes()
        for side in range(2):
            for t in range(count):
                edge = PAD if side == 0 else PAD + rows
                left = [q[v, t + 1, edge - 1 : edge] for v in range(NVAR)]
                right = [q[v, t + 1, edge : edge + 1] for v in range(NVAR)]
                for v in range(NVAR):
                    if side == 0:
                        right[v] = right[v] - slopes[v, t, 1:2]
                    else:
                        left[v] = left[v] + slopes[v, t, rows : rows + 1]
                flux = flux_of(left, right, 0)
                for v in range(NVAR):
                    at = 5 * side + v
                    if step == 0:
                        faces[t, at : at + 1] = flux[v]
                    else:
                        faces[t, at : at + 1] = faces[t, at : at + 1] + flux[v]

        fresh = []
        for s in range(rows // SUB):

            def seen(parts, s=s):
                left = []
                right = []
                second = (lane >= depth) & (lane < 2 * depth)
                for v in range(NVAR):
                    tiles, low, slope = parts[v]
                    ghost_low = roll(tiles[0], depth)
                    inner_high = roll(tiles[count] + slope[count], 2 * depth)
                    left.append(jnp.where(second, inner_high, ghost_low))
                    right.append(jnp.where(second, roll(tiles[count + 1], depth), tiles[1] - slope[1]))
                flux = flux_of(left, right, 1)
                for v in range(NVAR):
                    if step == 0:
                        sides[v, SUB * s : SUB * (s + 1)] = flux[v]
                    else:
                        sides[v, SUB * s : SUB * (s + 1)] = sides[v, SUB * s : SUB * (s + 1)] + flux[v]

            new = level.block(s, seen)
            for v in range(NVAR):
                for t in range(count):
                    if step == 0:
                        q2 = new[v][t]
                        fresh.append((v, t, s, q2))
                    else:
                        out_ref[0, v, SUB * s : SUB * (s + 1), LANES * t : LANES * (t + 1)] = new[v][t]
                        fresh.append((v, t, s, new[v][t]))
        for v, t, s, tile in fresh:
            q[v, t + 1, PAD + SUB * s : PAD + SUB * (s + 1)] = tile

    within = ((lane % 32) // plan.depth) * (2 * depth) + (lane % plan.depth) * 2

    def pack(tiles):
        out = None
        for t, tile in enumerate(tiles):
            tile = tile + roll(tile, -1)
            tile = tile + roll(tile, -depth)
            tile = take(tile, within)
            out = tile if out is None else jnp.where(lane // 32 == t, tile, out)
        return out

    for v in range(NVAR):
        for half in range(plan.patch // SUB):
            row = PAD + 2 * SUB * half
            tiles = [
                q[v, t + 1, pl.ds(row, SUB, stride=2)] + q[v, t + 1, pl.ds(row + 1, SUB, stride=2)]
                for t in range(count)
            ]
            at = v * plan.patch + SUB * half
            pay_ref[at : at + SUB] = 0.125 * pack(tiles)
    pair = ((lane // plan.depth) % 2) * depth + (lane % plan.depth) * 2
    for half in range(plan.patch // SUB):
        out = None
        for v in range(NVAR):
            row = 2 * SUB * half
            tile = sides[v, pl.ds(row, SUB, stride=2)] + sides[v, pl.ds(row + 1, SUB, stride=2)]
            tile = take(tile + roll(tile, -1), pair)
            out = tile if out is None else jnp.where(lane // depth == v, tile, out)
        at = plan.side_at + SUB * half
        pay_ref[at : at + SUB] = 0.125 * out
    owner = jnp.zeros((SUB, LANES), jnp.float32) + site_ref[0, 0].astype(jnp.float32)
    pay_ref[plan.payload_rows - SUB : plan.payload_rows] = owner
    pay_ref[plan.face_at : plan.face_at + SUB] = 0.125 * pack([faces[t, 0:SUB] for t in range(count)])
    tail = pack([faces[t, SUB : 2 * SUB] for t in range(count)])
    pay_ref[plan.face_at + SUB : plan.face_at + SUB + 2] = 0.125 * tail[0:2]


def reflux_kernel(plan, others, live_ref, me_ref, c_ref, low_ref, high_ref, before_ref, after_ref, *refs):
    payloads = refs[: others + 1]
    out_ref, q, slopes, pay = refs[others + 1 :]
    count, depth, rows = plan.count, plan.depth, plan.rows
    lane, single = lanes_of(), lanes_of(1)
    split(plan, c_ref, q)
    wide = 2 * depth
    for v in range(NVAR):
        for t in range(count):
            at = (v * count + t) * 2
            q[v, t + 1, PAD - 2 : PAD] = before_ref[at : at + 2]
            q[v, t + 1, PAD + rows : PAD + rows + 2] = after_ref[at : at + 2]
        for s in range(rows // SUB):
            piece = v * (rows // SUB) + s
            at = plan.ring_rows + SUB * (piece // 8)
            slot = piece % 8
            row = PAD + SUB * s
            q[v, 0, row : row + SUB] = roll(low_ref[at : at + SUB], LANES - wide - slot * wide)
            q[v, count + 1, row : row + SUB] = roll(high_ref[at : at + SUB], -slot * wide)
    mine = me_ref[0].astype(jnp.float32)
    owners = [ref[plan.owner_at : plan.owner_at + 1] == mine for ref in payloads]
    for at in range(0, plan.payload_rows, SUB):
        chosen = payloads[0][at : at + SUB]
        for k in range(1, others + 1):
            chosen = jnp.where(jnp.broadcast_to(owners[k], (SUB, LANES)), payloads[k][at : at + SUB], chosen)
        pay[at : at + SUB] = chosen
    live = live_ref[0]
    weight = courant * live.astype(jnp.float32)
    present = live > 0
    level = Level(q, slopes, count, rows, depth)
    level.x_slopes()
    half = LANES // 2
    low_lane = (plan.start - 1) * depth
    high_lane = plan.end * depth - LANES
    at_low = (lane >= low_lane) & (lane < low_lane + depth)
    at_high = (lane >= high_lane) & (lane < high_lane + depth)
    for s in range(rows // SUB):
        inside = plan.start <= SUB * s < plan.end
        change = {}

        def seen(parts):
            left = [level.from_low([p[0][1] + p[2][1], p[0][2] + p[2][2]]) for p in parts.values()]
            plain = [[p[0][1] + p[2][1], p[0][2] + p[2][2]] for p in parts.values()]
            right = [[p[0][1] - p[2][1], p[0][2] - p[2][2]] for p in parts.values()]
            moved = [level.from_high(r) for r in right]
            low = flux_of([p[0] for p in plain], [m[0] for m in moved], 1)
            high = flux_of([p[1] for p in left], [r[1] for r in right], 1)
            base = plan.side_at + SUB * s - plan.start
            tile = pay[base : base + SUB]
            for v in range(NVAR):
                reg_low = roll(tile, low_lane - v * wide)
                reg_high = roll(tile, high_lane - v * wide - depth)
                change[v] = (
                    jnp.where(at_low, weight * (low[v] - reg_low), 0.0),
                    jnp.where(at_high, weight * (reg_high - high[v]), 0.0),
                )

        new = level.block(s, seen if inside else None)
        for v in range(NVAR):
            if inside:
                base = v * plan.patch + SUB * s - plan.start
                average = roll(pay[base : base + SUB], half)
                new[v][0] = new[v][0] + change[v][0]
                new[v][1] = new[v][1] + change[v][1]
                new[v][0] = jnp.where(present & (lane >= half), average, new[v][0])
                new[v][1] = jnp.where(present & (lane < half), average, new[v][1])
            for t in range(count):
                out_ref[v, SUB * s : SUB * (s + 1), LANES * t : LANES * (t + 1)] = new[v][t]
    for side, x in enumerate((plan.start - 1, plan.end)):
        for t in range(count):
            face = x if side == 0 else x - 1
            left = [q[v, t + 1, PAD + face : PAD + face + 1] + slopes[v, t, face + 1 : face + 2] for v in range(NVAR)]
            right = [
                q[v, t + 1, PAD + face + 1 : PAD + face + 2] - slopes[v, t, face + 2 : face + 3]
                for v in range(NVAR)
            ]
            flux = flux_of(left, right, 0)
            inner = single >= half if t == 0 else single < half
            for v in range(NVAR):
                at = plan.face_at + 5 * side + v
                register = roll(pay[at : at + 1], half)
                gap = flux[v] - register if side == 0 else register - flux[v]
                old = out_ref[v, x : x + 1, LANES * t : LANES * (t + 1)]
                out_ref[v, x : x + 1, LANES * t : LANES * (t + 1)] = old + jnp.where(inner, weight * gap, 0.0)


def call(body, out_shape, scratch, flops, moved, smem=0, operands=0):
    specs = [pl.BlockSpec(memory_space=pltpu.SMEM)] * smem + [pl.BlockSpec(memory_space=VMEM)] * (operands - smem)
    return pl.pallas_call(
        body,
        out_shape=out_shape,
        in_specs=specs,
        out_specs=jax.tree.map(lambda _: pl.BlockSpec(memory_space=VMEM), out_shape),
        scratch_shapes=scratch,
        cost_estimate=pl.CostEstimate(flops=flops, bytes_accessed=moved, transcendentals=0),
        compiler_params=pltpu.CompilerParams(vmem_limit_bytes=16 << 20),
    )


def rotate(array, axis, step):
    size = lax.axis_size(axis)
    return lax.ppermute(array, axis, [(i, (i + step) % size) for i in range(size)])


def shards(coarse_state, fine_state, slot_site, box_live):
    size = lax.axis_size("gy")
    plan = Plan(coarse_state.shape, fine_state.shape, size)
    f32 = jnp.float32
    shape = jax.ShapeDtypeStruct
    coarse_scratch = [
        VMEM((NVAR, plan.count + 2, plan.rows + 2 * PAD, LANES), f32),
        VMEM((NVAR, plan.count, plan.rows + SUB, LANES), f32),
    ]
    sent = shape((plan.sent_rows, LANES), f32)
    edge = shape((24, LANES), f32)
    up, down, mid, xup, xdown = call(
        partial(coarse_kernel, plan),
        (sent, sent, shape((plan.ring_rows, LANES), f32), edge, edge),
        coarse_scratch + [VMEM((NVAR, plan.count, plan.rows, LANES), f32)],
        4_000_000,
        400_000,
        operands=1,
    )(coarse_state)
    others = size - 1
    rings = {0: mid}
    for k in range(1, size):
        rings[k] = rotate(up if k == 1 else down if k == size - 1 else mid, "gy", k)
    before = rotate(xup, "gx", 1)
    after = rotate(xdown, "gx", -1)
    me = lax.axis_index("gy").astype(jnp.int32).reshape(1)
    fine_out, payload = call(
        partial(fine_kernel, plan, others),
        (shape(fine_state.shape, f32), shape((plan.payload_rows, LANES), f32)),
        [
            VMEM((NVAR, plan.fine_count + 2, plan.fine_rows + 2 * PAD, LANES), f32),
            VMEM((NVAR, plan.fine_count, plan.fine_rows + SUB, LANES), f32),
            VMEM((plan.fine_count, plan.line_rows, LANES), f32),
            VMEM((plan.fine_count, 2 * SUB, LANES), f32),
            VMEM((NVAR, plan.fine_rows, LANES), f32),
        ],
        16_000_000,
        1_000_000,
        smem=2,
        operands=3 + size,
    )(slot_site, me, fine_state, *[rings[k] for k in range(size)])
    payloads = [payload] + [rotate(payload, "gy", k) for k in range(1, size)]
    coarse_out = call(
        partial(reflux_kernel, plan, others),
        shape(coarse_state.shape, f32),
        coarse_scratch + [VMEM((plan.payload_rows, LANES), f32)],
        4_000_000,
        400_000,
        smem=2,
        operands=7 + size,
    )(box_live, me, coarse_state, rings[1], rings[size - 1], before, after, *payloads)
    return (coarse_out, fine_out)


def solution(mesh):
    return jax.shard_map(
        shards,
        mesh=mesh,
        in_specs=(
            P(None, "gx", "gy"),
            P(("gx", "gy"), None, None, None),
            P(("gx", "gy"), None),
            P(("gx", "gy")),
        ),
        out_specs=(P(None, "gx", "gy"), P(("gx", "gy"), None, None, None)),
        check_vma=False,
    )
```

profile of v0, /device:TPU:0, one launch (start us, length us, event | category | flops | bytes accessed | tf_op | source)
XLA Modules:
  0.0 67.7 jit_solution(5327671442503952301)
XLA Ops:
  0.6 0.0 copy-start
  0.6 0.9 %copy-done = f32[5,32,256]{2,1,0:T(8,128)S(1)} copy-done((f32[5,32,256]{2,1,0:T(8,128)S(1)}, f32[5,32,256]{2,1,0:T(8,128)}, u32[]{:S(2)}) %copy-start) | copy-done | bytes 163864
  1.5 7.0 %shard_map.59 = (f32[72,128]{1,0:T(8,128)S(1)}, f32[72,128]{1,0:T(8,128)S(1)}, f32[48,128]{1,0:T(8,128)S(1)}, f32[24,128]{1,0:T(8,128)S(1)}, f32[24,128]{1,0:T(8,128)S(1)}) custom-call(f32[5,32,256]{2,1,0:T(8,128)S(1)} %copy-done), custom_call_target="tpu_custom_call" | custom-call | flops 4000000 | bytes 400000 | tf_op jit(solution)/shard_map/pallas_call | solution.py:518
  8.6 0.5 collective-permute-start
  9.1 2.0 %collective-permute-start.1 = (f32[72,128]{1,0:T(8,128)S(1)}, f32[72,128]{1,0:T(8,128)S(1)}, u32[]{:S(2)}, u32[]{:S(2)}) collective-permute-start(f32[72,128]{1,0:T(8,128)S(1)} %get-tuple-element.10), channel_id=1, source_target_pairs={{0,3},{1,0},{2,1},{3,2},{4,7},{5,4},{6,5},{7,6},{8,11},{9,8},{10,9... | collective-permute-start | bytes 110600 | tf_op jit(solution)/shard_map/ppermute | solution.py:504
  11.1 2.2 %collective-permute-start.4 = (f32[48,128]{1,0:T(8,128)S(1)}, f32[48,128]{1,0:T(8,128)S(1)}, u32[]{:S(2)}, u32[]{:S(2)}) collective-permute-start(f32[48,128]{1,0:T(8,128)S(1)} %get-tuple-element.13.refs_0_), channel_id=1, source_target_pairs={{0,2},{1,3},{2,0},{3,1},{4,6},{5,7},{6,4},{7,5},{8,10},{9,11},{10,... | collective-permute-start | bytes 73736 | tf_op jit(solution)/shard_map/ppermute | solution.py:504
  13.3 0.0 copy-start.3
  13.3 2.2 %collective-permute-done.4.refs_2_ = f32[48,128]{1,0:T(8,128)S(1)} collective-permute-done((f32[48,128]{1,0:T(8,128)S(1)}, f32[48,128]{1,0:T(8,128)S(1)}, u32[]{:S(2)}, u32[]{:S(2)}) %collective-permute-start.4) | collective-permute-done | bytes 24608 | tf_op jit(solution)/shard_map/ppermute | solution.py:504
  15.5 0.0 collective-permute-done.refs_1_.low_ref
  15.5 0.0 collective-permute-done.1.refs_3_.high_ref
  15.5 0.0 copy-done.3
  15.6 0.0 copy-start.2
  15.6 1.0 %copy-done.2 = f32[1,5,32,512]{3,2,1,0:T(8,128)S(1)} copy-done((f32[1,5,32,512]{3,2,1,0:T(8,128)S(1)}, f32[1,5,32,512]{3,2,1,0:T(8,128)}, u32[]{:S(2)}) %copy-start.2) | copy-done | bytes 327704
  16.5 0.0 copy-start.1
  16.5 36.2 %shard_map.60 = (f32[1,5,32,512]{3,2,1,0:T(8,128)}, f32[112,128]{1,0:T(8,128)S(1)}) custom-call(s32[1,2]{1,0:T(1,128)S(1)} %copy-done.3, s32[1]{0:T(128)} %bitcast.me_ref, f32[1,5,32,512]{3,2,1,0:T(8,128)S(1)} %copy-done.2, f32[48,128]{1,0:T(8,128)S(1)} %get-tuple-element.13.refs_0_, f32[72,128]{1,0:T(8,128)S(1)} %collective-permute-done.refs_1_.low_ref, ...), custom_call_target="tpu_custom_call" | custom-call | flops 16000000 | bytes 1000000 | tf_op jit(solution)/shard_map/pallas_call | solution.py:533
  52.7 0.1 collective-permute-start.7
  52.8 1.7 %collective-permute-start.6 = (f32[112,128]{1,0:T(8,128)S(1)}, f32[112,128]{1,0:T(8,128)S(1)}, u32[]{:S(2)}, u32[]{:S(2)}) collective-permute-start(f32[112,128]{1,0:T(8,128)S(1)} %get-tuple-element.14.refs_0_), channel_id=1, source_target_pairs={{0,2},{1,3},{2,0},{3,1},{4,6},{5,7},{6,4},{7,5},{8,10},{9,11},{10,... | collective-permute-start | bytes 172040 | tf_op jit(solution)/shard_map/ppermute | solution.py:504
  54.5 0.2 collective-permute-start.5
  54.6 1.5 %collective-permute-start.2 = (f32[24,128]{1,0:T(8,128)S(1)}, f32[24,128]{1,0:T(8,128)S(1)}, u32[]{:S(2)}, u32[]{:S(2)}) collective-permute-start(f32[24,128]{1,0:T(8,128)S(1)} %get-tuple-element.11), channel_id=1, source_target_pairs={{0,4},{4,8},{8,12},{12,16},{16,20},{20,24},{24,28},{28,0},{1,5},{5... | collective-permute-start | bytes 36872 | tf_op jit(solution)/shard_map/ppermute | solution.py:504
  56.1 3.2 %collective-permute-start.3 = (f32[24,128]{1,0:T(8,128)S(1)}, f32[24,128]{1,0:T(8,128)S(1)}, u32[]{:S(2)}, u32[]{:S(2)}) collective-permute-start(f32[24,128]{1,0:T(8,128)S(1)} %get-tuple-element.12), channel_id=1, source_target_pairs={{0,28},{4,0},{8,4},{12,8},{16,12},{20,16},{24,20},{28,24},{1,29},{... | collective-permute-start | bytes 36872 | tf_op jit(solution)/shard_map/ppermute | solution.py:504
  60.0 1.0 %collective-permute-done.2.before_ref = f32[24,128]{1,0:T(8,128)S(1)} collective-permute-done((f32[24,128]{1,0:T(8,128)S(1)}, f32[24,128]{1,0:T(8,128)S(1)}, u32[]{:S(2)}, u32[]{:S(2)}) %collective-permute-start.2) | collective-permute-done | bytes 12320 | tf_op jit(solution)/shard_map/ppermute | solution.py:504
  61.0 0.0 collective-permute-done.3.after_ref
  61.0 0.0 collective-permute-done.7.refs_3_
  61.0 0.0 collective-permute-done.6.refs_2_
  61.0 0.0 collective-permute-done.5.refs_1_
  61.0 0.0 copy-done.1
  61.0 6.6 %shard_map.61 = f32[5,32,256]{2,1,0:T(8,128)} custom-call(s32[1]{0:T(128)S(6)} %copy.6.live_ref, s32[1]{0:T(128)} %bitcast.me_ref, f32[5,32,256]{2,1,0:T(8,128)S(1)} %copy-done.1, f32[72,128]{1,0:T(8,128)S(1)} %collective-permute-done.refs_1_.low_ref, f32[72,128]{1,0:T(8,128)S(1)} %collective-permute-done.1.refs_3_.high_ref, ...), custom_call_target="tpu_custom_call" | custom-call | flops 4000000 | bytes 400000 | tf_op jit(solution)/shard_map/pallas_call | solution.py:549
Async XLA Ops:
  0.6 0.9 %copy-start = (f32[5,32,256]{2,1,0:T(8,128)S(1)}, f32[5,32,256]{2,1,0:T(8,128)}, u32[]{:S(2)}) copy-start(f32[5,32,256]{2,1,0:T(8,128)} %c_ref.3) | copy-start | bytes 491524
  8.6 7.0 %collective-permute-start = (f32[72,128]{1,0:T(8,128)S(1)}, f32[72,128]{1,0:T(8,128)S(1)}, u32[]{:S(2)}, u32[]{:S(2)}) collective-permute-start(f32[72,128]{1,0:T(8,128)S(1)} %get-tuple-element.9), channel_id=1, source_target_pairs={{0,1},{1,2},{2,3},{3,0},{4,5},{5,6},{6,7},{7,4},{8,9},{9,10},{10,1... | collective-permute-start | bytes 110600 | tf_op jit(solution)/shard_map/ppermute | solution.py:504
  9.1 6.5 %collective-permute-start.1 = (f32[72,128]{1,0:T(8,128)S(1)}, f32[72,128]{1,0:T(8,128)S(1)}, u32[]{:S(2)}, u32[]{:S(2)}) collective-permute-start(f32[72,128]{1,0:T(8,128)S(1)} %get-tuple-element.10), channel_id=1, source_target_pairs={{0,3},{1,0},{2,1},{3,2},{4,7},{5,4},{6,5},{7,6},{8,11},{9,8},{10,9... | collective-permute-start | bytes 110600 | tf_op jit(solution)/shard_map/ppermute | solution.py:504
  11.1 4.4 %collective-permute-start.4 = (f32[48,128]{1,0:T(8,128)S(1)}, f32[48,128]{1,0:T(8,128)S(1)}, u32[]{:S(2)}, u32[]{:S(2)}) collective-permute-start(f32[48,128]{1,0:T(8,128)S(1)} %get-tuple-element.13.refs_0_), channel_id=1, source_target_pairs={{0,2},{1,3},{2,0},{3,1},{4,6},{5,7},{6,4},{7,5},{8,10},{9,11},{10,... | collective-permute-start | bytes 73736 | tf_op jit(solution)/shard_map/ppermute | solution.py:504
  13.3 2.2 %copy-start.3 = (s32[1,2]{1,0:T(1,128)S(1)}, s32[1,2]{1,0:T(1,128)}, u32[]{:S(2)}) copy-start(s32[1,2]{1,0:T(1,128)} %site_ref.1) | copy-start | bytes 28
  15.6 1.0 %copy-start.2 = (f32[1,5,32,512]{3,2,1,0:T(8,128)S(1)}, f32[1,5,32,512]{3,2,1,0:T(8,128)}, u32[]{:S(2)}) copy-start(f32[1,5,32,512]{3,2,1,0:T(8,128)} %f_ref.1) | copy-start | bytes 983044
  16.5 44.5 %copy-start.1 = (f32[5,32,256]{2,1,0:T(8,128)S(1)}, f32[5,32,256]{2,1,0:T(8,128)}, u32[]{:S(2)}) copy-start(f32[5,32,256]{2,1,0:T(8,128)} %c_ref.3) | copy-start | bytes 491524
  52.7 8.3 %collective-permute-start.7 = (f32[112,128]{1,0:T(8,128)S(1)}, f32[112,128]{1,0:T(8,128)S(1)}, u32[]{:S(2)}, u32[]{:S(2)}) collective-permute-start(f32[112,128]{1,0:T(8,128)S(1)} %get-tuple-element.14.refs_0_), channel_id=1, source_target_pairs={{0,3},{1,0},{2,1},{3,2},{4,7},{5,4},{6,5},{7,6},{8,11},{9,8},{10,9... | collective-permute-start | bytes 172040 | tf_op jit(solution)/shard_map/ppermute | solution.py:504
  52.8 8.3 %collective-permute-start.6 = (f32[112,128]{1,0:T(8,128)S(1)}, f32[112,128]{1,0:T(8,128)S(1)}, u32[]{:S(2)}, u32[]{:S(2)}) collective-permute-start(f32[112,128]{1,0:T(8,128)S(1)} %get-tuple-element.14.refs_0_), channel_id=1, source_target_pairs={{0,2},{1,3},{2,0},{3,1},{4,6},{5,7},{6,4},{7,5},{8,10},{9,11},{10,... | collective-permute-start | bytes 172040 | tf_op jit(solution)/shard_map/ppermute | solution.py:504
  54.5 6.6 %collective-permute-start.5 = (f32[112,128]{1,0:T(8,128)S(1)}, f32[112,128]{1,0:T(8,128)S(1)}, u32[]{:S(2)}, u32[]{:S(2)}) collective-permute-start(f32[112,128]{1,0:T(8,128)S(1)} %get-tuple-element.14.refs_0_), channel_id=1, source_target_pairs={{0,1},{1,2},{2,3},{3,0},{4,5},{5,6},{6,7},{7,4},{8,9},{9,10},{10,1... | collective-permute-start | bytes 172040 | tf_op jit(solution)/shard_map/ppermute | solution.py:504
  54.6 6.4 %collective-permute-start.2 = (f32[24,128]{1,0:T(8,128)S(1)}, f32[24,128]{1,0:T(8,128)S(1)}, u32[]{:S(2)}, u32[]{:S(2)}) collective-permute-start(f32[24,128]{1,0:T(8,128)S(1)} %get-tuple-element.11), channel_id=1, source_target_pairs={{0,4},{4,8},{8,12},{12,16},{16,20},{20,24},{24,28},{28,0},{1,5},{5... | collective-permute-start | bytes 36872 | tf_op jit(solution)/shard_map/ppermute | solution.py:504
  56.1 4.9 %collective-permute-start.3 = (f32[24,128]{1,0:T(8,128)S(1)}, f32[24,128]{1,0:T(8,128)S(1)}, u32[]{:S(2)}, u32[]{:S(2)}) collective-permute-start(f32[24,128]{1,0:T(8,128)S(1)} %get-tuple-element.12), channel_id=1, source_target_pairs={{0,28},{4,0},{8,4},{12,8},{16,12},{20,16},{24,20},{28,24},{1,29},{... | collective-permute-start | bytes 36872 | tf_op jit(solution)/shard_map/ppermute | solution.py:504
where the time goes:
time: 67.8 us; the launch traced here: 67.7 us
  Pallas kernels  49.8 us (73%)
  starting transfers between devices  11.4 us (17%)
  waiting for transfers between devices  3.23 us (5%)
  local copies, waits for them, and re-layouts  1.89 us (3%)
  between operations  1.35 us (2%)
    pallas_call x1, Pallas kernels, shards(): call(partial(fine_kernel, plan, others), (shape(fine_state.shape, f32), s...  36.2 us
    ppermute x8, starting transfers between devices, rotate(): lax.ppermute(array, axis, [(i, (i + step) % size) for i in range(size)])  11.4 us
    pallas_call x1, Pallas kernels, shards(): call(partial(coarse_kernel, plan), (sent, sent, shape((plan.ring_rows, LA...  6.99 us
    pallas_call x1, Pallas kernels, shards(): call(partial(reflux_kernel, plan, others), shape(coarse_state.shape, f32)...  6.62 us
    ppermute x8, waiting for transfers between devices, rotate(): lax.ppermute(array, axis, [(i, (i + step) % size) for i in range(size)])  3.23 us
    unnamed x8, local copies, waits for them, and re-layouts  1.89 us
  transfers between devices with their start and end apart: 8, of which 2 were waited for; matrix products, arithmetic and copies ran while one was open for 0% of the time, Pallas kernels for 0%

commit v1 on v0

v1 whole, which is shorter than its diff:
```python
from functools import partial

import jax
import jax.numpy as jnp
from jax import lax
from jax.experimental import pallas as pl
from jax.experimental.pallas import tpu as pltpu
from jax.sharding import PartitionSpec as P

LANES = 128
SUB = 8
PAD = 8

courant = 0.2
drift = (0.5, 0.3, 0.2)
signal = (1.5, 1.3, 1.2)
PLUS = tuple(0.5 * (a + s) for a, s in zip(drift, signal))
MINUS = tuple(0.5 * (a - s) for a, s in zip(drift, signal))

NVAR = 5
VMEM = pltpu.VMEM


def minmod(first, second):
    return jnp.maximum(jnp.minimum(first, second), jnp.minimum(jnp.maximum(first, second), 0.0))


def lanes_of(rows=SUB):
    return lax.broadcasted_iota(jnp.int32, (rows, LANES), 1)


def roll(values, step):
    step = step % LANES
    return values if step == 0 else pltpu.roll(values, step, 1)


def take(values, index):
    return jnp.take_along_axis(values, index, axis=1, mode="promise_in_bounds")


def coupled(direction):
    return {0: 1 + direction, 1 + direction: 4, 4: 1 + direction}


def flux_of(left, right, direction):
    couples = coupled(direction)
    out = []
    for v in range(NVAR):
        flux = PLUS[direction] * left[v] + MINUS[direction] * right[v]
        if v in couples:
            w = couples[v]
            flux = flux + 0.5 * (left[w] + right[w])
        out.append(flux)
    return out


class Level:
    def __init__(self, work, count, rows, depth, ghosts):
        self.slopes, self.low, self.slope, self.left, self.right = work[:5]
        self.zlow, self.zslope, self.zleft, self.zright = work[5:]
        self.count, self.rows, self.depth, self.ghosts = count, rows, depth, ghosts
        lane = lanes_of()
        self.first = lane < depth
        self.last = lane >= LANES - depth
        place = lane % depth
        self.behind = jnp.where(place == 0, lane + depth - 1, lane - 1)
        self.ahead = jnp.where(place == depth - 1, lane - depth + 1, lane + 1)

    @staticmethod
    def work(count, rows):
        f32 = jnp.float32
        wide = VMEM((NVAR, count + 2, rows, LANES), f32)
        narrow = VMEM((NVAR, count, rows, LANES), f32)
        return [VMEM((NVAR, count, rows + SUB, LANES), f32)] + [wide] * 4 + [narrow] * 4

    def columns(self):
        for v in range(NVAR):
            for s in range(self.rows // SUB):
                yield v, slice(SUB * s, SUB * (s + 1)), slice(PAD + SUB * s, PAD + SUB * (s + 1))

    def tiles(self):
        for v, here, padded in self.columns():
            for t in range(self.count):
                yield v, t, here, padded

    def prepare(self, q):
        count, depth = self.count, self.depth
        full, flat = self.ghosts == "full", self.ghosts == "flat"
        inner = range(1, count + 1)
        for v, here, padded in self.columns():
            cells = {t: q[v, t, padded] for t in range(count + 2)}
            moved = {t: roll(cells[t], depth) for t in inner}
            moved[0] = roll(cells[0], depth) if full else cells[0] if flat else moved[1]
            for t in inner:
                self.low[v, t, here] = cells[t] - jnp.where(self.first, moved[t - 1], moved[t])
            if full:
                top = roll(cells[count + 1], depth)
                self.low[v, 0, here] = cells[0] - moved[0]
                self.low[v, count + 1, here] = cells[count + 1] - jnp.where(self.first, moved[count], top)
            if flat:
                self.low[v, count + 1, here] = cells[count + 1] - moved[count]
        for v, t, here, padded in self.tiles():
            cell = q[v, t + 1, padded]
            self.zlow[v, t, here] = cell - take(cell, self.behind)
        for v in range(NVAR):
            for t in range(count):
                for b in range((self.rows + 2 + SUB - 1) // SUB):
                    row = PAD - 1 + SUB * b
                    cell = q[v, t + 1, row : row + SUB]
                    low = cell - q[v, t + 1, row - 1 : row - 1 + SUB]
                    high = q[v, t + 1, row + 1 : row + 1 + SUB] - cell
                    self.slopes[v, t, SUB * b : SUB * (b + 1)] = 0.5 * minmod(low, high)
        for v, here, padded in self.columns():
            low = {t: self.low[v, t, here] for t in inner}
            moved = {t: roll(low[t], -depth) for t in inner}
            if full or flat:
                low[count + 1] = self.low[v, count + 1, here]
                moved[count + 1] = roll(low[count + 1], -depth)
            else:
                moved[count + 1] = moved[count]
            for t in inner:
                high = jnp.where(self.last, moved[t + 1], moved[t])
                self.slope[v, t, here] = 0.5 * minmod(low[t], high)
            if full:
                low[0] = self.low[v, 0, here]
                high = jnp.where(self.last, moved[1], roll(low[0], -depth))
                self.slope[v, 0, here] = 0.5 * minmod(low[0], high)
                self.slope[v, count + 1, here] = 0.5 * minmod(low[count + 1], moved[count + 1])
        for v, t, here, padded in self.tiles():
            low = self.zlow[v, t, here]
            self.zslope[v, t, here] = 0.5 * minmod(low, take(low, self.ahead))

    def finish(self, q, store):
        count, depth = self.count, self.depth
        full, flat = self.ghosts == "full", self.ghosts == "flat"
        inner = range(1, count + 1)
        for v, t, here, padded in self.tiles():
            slope = self.zslope[v, t, here]
            rise = slope - take(slope, self.behind)
            low = self.zlow[v, t, here]
            self.zleft[v, t, here] = low + rise
            self.zright[v, t, here] = low - rise
        for v, here, padded in self.columns():
            slope = {t: self.slope[v, t, here] for t in inner}
            moved = {t: roll(slope[t], depth) for t in inner}
            if full:
                moved[0] = roll(self.slope[v, 0, here], depth)
            else:
                moved[0] = jnp.zeros((SUB, LANES), jnp.float32) if flat else moved[1]
            for t in inner:
                rise = slope[t] - jnp.where(self.first, moved[t - 1], moved[t])
                low = self.low[v, t, here]
                self.left[v, t, here] = low + rise
                self.right[v, t, here] = low - rise
            if full:
                rise = self.slope[v, count + 1, here] - moved[count]
                self.right[v, count + 1, here] = self.low[v, count + 1, here] - rise
            if flat:
                self.right[v, count + 1, here] = self.low[v, count + 1, here] + moved[count]
        for v, t, here, padded in self.tiles():
            self.zright[v, t, here] = take(self.zright[v, t, here], self.ahead)
        for v, here, padded in self.columns():
            moved = {t: roll(self.right[v, t, here], -depth) for t in inner}
            if full or flat:
                moved[count + 1] = roll(self.right[v, count + 1, here], -depth)
            else:
                moved[count + 1] = moved[count]
            for t in inner:
                self.right[v, t, here] = jnp.where(self.last, moved[t + 1], moved[t])
        for s in range(self.rows // SUB):
            for t in range(count):
                self.gather(q, s, t, store)

    def gather(self, q, s, t, store):
        here = slice(SUB * s, SUB * (s + 1))
        row = PAD + SUB * s
        cell = [q[v, t + 1, row : row + SUB] for v in range(NVAR)]
        acc = [None] * NVAR

        def add(v, term):
            acc[v] = term if acc[v] is None else acc[v] + term

        for direction in range(3):
            couples = coupled(direction)
            for v in range(NVAR):
                if direction == 0:
                    low = cell[v] - q[v, t + 1, row - 1 : row - 1 + SUB]
                    high = q[v, t + 1, row + 1 : row + 1 + SUB] - cell[v]
                    slope = self.slopes[v, t, SUB * s + 1 : SUB * s + 1 + SUB]
                    left = low + (slope - self.slopes[v, t, SUB * s : SUB * s + SUB])
                    right = high - (self.slopes[v, t, SUB * s + 2 : SUB * s + 2 + SUB] - slope)
                elif direction == 1:
                    left, right = self.left[v, t + 1, here], self.right[v, t + 1, here]
                else:
                    left, right = self.zleft[v, t, here], self.zright[v, t, here]
                add(v, (courant * PLUS[direction]) * left + (courant * MINUS[direction]) * right)
                targets = [w for w in couples if couples[w] == v]
                if targets:
                    shared = (0.5 * courant) * (left + right)
                    for w in targets:
                        add(w, shared)
        for v in range(NVAR):
            store(v, t, s, cell[v] - acc[v])


class Plan:
    def __init__(self, coarse, fine, size):
        self.rows = coarse[1]
        self.depth = 8
        self.count = coarse[2] // LANES
        self.fine_rows = fine[2]
        self.fine_depth = 2 * self.depth
        self.fine_count = fine[3] // LANES
        self.patch = self.fine_rows // 2
        self.start = (self.rows - self.patch) // 2
        self.end = self.start + self.patch
        self.size = size
        self.line_rows = 24
        self.ring_rows = 48
        self.sent_rows = 72
        self.average_rows = NVAR * self.patch
        self.side_at = self.average_rows
        self.face_at = self.side_at + self.patch
        self.owner_at = self.face_at + 10
        self.payload_rows = self.owner_at + 6


def split(plan, c_ref, q):
    for v in range(NVAR):
        for t in range(plan.count):
            q[v, t + 1, PAD : PAD + plan.rows] = c_ref[v, :, LANES * t : LANES * (t + 1)]


def window_row(plan, tiles, lane):
    low, high = (roll(tile, LANES // 2) for tile in tiles)
    return jnp.where(lane < LANES // 2, low, high)


def coarse_kernel(plan, c_ref, f_ref, up_ref, down_ref, mid_ref, xup_ref, xdown_ref, held_ref, q, fresh, sem, *work):
    load = pltpu.make_async_copy(f_ref, held_ref, sem)
    load.start()
    split(plan, c_ref, q)
    for v in range(NVAR):
        for t in range(plan.count):
            for edge in (0, PAD + plan.rows):
                q[v, t + 1, edge : edge + PAD] = jnp.zeros((PAD, LANES), jnp.float32)
        for t in (0, plan.count + 1):
            q[v, t, PAD : PAD + plan.rows] = jnp.zeros((plan.rows, LANES), jnp.float32)
    level = Level(work, plan.count, plan.rows, plan.depth, "none")
    level.prepare(q)

    def store(v, t, s, tile):
        row = PAD + SUB * s
        fresh[v, t, SUB * s : SUB * (s + 1)] = 0.5 * (q[v, t + 1, row : row + SUB] + tile)

    level.finish(q, store)
    lane, single = lanes_of(), lanes_of(1)
    sent = (up_ref, down_ref, mid_ref)
    blank = jnp.zeros((SUB, LANES), jnp.float32)
    for ref in sent:
        ref[16:24] = blank
    for level_id in range(2):
        for side, x in enumerate((plan.start - 1, plan.end)):
            for v in range(NVAR):
                if level_id == 0:
                    tiles = [q[v, t + 1, PAD + x : PAD + x + 1] for t in range(2)]
                else:
                    tiles = [fresh[v, t, x : x + 1] for t in range(2)]
                line = window_row(plan, tiles, single)
                at = 10 * level_id + 5 * side + v
                for ref in sent:
                    ref[at : at + 1] = line
    depth = plan.depth
    low_lane = (plan.start - 1) * depth
    high_lane = plan.end * depth - LANES
    packed = [None] * 3
    for level_id in range(2):
        for side, (t, at) in enumerate(((0, low_lane), (1, high_lane))):
            for v in range(NVAR):
                for half in range(plan.patch // SUB):
                    x = plan.start + SUB * half
                    if level_id == 0:
                        tile = q[v, t + 1, PAD + x : PAD + x + SUB]
                    else:
                        tile = fresh[v, t, x : x + SUB]
                    piece = ((level_id * 2 + side) * NVAR + v) * 2 + half
                    slot = piece % 16
                    moved = roll(tile, slot * depth - at)
                    where, old = piece // 16, packed[piece // 16]
                    packed[where] = moved if old is None else jnp.where(lane // depth == slot, moved, old)
    for index, tile in enumerate(packed):
        for ref in sent:
            ref[plan.line_rows + SUB * index : plan.line_rows + SUB * (index + 1)] = tile
    wide = 2 * depth
    for ref, t, at in ((up_ref, plan.count - 1, LANES - wide), (down_ref, 0, 0)):
        packed = [None] * 3
        for v in range(NVAR):
            for s in range(plan.rows // SUB):
                piece = v * (plan.rows // SUB) + s
                slot = piece % 8
                moved = roll(q[v, t + 1, PAD + SUB * s : PAD + SUB * (s + 1)], slot * wide - at)
                where, old = piece // 8, packed[piece // 8]
                packed[where] = moved if old is None else jnp.where(lane // wide == slot, moved, old)
        for index, tile in enumerate(packed):
            ref[plan.ring_rows + SUB * index : plan.ring_rows + SUB * (index + 1)] = tile
    for ref, x in ((xup_ref, plan.rows - 2), (xdown_ref, 0)):
        ref[16:24] = blank
        for v in range(NVAR):
            for t in range(plan.count):
                at = (v * plan.count + t) * 2
                ref[at : at + 2] = q[v, t + 1, PAD + x : PAD + x + 2]
    load.wait()


def fine_kernel(plan, others, site_ref, me_ref, f_ref, *refs):
    rings = refs[: others + 1]
    out_ref, pay_ref, q, q_later, lines, faces, sides = refs[others + 1 : others + 8]
    work = refs[others + 8 :]
    turn = (me_ref[0] - site_ref[0, 0] + plan.size) % plan.size
    count, depth, rows = plan.fine_count, plan.fine_depth, plan.fine_rows
    lane = lanes_of()
    ring = []
    for at in range(0, plan.ring_rows, SUB):
        chosen = rings[0][at : at + SUB]
        for k in range(1, others + 1):
            chosen = jnp.where(turn == k, rings[k][at : at + SUB], chosen)
        ring.append(chosen)
    for t in range(count):
        cells = (lane // depth + t * (LANES // depth)) // 2
        index = cells * plan.depth + (lane % depth) // 2
        for at in range(plan.line_rows // SUB):
            lines[t, SUB * at : SUB * (at + 1)] = take(ring[at], index)
    spread = (lane % depth) // 2

    def ghosts(q, level_id):
        for v in range(NVAR):
            for side, row in enumerate((PAD - 2, PAD + rows)):
                at = 10 * level_id + 5 * side + v
                for t in range(count):
                    q[v, t + 1, row : row + 2] = jnp.broadcast_to(lines[t, at : at + 1], (2, LANES))
            for side, t in enumerate((0, count + 1)):
                for half in range(plan.patch // SUB):
                    piece = ((level_id * 2 + side) * NVAR + v) * 2 + half
                    tile = ring[plan.line_rows // SUB + piece // 16]
                    column = take(roll(tile, -(piece % 16) * plan.depth), spread)
                    row = PAD + 2 * SUB * half
                    q[v, t, pl.ds(row, SUB, stride=2)] = column
                    q[v, t, pl.ds(row + 1, SUB, stride=2)] = column

    for v in range(NVAR):
        for t in range(count):
            q[v, t + 1, PAD : PAD + rows] = f_ref[0, v, :, LANES * t : LANES * (t + 1)]
    level = Level(work, count, rows, depth, "flat")
    slopes = level.slopes
    second = (lane >= depth) & (lane < 2 * depth)
    ghosts(q, 0)
    ghosts(q_later, 1)
    for step, (now, later) in enumerate(((q, q_later), (q_later, q))):

        def add(ref, index, value, step=step):
            ref[index] = value if step == 0 else ref[index] + value

        level.prepare(now)
        for side in range(2):
            for t in range(count):
                edge = PAD if side == 0 else PAD + rows
                left = [now[v, t + 1, edge - 1 : edge] for v in range(NVAR)]
                right = [now[v, t + 1, edge : edge + 1] for v in range(NVAR)]
                for v in range(NVAR):
                    if side == 0:
                        right[v] = right[v] - slopes[v, t, 1:2]
                    else:
                        left[v] = left[v] + slopes[v, t, rows : rows + 1]
                flux = flux_of(left, right, 0)
                for v in range(NVAR):
                    add(faces, (t, slice(5 * side + v, 5 * side + v + 1)), flux[v])
        for s in range(rows // SUB):
            here = slice(SUB * s, SUB * (s + 1))
            padded = slice(PAD + SUB * s, PAD + SUB * (s + 1))
            left, right = [], []
            for v in range(NVAR):
                inner = roll(now[v, count, padded] + level.slope[v, count, here], 2 * depth)
                left.append(jnp.where(second, inner, now[v, 0, padded]))
                right.append(jnp.where(second, now[v, count + 1, padded], now[v, 1, padded] - level.slope[v, 1, here]))
            flux = flux_of(left, right, 1)
            for v in range(NVAR):
                add(sides, (v, here), flux[v])

        def store(v, t, s, tile, step=step, later=later):
            later[v, t + 1, PAD + SUB * s : PAD + SUB * (s + 1)] = tile
            if step == 1:
                out_ref[0, v, SUB * s : SUB * (s + 1), LANES * t : LANES * (t + 1)] = tile

        level.finish(now, store)

    within = ((lane % 32) // plan.depth) * (2 * depth) + (lane % plan.depth) * 2

    def pack(tiles):
        out = None
        for t, tile in enumerate(tiles):
            tile = tile + roll(tile, -1)
            tile = tile + roll(tile, -depth)
            tile = take(tile, within)
            out = tile if out is None else jnp.where(lane // 32 == t, tile, out)
        return out

    for v in range(NVAR):
        for half in range(plan.patch // SUB):
            row = PAD + 2 * SUB * half
            tiles = [
                q[v, t + 1, pl.ds(row, SUB, stride=2)] + q[v, t + 1, pl.ds(row + 1, SUB, stride=2)]
                for t in range(count)
            ]
            at = v * plan.patch + SUB * half
            pay_ref[at : at + SUB] = 0.125 * pack(tiles)
    pair = ((lane // plan.depth) % 2) * depth + (lane % plan.depth) * 2
    for half in range(plan.patch // SUB):
        out = None
        for v in range(NVAR):
            row = 2 * SUB * half
            tile = sides[v, pl.ds(row, SUB, stride=2)] + sides[v, pl.ds(row + 1, SUB, stride=2)]
            tile = take(tile + roll(tile, -1), pair)
            out = tile if out is None else jnp.where(lane // depth == v, tile, out)
        at = plan.side_at + SUB * half
        pay_ref[at : at + SUB] = 0.125 * out
    owner = jnp.zeros((SUB, LANES), jnp.float32) + site_ref[0, 0].astype(jnp.float32)
    pay_ref[plan.payload_rows - SUB : plan.payload_rows] = owner
    pay_ref[plan.face_at : plan.face_at + SUB] = 0.125 * pack([faces[t, 0:SUB] for t in range(count)])
    tail = pack([faces[t, SUB : 2 * SUB] for t in range(count)])
    pay_ref[plan.face_at + SUB : plan.face_at + SUB + 2] = 0.125 * tail[0:2]


def outer_kernel(plan, live_ref, c_ref, held_ref, low_ref, high_ref, before_ref, after_ref, out_ref, fine_ref, q, sem, *work):
    put = pltpu.make_async_copy(held_ref, fine_ref, sem)
    put.start()
    count, depth, rows = plan.count, plan.depth, plan.rows
    lane, single = lanes_of(), lanes_of(1)
    split(plan, c_ref, q)
    wide = 2 * depth
    blank = jnp.zeros((PAD, LANES), jnp.float32)
    for v in range(NVAR):
        for t in range(count):
            at = (v * count + t) * 2
            q[v, t + 1, 0:PAD] = blank
            q[v, t + 1, PAD + rows : 2 * PAD + rows] = blank
            q[v, t + 1, PAD - 2 : PAD] = before_ref[at : at + 2]
            q[v, t + 1, PAD + rows : PAD + rows + 2] = after_ref[at : at + 2]
        for s in range(rows // SUB):
            piece = v * (rows // SUB) + s
            at = plan.ring_rows + SUB * (piece // 8)
            slot = piece % 8
            row = PAD + SUB * s
            q[v, 0, row : row + SUB] = roll(low_ref[at : at + SUB], LANES - wide - slot * wide)
            q[v, count + 1, row : row + SUB] = roll(high_ref[at : at + SUB], -slot * wide)
    weight = courant * live_ref[0].astype(jnp.float32)
    level = Level(work, count, rows, depth, "full")
    slopes = level.slopes
    level.prepare(q)

    def store(v, t, s, tile):
        out_ref[v, SUB * s : SUB * (s + 1), LANES * t : LANES * (t + 1)] = tile

    level.finish(q, store)
    half = LANES // 2
    low_lane = (plan.start - 1) * depth
    high_lane = plan.end * depth - LANES
    at_low = (lane >= low_lane) & (lane < low_lane + depth)
    at_high = (lane >= high_lane) & (lane < high_lane + depth)
    for x in range(plan.start, plan.end, SUB):
        here, padded = slice(x, x + SUB), slice(PAD + x, PAD + x + SUB)
        cells = [[q[v, t + 1, padded] for v in range(NVAR)] for t in range(2)]
        slope = [[level.slope[v, t + 1, here] for v in range(NVAR)] for t in range(2)]
        left = [[c + d for c, d in zip(cells[t], slope[t])] for t in range(2)]
        right = [[c - d for c, d in zip(cells[t], slope[t])] for t in range(2)]
        last, first = level.last, level.first
        ahead = [
            jnp.where(last, roll(b, -depth), roll(a, -depth)) for a, b in zip(right[0], right[1])
        ]
        behind = [
            jnp.where(first, roll(a, depth), roll(b, depth)) for a, b in zip(left[0], left[1])
        ]
        low = flux_of(left[0], ahead, 1)
        high = flux_of(behind, right[1], 1)
        for v in range(NVAR):
            out_ref[v, here, 0:LANES] = out_ref[v, here, 0:LANES] + jnp.where(at_low, weight * low[v], 0.0)
            out_ref[v, here, LANES : 2 * LANES] = out_ref[v, here, LANES : 2 * LANES] - jnp.where(
                at_high, weight * high[v], 0.0
            )
    for side, x in enumerate((plan.start - 1, plan.end)):
        face = x if side == 0 else x - 1
        for t in range(2):
            left = [q[v, t + 1, PAD + face : PAD + face + 1] + slopes[v, t, face + 1 : face + 2] for v in range(NVAR)]
            right = [
                q[v, t + 1, PAD + face + 1 : PAD + face + 2] - slopes[v, t, face + 2 : face + 3]
                for v in range(NVAR)
            ]
            flux = flux_of(left, right, 0)
            inner = single >= half if t == 0 else single < half
            signed = weight if side == 0 else -weight
            for v in range(NVAR):
                at = (v, slice(x, x + 1), slice(LANES * t, LANES * (t + 1)))
                out_ref[at] = out_ref[at] + jnp.where(inner, signed * flux[v], 0.0)
    put.wait()


def patch_kernel(plan, others, live_ref, me_ref, c_ref, *refs):
    payloads = refs[: others + 1]
    out_ref, pay = refs[others + 1 :]
    depth = plan.depth
    lane, single = lanes_of(), lanes_of(1)
    mine = me_ref[0].astype(jnp.float32)
    owners = [
        jnp.broadcast_to(ref[plan.owner_at : plan.owner_at + 1], (SUB, LANES)) == mine for ref in payloads
    ]
    for at in range(0, plan.payload_rows, SUB):
        chosen = payloads[0][at : at + SUB]
        for k in range(1, others + 1):
            chosen = jnp.where(owners[k], payloads[k][at : at + SUB], chosen)
        pay[at : at + SUB] = chosen
    live = live_ref[0]
    weight = courant * live.astype(jnp.float32)
    present = jnp.full((SUB, LANES), live, jnp.int32) > 0
    half = LANES // 2
    low_lane = (plan.start - 1) * depth
    high_lane = plan.end * depth - LANES
    at_low = (lane >= low_lane) & (lane < low_lane + depth)
    at_high = (lane >= high_lane) & (lane < high_lane + depth)
    under = (present & (lane >= half), present & (lane < half))
    for v in range(NVAR):
        for x in range(0, plan.rows, SUB):
            here = slice(x, x + SUB)
            tiles = [c_ref[v, here, LANES * t : LANES * (t + 1)] for t in range(plan.count)]
            if plan.start <= x < plan.end:
                base = plan.side_at + x - plan.start
                side = pay[base : base + SUB]
                low = roll(side, low_lane - v * 2 * depth)
                high = roll(side, high_lane - v * 2 * depth - depth)
                tiles[0] = tiles[0] - jnp.where(at_low, weight * low, 0.0)
                tiles[1] = tiles[1] + jnp.where(at_high, weight * high, 0.0)
                base = v * plan.patch + x - plan.start
                average = roll(pay[base : base + SUB], half)
                for t in range(2):
                    tiles[t] = jnp.where(under[t], average, tiles[t])
            for t in range(plan.count):
                out_ref[v, here, LANES * t : LANES * (t + 1)] = tiles[t]
        for side, x in enumerate((plan.start - 1, plan.end)):
            at = plan.face_at + 5 * side + v
            register = roll(pay[at : at + 1], half)
            signed = -weight if side == 0 else weight
            for t in range(2):
                inner = single >= half if t == 0 else single < half
                at = (v, slice(x, x + 1), slice(LANES * t, LANES * (t + 1)))
                out_ref[at] = c_ref[at] + jnp.where(inner, signed * register, 0.0)


def call(body, out_shape, scratch, flops, moved, spaces, out_spaces=None):
    if out_spaces is None:
        out_spaces = jax.tree.map(lambda _: VMEM, out_shape)
    return pl.pallas_call(
        body,
        out_shape=out_shape,
        in_specs=[pl.BlockSpec(memory_space=space) for space in spaces],
        out_specs=jax.tree.map(lambda space: pl.BlockSpec(memory_space=space), out_spaces),
        scratch_shapes=scratch,
        cost_estimate=pl.CostEstimate(flops=flops, bytes_accessed=moved, transcendentals=0),
        compiler_params=pltpu.CompilerParams(vmem_limit_bytes=16 << 20),
    )


def rotate(array, axis, step):
    size = lax.axis_size(axis)
    return lax.ppermute(array, axis, [(i, (i + step) % size) for i in range(size)])


def shards(coarse_state, fine_state, slot_site, box_live):
    size = lax.axis_size("gy")
    plan = Plan(coarse_state.shape, fine_state.shape, size)
    f32 = jnp.float32
    shape = jax.ShapeDtypeStruct
    smem, anywhere = pltpu.SMEM, pl.ANY
    cells = VMEM((NVAR, plan.count + 2, plan.rows + 2 * PAD, LANES), f32)
    copying = pltpu.SemaphoreType.DMA
    sent = shape((plan.sent_rows, LANES), f32)
    edge = shape((24, LANES), f32)
    held_shape = shape(fine_state.shape, f32)
    up, down, mid, xup, xdown, held = call(
        partial(coarse_kernel, plan),
        (sent, sent, shape((plan.ring_rows, LANES), f32), edge, edge, held_shape),
        [cells, VMEM((NVAR, plan.count, plan.rows, LANES), f32), copying] + Level.work(plan.count, plan.rows),
        4_000_000,
        400_000,
        [VMEM, anywhere],
    )(coarse_state, fine_state)
    others = size - 1
    rings = {0: mid}
    for k in range(1, size):
        rings[k] = rotate(up if k == 1 else down if k == size - 1 else mid, "gy", k)
    before = rotate(xup, "gx", 1)
    after = rotate(xdown, "gx", -1)
    me = lax.axis_index("gy").astype(jnp.int32).reshape(1)
    fine_cells = VMEM((NVAR, plan.fine_count + 2, plan.fine_rows + 2 * PAD, LANES), f32)
    second, payload = call(
        partial(fine_kernel, plan, others),
        (held_shape, shape((plan.payload_rows, LANES), f32)),
        [
            fine_cells,
            fine_cells,
            VMEM((plan.fine_count, plan.line_rows, LANES), f32),
            VMEM((plan.fine_count, 2 * SUB, LANES), f32),
            VMEM((NVAR, plan.fine_rows, LANES), f32),
        ]
        + Level.work(plan.fine_count, plan.fine_rows),
        16_000_000,
        1_000_000,
        [smem, smem, VMEM] + [VMEM] * size,
    )(slot_site, me, held, *[rings[k] for k in range(size)])
    payloads = [payload] + [rotate(payload, "gy", k) for k in range(1, size)]
    coarse_new, fine_out = call(
        partial(outer_kernel, plan),
        (shape(coarse_state.shape, f32), held_shape),
        [cells, copying] + Level.work(plan.count, plan.rows),
        4_000_000,
        400_000,
        [smem] + [VMEM] * 6,
        (VMEM, anywhere),
    )(box_live, coarse_state, second, rings[1], rings[size - 1], before, after)
    coarse_out = call(
        partial(patch_kernel, plan, others),
        shape(coarse_state.shape, f32),
        [VMEM((plan.payload_rows, LANES), f32)],
        400_000,
        400_000,
        [smem, smem, VMEM] + [VMEM] * size,
    )(box_live, me, coarse_new, *payloads)
    return (coarse_out, fine_out)


def solution(mesh):
    return jax.shard_map(
        shards,
        mesh=mesh,
        in_specs=(
            P(None, "gx", "gy"),
            P(("gx", "gy"), None, None, None),
            P(("gx", "gy"), None),
            P(("gx", "gy")),
        ),
        out_specs=(P(None, "gx", "gy"), P(("gx", "gy"), None, None, None)),
        check_vma=False,
    )
```

time: 67.8 us -> 26.9 us (0.40)
  Pallas kernels: 49.8 us -> 8.13 us
    pallas_call x2 -> x3, Pallas kernels: 42.8 us -> 7.21 us  [the longest x1 5.48 us: shards(): call(partial(fine_kernel, plan, others), (held_shape, shape((plan.payload...]
    pallas_call x1, Pallas kernels: 6.99 us -> 0.92 us  [shards(): call(partial(coarse_kernel, plan), (sent, sent, shape((plan.ring_rows, LA...]
  transfers between devices with their start and end apart: 8 -> 8, of which waited for: 2 -> 2; matrix products, arithmetic and copies ran while one was open for 0% -> 0% of each run, Pallas kernels for 0% -> 4%
where the time goes in v1:
time: 26.9 us; the launch traced here: 26.7 us
  starting transfers between devices  11.4 us (42%)
  Pallas kernels  8.13 us (30%)
  waiting for transfers between devices  3.23 us (12%)
  local copies, waits for them, and re-layouts  2.54 us (9%)
  between operations  1.36 us (5%)
    ppermute x8, starting transfers between devices, rotate(): lax.ppermute(array, axis, [(i, (i + step) % size) for i in range(size)])  11.4 us
    pallas_call x1, Pallas kernels, shards(): call(partial(fine_kernel, plan, others), (held_shape, shape((plan.payload...  5.48 us
    ppermute x8, waiting for transfers between devices, rotate(): lax.ppermute(array, axis, [(i, (i + step) % size) for i in range(size)])  3.23 us
    unnamed x8, local copies, waits for them, and re-layouts  2.54 us
    pallas_call x1, Pallas kernels, shards(): call(partial(outer_kernel, plan), (shape(coarse_state.shape, f32), held_s...  0.95 us
    pallas_call x1, Pallas kernels, shards(): call(partial(coarse_kernel, plan), (sent, sent, shape((plan.ring_rows, LA...  0.92 us
    pallas_call x1, Pallas kernels, shards(): call(partial(patch_kernel, plan, others), shape(coarse_state.shape, f32),...  0.78 us
  transfers between devices with their start and end apart: 8, of which 2 were waited for; matrix products, arithmetic and copies ran while one was open for 0% of the time, Pallas kernels for 4%

profile of v1, /device:TPU:0, one launch (start us, length us, event | category | flops | bytes accessed | tf_op | source)
XLA Modules:
  0.0 26.7 jit_solution(8863114668988412363)
XLA Ops:
  0.6 0.0 copy-start
  0.6 0.9 %copy-done = f32[5,32,256]{2,1,0:T(8,128)S(1)} copy-done((f32[5,32,256]{2,1,0:T(8,128)S(1)}, f32[5,32,256]{2,1,0:T(8,128)}, u32[]{:S(2)}) %copy-start) | copy-done | bytes 163864
  1.5 0.0 copy-start.2
  1.6 1.0 %copy-done.2 = f32[1,5,32,512]{3,2,1,0:T(8,128)S(1)} copy-done((f32[1,5,32,512]{3,2,1,0:T(8,128)S(1)}, f32[1,5,32,512]{3,2,1,0:T(8,128)}, u32[]{:S(2)}) %copy-start.2) | copy-done | bytes 327704
  2.5 0.9 %shard_map.59 = (f32[72,128]{1,0:T(8,128)S(1)}, f32[72,128]{1,0:T(8,128)S(1)}, f32[48,128]{1,0:T(8,128)S(1)}, f32[24,128]{1,0:T(8,128)S(1)}, f32[24,128]{1,0:T(8,128)S(1)}, /*index=5*/f32[1,5,32,512]{3,2,1,0:T(8,128)S(1)}) custom-call(f32[5,32,256]{2,1,0:T(8,128)S(1)} %copy-done, f32[1,5,32,512]{3,2,1,0:T(8,128)S(1)} %copy-done.2), custom_call_target="tpu_custom_call" | custom-call | flops 4000000 | bytes 400000 | tf_op jit(solution)/shard_map/pallas_call | solution.py:586
  3.5 0.5 %collective-permute-start = (f32[72,128]{1,0:T(8,128)S(1)}, f32[72,128]{1,0:T(8,128)S(1)}, u32[]{:S(2)}, u32[]{:S(2)}) collective-permute-start(f32[72,128]{1,0:T(8,128)S(1)} %get-tuple-element.14), channel_id=1, source_target_pairs={{0,1},{1,2},{2,3},{3,0},{4,5},{5,6},{6,7},{7,4},{8,9},{9,10},{10,1... | collective-permute-start | bytes 110600 | tf_op jit(solution)/shard_map/ppermute | solution.py:572
  4.0 2.0 %collective-permute-start.2 = (f32[72,128]{1,0:T(8,128)S(1)}, f32[72,128]{1,0:T(8,128)S(1)}, u32[]{:S(2)}, u32[]{:S(2)}) collective-permute-start(f32[72,128]{1,0:T(8,128)S(1)} %get-tuple-element.15), channel_id=1, source_target_pairs={{0,3},{1,0},{2,1},{3,2},{4,7},{5,4},{6,5},{7,6},{8,11},{9,8},{10,9... | collective-permute-start | bytes 110600 | tf_op jit(solution)/shard_map/ppermute | solution.py:572
  6.0 2.2 %collective-permute-start.1 = (f32[48,128]{1,0:T(8,128)S(1)}, f32[48,128]{1,0:T(8,128)S(1)}, u32[]{:S(2)}, u32[]{:S(2)}) collective-permute-start(f32[48,128]{1,0:T(8,128)S(1)} %get-tuple-element.13.refs_0_), channel_id=1, source_target_pairs={{0,2},{1,3},{2,0},{3,1},{4,6},{5,7},{6,4},{7,5},{8,10},{9,11},{10,... | collective-permute-start | bytes 73736 | tf_op jit(solution)/shard_map/ppermute | solution.py:572
  8.2 2.2 %collective-permute-done.1.refs_2_ = f32[48,128]{1,0:T(8,128)S(1)} collective-permute-done((f32[48,128]{1,0:T(8,128)S(1)}, f32[48,128]{1,0:T(8,128)S(1)}, u32[]{:S(2)}, u32[]{:S(2)}) %collective-permute-start.1) | collective-permute-done | bytes 24608 | tf_op jit(solution)/shard_map/ppermute | solution.py:572
  10.4 0.0 collective-permute-done.refs_1_.low_ref
  10.4 0.0 collective-permute-done.2.refs_3_.high_ref
  10.4 0.0 copy-start.3
  10.5 0.7 %copy-done.3 = s32[1,2]{1,0:T(1,128)S(1)} copy-done((s32[1,2]{1,0:T(1,128)S(1)}, s32[1,2]{1,0:T(1,128)}, u32[]{:S(2)}) %copy-start.3) | copy-done | bytes 32
  11.1 0.0 copy-start.1
  11.1 5.5 %shard_map.60 = (f32[1,5,32,512]{3,2,1,0:T(8,128)S(1)}, f32[112,128]{1,0:T(8,128)S(1)}) custom-call(s32[1,2]{1,0:T(1,128)S(1)} %copy-done.3, s32[1]{0:T(128)} %bitcast.me_ref, f32[1,5,32,512]{3,2,1,0:T(8,128)S(1)} %get-tuple-element.12.f_ref, f32[48,128]{1,0:T(8,128)S(1)} %get-tuple-element.13.refs_0_, f32[72,128]{1,0:T(8,128)S(1)} %collective-permute-done.refs_1_.low_ref, ...), custom_call_target="tpu_custom_call" | custom-call | flops 16000000 | bytes 1000000 | tf_op jit(solution)/shard_map/pallas_call | solution.py:602
  16.6 0.1 collective-permute-start.7
  16.7 1.7 %collective-permute-start.6 = (f32[112,128]{1,0:T(8,128)S(1)}, f32[112,128]{1,0:T(8,128)S(1)}, u32[]{:S(2)}, u32[]{:S(2)}) collective-permute-start(f32[112,128]{1,0:T(8,128)S(1)} %get-tuple-element.20.refs_0_), channel_id=1, source_target_pairs={{0,2},{1,3},{2,0},{3,1},{4,6},{5,7},{6,4},{7,5},{8,10},{9,11},{10,... | collective-permute-start | bytes 172040 | tf_op jit(solution)/shard_map/ppermute | solution.py:572
  18.4 0.2 collective-permute-start.5
  18.5 1.5 %collective-permute-start.3 = (f32[24,128]{1,0:T(8,128)S(1)}, f32[24,128]{1,0:T(8,128)S(1)}, u32[]{:S(2)}, u32[]{:S(2)}) collective-permute-start(f32[24,128]{1,0:T(8,128)S(1)} %get-tuple-element.17), channel_id=1, source_target_pairs={{0,4},{4,8},{8,12},{12,16},{16,20},{20,24},{24,28},{28,0},{1,5},{5... | collective-permute-start | bytes 36872 | tf_op jit(solution)/shard_map/ppermute | solution.py:572
  20.0 3.2 %collective-permute-start.4 = (f32[24,128]{1,0:T(8,128)S(1)}, f32[24,128]{1,0:T(8,128)S(1)}, u32[]{:S(2)}, u32[]{:S(2)}) collective-permute-start(f32[24,128]{1,0:T(8,128)S(1)} %get-tuple-element.18), channel_id=1, source_target_pairs={{0,28},{4,0},{8,4},{12,8},{16,12},{20,16},{24,20},{28,24},{1,29},{... | collective-permute-start | bytes 36872 | tf_op jit(solution)/shard_map/ppermute | solution.py:572
  23.9 1.0 %collective-permute-done.3.before_ref = f32[24,128]{1,0:T(8,128)S(1)} collective-permute-done((f32[24,128]{1,0:T(8,128)S(1)}, f32[24,128]{1,0:T(8,128)S(1)}, u32[]{:S(2)}, u32[]{:S(2)}) %collective-permute-start.3) | collective-permute-done | bytes 12320 | tf_op jit(solution)/shard_map/ppermute | solution.py:572
  24.9 0.0 collective-permute-done.4.after_ref
  24.9 0.0 copy-done.1
  24.9 0.9 %shard_map.61 = (f32[5,32,256]{2,1,0:T(8,128)S(1)}, f32[1,5,32,512]{3,2,1,0:T(8,128)}) custom-call(s32[1]{0:T(128)S(6)} %copy.6.live_ref, f32[5,32,256]{2,1,0:T(8,128)S(1)} %copy-done.1, f32[1,5,32,512]{3,2,1,0:T(8,128)S(1)} %get-tuple-element.16.held_ref, f32[72,128]{1,0:T(8,128)S(1)} %collective-permute-done.refs_1_.low_ref, ...), custom_call_target="tpu_custom_call" | custom-call | flops 4000000 | bytes 400000 | tf_op jit(solution)/shard_map/pallas_call | solution.py:618
  25.9 0.0 collective-permute-done.7.refs_3_
  25.9 0.0 collective-permute-done.6.refs_2_
  25.9 0.0 collective-permute-done.5.refs_1_
  25.9 0.8 %shard_map.62 = f32[5,32,256]{2,1,0:T(8,128)} custom-call(s32[1]{0:T(128)S(6)} %copy.6.live_ref, s32[1]{0:T(128)} %bitcast.me_ref, f32[5,32,256]{2,1,0:T(8,128)S(1)} %get-tuple-element.19.c_ref, f32[112,128]{1,0:T(8,128)S(1)} %get-tuple-element.20.refs_0_, f32[112,128]{1,0:T(8,128)S(1)} %collective-permute-done.5.refs_1_, ...), custom_call_target="tpu_custom_call" | custom-call | flops 400000 | bytes 400000 | tf_op jit(solution)/shard_map/pallas_call | solution.py:627
Async XLA Ops:
  0.6 0.9 %copy-start = (f32[5,32,256]{2,1,0:T(8,128)S(1)}, f32[5,32,256]{2,1,0:T(8,128)}, u32[]{:S(2)}) copy-start(f32[5,32,256]{2,1,0:T(8,128)} %c_ref.3) | copy-start | bytes 491524
  1.5 1.0 %copy-start.2 = (f32[1,5,32,512]{3,2,1,0:T(8,128)S(1)}, f32[1,5,32,512]{3,2,1,0:T(8,128)}, u32[]{:S(2)}) copy-start(f32[1,5,32,512]{3,2,1,0:T(8,128)} %f_ref.1) | copy-start | bytes 983044
  3.5 7.0 %collective-permute-start = (f32[72,128]{1,0:T(8,128)S(1)}, f32[72,128]{1,0:T(8,128)S(1)}, u32[]{:S(2)}, u32[]{:S(2)}) collective-permute-start(f32[72,128]{1,0:T(8,128)S(1)} %get-tuple-element.14), channel_id=1, source_target_pairs={{0,1},{1,2},{2,3},{3,0},{4,5},{5,6},{6,7},{7,4},{8,9},{9,10},{10,1... | collective-permute-start | bytes 110600 | tf_op jit(solution)/shard_map/ppermute | solution.py:572
  4.0 6.5 %collective-permute-start.2 = (f32[72,128]{1,0:T(8,128)S(1)}, f32[72,128]{1,0:T(8,128)S(1)}, u32[]{:S(2)}, u32[]{:S(2)}) collective-permute-start(f32[72,128]{1,0:T(8,128)S(1)} %get-tuple-element.15), channel_id=1, source_target_pairs={{0,3},{1,0},{2,1},{3,2},{4,7},{5,4},{6,5},{7,6},{8,11},{9,8},{10,9... | collective-permute-start | bytes 110600 | tf_op jit(solution)/shard_map/ppermute | solution.py:572
  6.0 4.4 %collective-permute-start.1 = (f32[48,128]{1,0:T(8,128)S(1)}, f32[48,128]{1,0:T(8,128)S(1)}, u32[]{:S(2)}, u32[]{:S(2)}) collective-permute-start(f32[48,128]{1,0:T(8,128)S(1)} %get-tuple-element.13.refs_0_), channel_id=1, source_target_pairs={{0,2},{1,3},{2,0},{3,1},{4,6},{5,7},{6,4},{7,5},{8,10},{9,11},{10,... | collective-permute-start | bytes 73736 | tf_op jit(solution)/shard_map/ppermute | solution.py:572
  10.4 0.7 %copy-start.3 = (s32[1,2]{1,0:T(1,128)S(1)}, s32[1,2]{1,0:T(1,128)}, u32[]{:S(2)}) copy-start(s32[1,2]{1,0:T(1,128)} %site_ref.1) | copy-start | bytes 28
  11.1 13.8 %copy-start.1 = (f32[5,32,256]{2,1,0:T(8,128)S(1)}, f32[5,32,256]{2,1,0:T(8,128)}, u32[]{:S(2)}) copy-start(f32[5,32,256]{2,1,0:T(8,128)} %c_ref.3) | copy-start | bytes 491524
  16.6 9.3 %collective-permute-start.7 = (f32[112,128]{1,0:T(8,128)S(1)}, f32[112,128]{1,0:T(8,128)S(1)}, u32[]{:S(2)}, u32[]{:S(2)}) collective-permute-start(f32[112,128]{1,0:T(8,128)S(1)} %get-tuple-element.20.refs_0_), channel_id=1, source_target_pairs={{0,3},{1,0},{2,1},{3,2},{4,7},{5,4},{6,5},{7,6},{8,11},{9,8},{10,9... | collective-permute-start | bytes 172040 | tf_op jit(solution)/shard_map/ppermute | solution.py:572
  16.7 9.2 %collective-permute-start.6 = (f32[112,128]{1,0:T(8,128)S(1)}, f32[112,128]{1,0:T(8,128)S(1)}, u32[]{:S(2)}, u32[]{:S(2)}) collective-permute-start(f32[112,128]{1,0:T(8,128)S(1)} %get-tuple-element.20.refs_0_), channel_id=1, source_target_pairs={{0,2},{1,3},{2,0},{3,1},{4,6},{5,7},{6,4},{7,5},{8,10},{9,11},{10,... | collective-permute-start | bytes 172040 | tf_op jit(solution)/shard_map/ppermute | solution.py:572
  18.4 7.5 %collective-permute-start.5 = (f32[112,128]{1,0:T(8,128)S(1)}, f32[112,128]{1,0:T(8,128)S(1)}, u32[]{:S(2)}, u32[]{:S(2)}) collective-permute-start(f32[112,128]{1,0:T(8,128)S(1)} %get-tuple-element.20.refs_0_), channel_id=1, source_target_pairs={{0,1},{1,2},{2,3},{3,0},{4,5},{5,6},{6,7},{7,4},{8,9},{9,10},{10,1... | collective-permute-start | bytes 172040 | tf_op jit(solution)/shard_map/ppermute | solution.py:572
  18.5 6.4 %collective-permute-start.3 = (f32[24,128]{1,0:T(8,128)S(1)}, f32[24,128]{1,0:T(8,128)S(1)}, u32[]{:S(2)}, u32[]{:S(2)}) collective-permute-start(f32[24,128]{1,0:T(8,128)S(1)} %get-tuple-element.17), channel_id=1, source_target_pairs={{0,4},{4,8},{8,12},{12,16},{16,20},{20,24},{24,28},{28,0},{1,5},{5... | collective-permute-start | bytes 36872 | tf_op jit(solution)/shard_map/ppermute | solution.py:572
  20.0 4.9 %collective-permute-start.4 = (f32[24,128]{1,0:T(8,128)S(1)}, f32[24,128]{1,0:T(8,128)S(1)}, u32[]{:S(2)}, u32[]{:S(2)}) collective-permute-start(f32[24,128]{1,0:T(8,128)S(1)} %get-tuple-element.18), channel_id=1, source_target_pairs={{0,28},{4,0},{8,4},{12,8},{16,12},{20,16},{24,20},{28,24},{1,29},{... | collective-permute-start | bytes 36872 | tf_op jit(solution)/shard_map/ppermute | solution.py:572

commit v2 on v1

--- a/solution.py
+++ b/solution.py
@@ -236,9 +236,19 @@
     return jnp.where(lane < LANES // 2, low, high)
 
 
-def coarse_kernel(plan, c_ref, f_ref, up_ref, down_ref, mid_ref, xup_ref, xdown_ref, held_ref, q, fresh, sem, *work):
-    load = pltpu.make_async_copy(f_ref, held_ref, sem)
-    load.start()
+def coarse_kernel(
+    plan, site_hbm, c_hbm, f_hbm, up_ref, down_ref, mid_ref, xup_ref, xdown_ref, ids_ref, held_ref, c_ref,
+    q, fresh, site_ref, sems, *work
+):
+    loads = [
+        pltpu.make_async_copy(source, target, sems.at[index])
+        for index, (source, target) in enumerate(
+            ((c_hbm, c_ref), (f_hbm, held_ref), (site_hbm, site_ref))
+        )
+    ]
+    for load in loads:
+        load.start()
+    loads[0].wait()
     split(plan, c_ref, q)
     for v in range(NVAR):
         for t in range(plan.count):
@@ -309,14 +319,20 @@
             for t in range(plan.count):
                 at = (v * plan.count + t) * 2
                 ref[at : at + 2] = q[v, t + 1, PAD + x : PAD + x + 2]
-    load.wait()
-
-
-def fine_kernel(plan, others, site_ref, me_ref, f_ref, *refs):
+    for load in loads[1:]:
+        load.wait()
+    zero = jnp.zeros((SUB, LANES), jnp.float32)
+    for index, number in enumerate((site_ref[0, 0], lax.axis_index("gy"))):
+        ids_ref[SUB * index : SUB * (index + 1)] = zero + number.astype(jnp.float32)
+
+
+def fine_kernel(plan, others, ids_ref, f_ref, *refs):
     rings = refs[: others + 1]
     out_ref, pay_ref, q, q_later, lines, faces, sides = refs[others + 1 : others + 8]
     work = refs[others + 8 :]
-    turn = (me_ref[0] - site_ref[0, 0] + plan.size) % plan.size
+    owner = ids_ref[0:SUB]
+    gap = ids_ref[SUB : 2 * SUB] - owner
+    turn = jnp.where(gap < 0, gap + plan.size, gap)
     count, depth, rows = plan.fine_count, plan.fine_depth, plan.fine_rows
     lane = lanes_of()
     ring = []
@@ -338,14 +354,19 @@
                 at = 10 * level_id + 5 * side + v
                 for t in range(count):
                     q[v, t + 1, row : row + 2] = jnp.broadcast_to(lines[t, at : at + 1], (2, LANES))
-            for side, t in enumerate((0, count + 1)):
-                for half in range(plan.patch // SUB):
-                    piece = ((level_id * 2 + side) * NVAR + v) * 2 + half
-                    tile = ring[plan.line_rows // SUB + piece // 16]
-                    column = take(roll(tile, -(piece % 16) * plan.depth), spread)
-                    row = PAD + 2 * SUB * half
-                    q[v, t, pl.ds(row, SUB, stride=2)] = column
-                    q[v, t, pl.ds(row + 1, SUB, stride=2)] = column
+        places = [
+            (v, side, half) for v in range(NVAR) for side in range(2) for half in range(plan.patch // SUB)
+        ]
+        moved = []
+        for v, side, half in places:
+            piece = ((level_id * 2 + side) * NVAR + v) * 2 + half
+            tile = ring[plan.line_rows // SUB + piece // 16]
+            moved.append(roll(tile, -(piece % 16) * plan.depth))
+        moved = [take(tile, spread) for tile in moved]
+        for (v, side, half), column in zip(places, moved):
+            row = PAD + 2 * SUB * half
+            q[v, (count + 1) * side, pl.ds(row, SUB, stride=2)] = column
+            q[v, (count + 1) * side, pl.ds(row + 1, SUB, stride=2)] = column
 
     for v in range(NVAR):
         for t in range(count):
@@ -395,39 +416,47 @@
 
     within = ((lane % 32) // plan.depth) * (2 * depth) + (lane % plan.depth) * 2
 
-    def pack(tiles):
-        out = None
-        for t, tile in enumerate(tiles):
-            tile = tile + roll(tile, -1)
-            tile = tile + roll(tile, -depth)
-            tile = take(tile, within)
-            out = tile if out is None else jnp.where(lane // 32 == t, tile, out)
-        return out
-
+    groups = []
     for v in range(NVAR):
         for half in range(plan.patch // SUB):
             row = PAD + 2 * SUB * half
-            tiles = [
-                q[v, t + 1, pl.ds(row, SUB, stride=2)] + q[v, t + 1, pl.ds(row + 1, SUB, stride=2)]
-                for t in range(count)
-            ]
-            at = v * plan.patch + SUB * half
-            pay_ref[at : at + SUB] = 0.125 * pack(tiles)
+            groups.append(
+                [
+                    q[v, t + 1, pl.ds(row, SUB, stride=2)] + q[v, t + 1, pl.ds(row + 1, SUB, stride=2)]
+                    for t in range(count)
+                ]
+            )
+    for part in range(2):
+        groups.append([faces[t, SUB * part : SUB * (part + 1)] for t in range(count)])
+    beside = []
+    for v in range(NVAR):
+        for half in range(plan.patch // SUB):
+            row = 2 * SUB * half
+            beside.append(sides[v, pl.ds(row, SUB, stride=2)] + sides[v, pl.ds(row + 1, SUB, stride=2)])
+    groups = [[tile + roll(tile, -1) for tile in tiles] for tiles in groups]
+    beside = [tile + roll(tile, -1) for tile in beside]
+    groups = [[tile + roll(tile, -depth) for tile in tiles] for tiles in groups]
     pair = ((lane // plan.depth) % 2) * depth + (lane % plan.depth) * 2
-    for half in range(plan.patch // SUB):
-        out = None
-        for v in range(NVAR):
-            row = 2 * SUB * half
-            tile = sides[v, pl.ds(row, SUB, stride=2)] + sides[v, pl.ds(row + 1, SUB, stride=2)]
-            tile = take(tile + roll(tile, -1), pair)
-            out = tile if out is None else jnp.where(lane // depth == v, tile, out)
+    beside = [take(tile, pair) for tile in beside]
+    groups = [[take(tile, within) for tile in tiles] for tiles in groups]
+    packed = []
+    for tiles in groups:
+        out = tiles[0]
+        for t in range(1, count):
+            out = jnp.where(lane // 32 == t, tiles[t], out)
+        packed.append(0.125 * out)
+    halves = plan.patch // SUB
+    for at in range(NVAR * halves):
+        pay_ref[SUB * at : SUB * (at + 1)] = packed[at]
+    for half in range(halves):
+        out = beside[half]
+        for v in range(1, NVAR):
+            out = jnp.where(lane // depth == v, beside[v * halves + half], out)
         at = plan.side_at + SUB * half
         pay_ref[at : at + SUB] = 0.125 * out
-    owner = jnp.zeros((SUB, LANES), jnp.float32) + site_ref[0, 0].astype(jnp.float32)
     pay_ref[plan.payload_rows - SUB : plan.payload_rows] = owner
-    pay_ref[plan.face_at : plan.face_at + SUB] = 0.125 * pack([faces[t, 0:SUB] for t in range(count)])
-    tail = pack([faces[t, SUB : 2 * SUB] for t in range(count)])
-    pay_ref[plan.face_at + SUB : plan.face_at + SUB + 2] = 0.125 * tail[0:2]
+    pay_ref[plan.face_at : plan.face_at + SUB] = packed[-2]
+    pay_ref[plan.face_at + SUB : plan.face_at + SUB + 2] = packed[-1][0:2]
 
 
 def outer_kernel(plan, live_ref, c_ref, held_ref, low_ref, high_ref, before_ref, after_ref, out_ref, fine_ref, q, sem, *work):
@@ -503,12 +532,12 @@
     put.wait()
 
 
-def patch_kernel(plan, others, live_ref, me_ref, c_ref, *refs):
+def patch_kernel(plan, others, live_ref, ids_ref, c_ref, *refs):
     payloads = refs[: others + 1]
     out_ref, pay = refs[others + 1 :]
     depth = plan.depth
     lane, single = lanes_of(), lanes_of(1)
-    mine = me_ref[0].astype(jnp.float32)
+    mine = ids_ref[SUB : 2 * SUB]
     owners = [
         jnp.broadcast_to(ref[plan.owner_at : plan.owner_at + 1], (SUB, LANES)) == mine for ref in payloads
     ]
@@ -517,9 +546,9 @@
         for k in range(1, others + 1):
             chosen = jnp.where(owners[k], payloads[k][at : at + SUB], chosen)
         pay[at : at + SUB] = chosen
-    live = live_ref[0]
-    weight = courant * live.astype(jnp.float32)
-    present = jnp.full((SUB, LANES), live, jnp.int32) > 0
+    live = jnp.zeros((SUB, LANES), jnp.float32) + live_ref[0].astype(jnp.float32)
+    weight = courant * live
+    present = live > 0
     half = LANES // 2
     low_lane = (plan.start - 1) * depth
     high_lane = plan.end * depth - LANES
@@ -546,7 +575,7 @@
         for side, x in enumerate((plan.start - 1, plan.end)):
             at = plan.face_at + 5 * side + v
             register = roll(pay[at : at + 1], half)
-            signed = -weight if side == 0 else weight
+            signed = -weight[0:1] if side == 0 else weight[0:1]
             for t in range(2):
                 inner = single >= half if t == 0 else single < half
                 at = (v, slice(x, x + 1), slice(LANES * t, LANES * (t + 1)))
@@ -577,27 +606,28 @@
     plan = Plan(coarse_state.shape, fine_state.shape, size)
     f32 = jnp.float32
     shape = jax.ShapeDtypeStruct
-    smem, anywhere = pltpu.SMEM, pl.ANY
+    smem = pltpu.SMEM
     cells = VMEM((NVAR, plan.count + 2, plan.rows + 2 * PAD, LANES), f32)
     copying = pltpu.SemaphoreType.DMA
     sent = shape((plan.sent_rows, LANES), f32)
     edge = shape((24, LANES), f32)
     held_shape = shape(fine_state.shape, f32)
-    up, down, mid, xup, xdown, held = call(
+    coarse_shape = shape(coarse_state.shape, f32)
+    up, down, mid, xup, xdown, ids, held, coarse = call(
         partial(coarse_kernel, plan),
-        (sent, sent, shape((plan.ring_rows, LANES), f32), edge, edge, held_shape),
-        [cells, VMEM((NVAR, plan.count, plan.rows, LANES), f32), copying] + Level.work(plan.count, plan.rows),
+        (sent, sent, shape((plan.ring_rows, LANES), f32), edge, edge, edge, held_shape, coarse_shape),
+        [cells, VMEM((NVAR, plan.count, plan.rows, LANES), f32), smem((1, 2), jnp.int32), copying((3,))]
+        + Level.work(plan.count, plan.rows),
         4_000_000,
         400_000,
-        [VMEM, anywhere],
-    )(coarse_state, fine_state)
+        [pltpu.HBM] * 3,
+    )(*[pltpu.with_memory_space_constraint(x, pltpu.HBM) for x in (slot_site, coarse_state, fine_state)])
     others = size - 1
     rings = {0: mid}
     for k in range(1, size):
         rings[k] = rotate(up if k == 1 else down if k == size - 1 else mid, "gy", k)
     before = rotate(xup, "gx", 1)
     after = rotate(xdown, "gx", -1)
-    me = lax.axis_index("gy").astype(jnp.int32).reshape(1)
     fine_cells = VMEM((NVAR, plan.fine_count + 2, plan.fine_rows + 2 * PAD, LANES), f32)
     second, payload = call(
         partial(fine_kernel, plan, others),
@@ -612,26 +642,26 @@
         + Level.work(plan.fine_count, plan.fine_rows),
         16_000_000,
         1_000_000,
-        [smem, smem, VMEM] + [VMEM] * size,
-    )(slot_site, me, held, *[rings[k] for k in range(size)])
+        [VMEM, VMEM] + [VMEM] * size,
+    )(ids, held, *[rings[k] for k in range(size)])
     payloads = [payload] + [rotate(payload, "gy", k) for k in range(1, size)]
     coarse_new, fine_out = call(
         partial(outer_kernel, plan),
-        (shape(coarse_state.shape, f32), held_shape),
+        (coarse_shape, held_shape),
         [cells, copying] + Level.work(plan.count, plan.rows),
         4_000_000,
         400_000,
         [smem] + [VMEM] * 6,
-        (VMEM, anywhere),
-    )(box_live, coarse_state, second, rings[1], rings[size - 1], before, after)
+        (VMEM, pltpu.HBM),
+    )(box_live, coarse, second, rings[1], rings[size - 1], before, after)
     coarse_out = call(
         partial(patch_kernel, plan, others),
-        shape(coarse_state.shape, f32),
+        coarse_shape,
         [VMEM((plan.payload_rows, LANES), f32)],
         400_000,
         400_000,
-        [smem, smem, VMEM] + [VMEM] * size,
-    )(box_live, me, coarse_new, *payloads)
+        [smem, VMEM, VMEM] + [VMEM] * size,
+    )(box_live, ids, coarse_new, *payloads)
     return (coarse_out, fine_out)
 
 

time: 26.9 us -> 22.3 us (0.83)
  local copies, waits for them, and re-layouts: 2.54 us -> 0 us
  Pallas kernels: 8.13 us -> 6.18 us
    pallas_call x1, Pallas kernels: 5.48 us -> 2.69 us  [shards(): call(partial(fine_kernel, plan, others), (held_shape, shape((plan.payload...]
    unnamed x8 -> x0, local copies, waits for them, and re-layouts: 2.54 us -> none
    pallas_call x1, Pallas kernels: 0.92 us -> 1.76 us  [shards(): call(partial(coarse_kernel, plan), (sent, sent, shape((plan.ring_rows, LA...]
where the time goes in v2:
time: 22.3 us; the launch traced here: 22.2 us
  starting transfers between devices  11.4 us (51%)
  Pallas kernels  6.18 us (28%)
  waiting for transfers between devices  3.23 us (14%)
  between operations  1.34 us (6%)
    ppermute x8, starting transfers between devices, rotate(): lax.ppermute(array, axis, [(i, (i + step) % size) for i in range(size)])  11.4 us
    ppermute x8, waiting for transfers between devices, rotate(): lax.ppermute(array, axis, [(i, (i + step) % size) for i in range(size)])  3.23 us
    pallas_call x1, Pallas kernels, shards(): call(partial(fine_kernel, plan, others), (held_shape, shape((plan.payload...  2.69 us
    pallas_call x1, Pallas kernels, shards(): call(partial(coarse_kernel, plan), (sent, sent, shape((plan.ring_rows, LA...  1.76 us
    pallas_call x1, Pallas kernels, shards(): call(partial(outer_kernel, plan), (coarse_shape, held_shape), [cells, cop...  0.95 us
    pallas_call x1, Pallas kernels, shards(): call(partial(patch_kernel, plan, others), coarse_shape, [VMEM((plan.paylo...  0.78 us
  transfers between devices with their start and end apart: 8, of which 2 were waited for; matrix products, arithmetic and copies ran while one was open for 0% of the time, Pallas kernels for 4%

profile of v2, /device:TPU:0, one launch (start us, length us, event | category | flops | bytes accessed | tf_op | source)
XLA Modules:
  0.0 22.2 jit_solution(9621367402717576130)
XLA Ops:
  0.6 1.8 %shard_map.59 = (f32[72,128]{1,0:T(8,128)S(1)}, f32[72,128]{1,0:T(8,128)S(1)}, f32[48,128]{1,0:T(8,128)S(1)}, f32[24,128]{1,0:T(8,128)S(1)}, f32[24,128]{1,0:T(8...) custom-call(s32[1,2]{1,0:T(1,128)} %site_hbm.1, f32[5,32,256]{2,1,0:T(8,128)} %c_hbm.1, ...), custom_call_target="tpu_custom_call" | custom-call | flops 4000000 | bytes 400000 | tf_op jit(solution)/shard_map/pallas_call | solution.py:616
  2.4 0.5 %collective-permute-start = (f32[72,128]{1,0:T(8,128)S(1)}, f32[72,128]{1,0:T(8,128)S(1)}, u32[]{:S(2)}, u32[]{:S(2)}) collective-permute-start(f32[72,128]{1,0:T(8,128)S(1)} %get-tuple-element.18), channel_id=1, source_target_pairs={{0,1},{1,2},{2,3},{3,0},{4,5},{5,6},{6,7},{7,4},{8,9},{9,10},{10,1... | collective-permute-start | bytes 110600 | tf_op jit(solution)/shard_map/ppermute | solution.py:601
  2.9 2.0 %collective-permute-start.2 = (f32[72,128]{1,0:T(8,128)S(1)}, f32[72,128]{1,0:T(8,128)S(1)}, u32[]{:S(2)}, u32[]{:S(2)}) collective-permute-start(f32[72,128]{1,0:T(8,128)S(1)} %get-tuple-element.19), channel_id=1, source_target_pairs={{0,3},{1,0},{2,1},{3,2},{4,7},{5,4},{6,5},{7,6},{8,11},{9,8},{10,9... | collective-permute-start | bytes 110600 | tf_op jit(solution)/shard_map/ppermute | solution.py:601
  5.0 2.2 %collective-permute-start.1 = (f32[48,128]{1,0:T(8,128)S(1)}, f32[48,128]{1,0:T(8,128)S(1)}, u32[]{:S(2)}, u32[]{:S(2)}) collective-permute-start(f32[48,128]{1,0:T(8,128)S(1)} %get-tuple-element.17.refs_0_), channel_id=1, source_target_pairs={{0,2},{1,3},{2,0},{3,1},{4,6},{5,7},{6,4},{7,5},{8,10},{9,11},{10,... | collective-permute-start | bytes 73736 | tf_op jit(solution)/shard_map/ppermute | solution.py:601
  7.2 2.2 %collective-permute-done.1.refs_2_ = f32[48,128]{1,0:T(8,128)S(1)} collective-permute-done((f32[48,128]{1,0:T(8,128)S(1)}, f32[48,128]{1,0:T(8,128)S(1)}, u32[]{:S(2)}, u32[]{:S(2)}) %collective-permute-start.1) | collective-permute-done | bytes 24608 | tf_op jit(solution)/shard_map/ppermute | solution.py:601
  9.4 0.0 collective-permute-done.refs_1_.low_ref
  9.4 0.0 collective-permute-done.2.refs_3_.high_ref
  9.4 2.7 %shard_map.60 = (f32[1,5,32,512]{3,2,1,0:T(8,128)S(1)}, f32[112,128]{1,0:T(8,128)S(1)}) custom-call(f32[24,128]{1,0:T(8,128)S(1)} %get-tuple-element.14.ids_ref, f32[1,5,32,512]{3,2,1,0:T(8,128)S(1)} %get-tuple-element.16.f_ref, f32[48,128]{1,0:T(8,128)S(1)} %get-tuple-element.17.refs_0_, f32[72,128]{1,0:T(8,128)S(1)} %collective-permute-done.refs_1_.low_ref, ...), custom_call_target="tpu_custom_call" | custom-call | flops 16000000 | bytes 1000000 | tf_op jit(solution)/shard_map/pallas_call | solution.py:632
  12.1 0.1 collective-permute-start.7
  12.2 1.7 %collective-permute-start.6 = (f32[112,128]{1,0:T(8,128)S(1)}, f32[112,128]{1,0:T(8,128)S(1)}, u32[]{:S(2)}, u32[]{:S(2)}) collective-permute-start(f32[112,128]{1,0:T(8,128)S(1)} %get-tuple-element.24.refs_0_), channel_id=1, source_target_pairs={{0,2},{1,3},{2,0},{3,1},{4,6},{5,7},{6,4},{7,5},{8,10},{9,11},{10,... | collective-permute-start | bytes 172040 | tf_op jit(solution)/shard_map/ppermute | solution.py:601
  13.9 0.2 collective-permute-start.5
  14.0 1.5 %collective-permute-start.3 = (f32[24,128]{1,0:T(8,128)S(1)}, f32[24,128]{1,0:T(8,128)S(1)}, u32[]{:S(2)}, u32[]{:S(2)}) collective-permute-start(f32[24,128]{1,0:T(8,128)S(1)} %get-tuple-element.21), channel_id=1, source_target_pairs={{0,4},{4,8},{8,12},{12,16},{16,20},{20,24},{24,28},{28,0},{1,5},{5... | collective-permute-start | bytes 36872 | tf_op jit(solution)/shard_map/ppermute | solution.py:601
  15.5 3.2 %collective-permute-start.4 = (f32[24,128]{1,0:T(8,128)S(1)}, f32[24,128]{1,0:T(8,128)S(1)}, u32[]{:S(2)}, u32[]{:S(2)}) collective-permute-start(f32[24,128]{1,0:T(8,128)S(1)} %get-tuple-element.22), channel_id=1, source_target_pairs={{0,28},{4,0},{8,4},{12,8},{16,12},{20,16},{24,20},{28,24},{1,29},{... | collective-permute-start | bytes 36872 | tf_op jit(solution)/shard_map/ppermute | solution.py:601
  19.4 1.0 %collective-permute-done.3.before_ref = f32[24,128]{1,0:T(8,128)S(1)} collective-permute-done((f32[24,128]{1,0:T(8,128)S(1)}, f32[24,128]{1,0:T(8,128)S(1)}, u32[]{:S(2)}, u32[]{:S(2)}) %collective-permute-start.3) | collective-permute-done | bytes 12320 | tf_op jit(solution)/shard_map/ppermute | solution.py:601
  20.4 0.0 collective-permute-done.4.after_ref
  20.4 0.9 %shard_map.61 = (f32[5,32,256]{2,1,0:T(8,128)S(1)}, f32[1,5,32,512]{3,2,1,0:T(8,128)}) custom-call(s32[1]{0:T(128)S(6)} %copy.6.live_ref, f32[5,32,256]{2,1,0:T(8,128)S(1)} %get-tuple-element.15.c_ref, f32[1,5,32,512]{3,2,1,0:T(8,128)S(1)} %get-tuple-element.20.held_ref, f32[72,128]{1,0:T(8,128)S(1)} %collective-permute-done.refs_1_.low_ref, ...), custom_call_target="tpu_custom_call" | custom-call | flops 4000000 | bytes 400000 | tf_op jit(solution)/shard_map/pallas_call | solution.py:648
  21.4 0.0 collective-permute-done.7.refs_3_
  21.4 0.0 collective-permute-done.6.refs_2_
  21.4 0.0 collective-permute-done.5.refs_1_
  21.4 0.8 %shard_map.62 = f32[5,32,256]{2,1,0:T(8,128)} custom-call(s32[1]{0:T(128)S(6)} %copy.6.live_ref, f32[24,128]{1,0:T(8,128)S(1)} %get-tuple-element.14.ids_ref, f32[5,32,256]{2,1,0:T(8,128)S(1)} %get-tuple-element.23.c_ref, f32[112,128]{1,0:T(8,128)S(1)} %get-tuple-element.24.refs_0_, f32[112,128]{1,0:T(8,128)S(1)} %collective-permute-done.5.refs_1_, ...), custom_call_target="tpu_custom_call" | custom-call | flops 400000 | bytes 400000 | tf_op jit(solution)/shard_map/pallas_call | solution.py:657
Async XLA Ops:
  2.4 7.0 %collective-permute-start = (f32[72,128]{1,0:T(8,128)S(1)}, f32[72,128]{1,0:T(8,128)S(1)}, u32[]{:S(2)}, u32[]{:S(2)}) collective-permute-start(f32[72,128]{1,0:T(8,128)S(1)} %get-tuple-element.18), channel_id=1, source_target_pairs={{0,1},{1,2},{2,3},{3,0},{4,5},{5,6},{6,7},{7,4},{8,9},{9,10},{10,1... | collective-permute-start | bytes 110600 | tf_op jit(solution)/shard_map/ppermute | solution.py:601
  2.9 6.5 %collective-permute-start.2 = (f32[72,128]{1,0:T(8,128)S(1)}, f32[72,128]{1,0:T(8,128)S(1)}, u32[]{:S(2)}, u32[]{:S(2)}) collective-permute-start(f32[72,128]{1,0:T(8,128)S(1)} %get-tuple-element.19), channel_id=1, source_target_pairs={{0,3},{1,0},{2,1},{3,2},{4,7},{5,4},{6,5},{7,6},{8,11},{9,8},{10,9... | collective-permute-start | bytes 110600 | tf_op jit(solution)/shard_map/ppermute | solution.py:601
  5.0 4.4 %collective-permute-start.1 = (f32[48,128]{1,0:T(8,128)S(1)}, f32[48,128]{1,0:T(8,128)S(1)}, u32[]{:S(2)}, u32[]{:S(2)}) collective-permute-start(f32[48,128]{1,0:T(8,128)S(1)} %get-tuple-element.17.refs_0_), channel_id=1, source_target_pairs={{0,2},{1,3},{2,0},{3,1},{4,6},{5,7},{6,4},{7,5},{8,10},{9,11},{10,... | collective-permute-start | bytes 73736 | tf_op jit(solution)/shard_map/ppermute | solution.py:601
  12.1 9.3 %collective-permute-start.7 = (f32[112,128]{1,0:T(8,128)S(1)}, f32[112,128]{1,0:T(8,128)S(1)}, u32[]{:S(2)}, u32[]{:S(2)}) collective-permute-start(f32[112,128]{1,0:T(8,128)S(1)} %get-tuple-element.24.refs_0_), channel_id=1, source_target_pairs={{0,3},{1,0},{2,1},{3,2},{4,7},{5,4},{6,5},{7,6},{8,11},{9,8},{10,9... | collective-permute-start | bytes 172040 | tf_op jit(solution)/shard_map/ppermute | solution.py:601
  12.2 9.2 %collective-permute-start.6 = (f32[112,128]{1,0:T(8,128)S(1)}, f32[112,128]{1,0:T(8,128)S(1)}, u32[]{:S(2)}, u32[]{:S(2)}) collective-permute-start(f32[112,128]{1,0:T(8,128)S(1)} %get-tuple-element.24.refs_0_), channel_id=1, source_target_pairs={{0,2},{1,3},{2,0},{3,1},{4,6},{5,7},{6,4},{7,5},{8,10},{9,11},{10,... | collective-permute-start | bytes 172040 | tf_op jit(solution)/shard_map/ppermute | solution.py:601
  13.9 7.5 %collective-permute-start.5 = (f32[112,128]{1,0:T(8,128)S(1)}, f32[112,128]{1,0:T(8,128)S(1)}, u32[]{:S(2)}, u32[]{:S(2)}) collective-permute-start(f32[112,128]{1,0:T(8,128)S(1)} %get-tuple-element.24.refs_0_), channel_id=1, source_target_pairs={{0,1},{1,2},{2,3},{3,0},{4,5},{5,6},{6,7},{7,4},{8,9},{9,10},{10,1... | collective-permute-start | bytes 172040 | tf_op jit(solution)/shard_map/ppermute | solution.py:601
  14.0 6.4 %collective-permute-start.3 = (f32[24,128]{1,0:T(8,128)S(1)}, f32[24,128]{1,0:T(8,128)S(1)}, u32[]{:S(2)}, u32[]{:S(2)}) collective-permute-start(f32[24,128]{1,0:T(8,128)S(1)} %get-tuple-element.21), channel_id=1, source_target_pairs={{0,4},{4,8},{8,12},{12,16},{16,20},{20,24},{24,28},{28,0},{1,5},{5... | collective-permute-start | bytes 36872 | tf_op jit(solution)/shard_map/ppermute | solution.py:601
  15.5 4.9 %collective-permute-start.4 = (f32[24,128]{1,0:T(8,128)S(1)}, f32[24,128]{1,0:T(8,128)S(1)}, u32[]{:S(2)}, u32[]{:S(2)}) collective-permute-start(f32[24,128]{1,0:T(8,128)S(1)} %get-tuple-element.22), channel_id=1, source_target_pairs={{0,28},{4,0},{8,4},{12,8},{16,12},{20,16},{24,20},{28,24},{1,29},{... | collective-permute-start | bytes 36872 | tf_op jit(solution)/shard_map/ppermute | solution.py:601

commit v3 on v2

--- a/solution.py
+++ b/solution.py
@@ -6,6 +6,7 @@
 from jax.experimental import pallas as pl
 from jax.experimental.pallas import tpu as pltpu
 from jax.sharding import PartitionSpec as P
+
 
 LANES = 128
 SUB = 8
@@ -215,9 +216,15 @@
         self.start = (self.rows - self.patch) // 2
         self.end = self.start + self.patch
         self.size = size
+        self.paired = size & (size - 1) == 0
+        self.exchanges = list(range(size // 2, size)) + list(range(1, size // 2))
+        near = {1, size - 1}
+        self.near = [k for k in self.exchanges if any((self.target(i, k) - i) % size in near for i in range(size))]
         self.line_rows = 24
+        self.source_at = 20
         self.ring_rows = 48
         self.sent_rows = 72
+        self.edge_rows = 24
         self.average_rows = NVAR * self.patch
         self.side_at = self.average_rows
         self.face_at = self.side_at + self.patch
@@ -225,21 +232,28 @@
         self.payload_rows = self.owner_at + 6
 
 
+    def target(self, i, k):
+        return i ^ k if self.paired else (i + k) % self.size
+
+
 def split(plan, c_ref, q):
     for v in range(NVAR):
         for t in range(plan.count):
             q[v, t + 1, PAD : PAD + plan.rows] = c_ref[v, :, LANES * t : LANES * (t + 1)]
 
 
-def window_row(plan, tiles, lane):
+def window_row(tiles, lane):
     low, high = (roll(tile, LANES // 2) for tile in tiles)
     return jnp.where(lane < LANES // 2, low, high)
 
 
 def coarse_kernel(
-    plan, site_hbm, c_hbm, f_hbm, up_ref, down_ref, mid_ref, xup_ref, xdown_ref, ids_ref, held_ref, c_ref,
-    q, fresh, site_ref, sems, *work
+    plan, site_hbm, c_hbm, f_hbm, mid_ref, rows_ref, ids_ref, held_ref, c_ref, *refs
 ):
+    near_refs = refs[: len(plan.near)]
+    q, fresh, site_ref, sems = refs[len(plan.near) : len(plan.near) + 4]
+    work = refs[len(plan.near) + 4 :]
+    me = lax.axis_index("gy")
     loads = [
         pltpu.make_async_copy(source, target, sems.at[index])
         for index, (source, target) in enumerate(
@@ -265,10 +279,11 @@
 
     level.finish(q, store)
     lane, single = lanes_of(), lanes_of(1)
-    sent = (up_ref, down_ref, mid_ref)
+    sent = (mid_ref, *near_refs)
     blank = jnp.zeros((SUB, LANES), jnp.float32)
+    mine = blank + me.astype(jnp.float32)
     for ref in sent:
-        ref[16:24] = blank
+        ref[16:24] = mine
     for level_id in range(2):
         for side, x in enumerate((plan.start - 1, plan.end)):
             for v in range(NVAR):
@@ -276,7 +291,7 @@
                     tiles = [q[v, t + 1, PAD + x : PAD + x + 1] for t in range(2)]
                 else:
                     tiles = [fresh[v, t, x : x + 1] for t in range(2)]
-                line = window_row(plan, tiles, single)
+                line = window_row(tiles, single)
                 at = 10 * level_id + 5 * side + v
                 for ref in sent:
                     ref[at : at + 1] = line
@@ -302,7 +317,8 @@
         for ref in sent:
             ref[plan.line_rows + SUB * index : plan.line_rows + SUB * (index + 1)] = tile
     wide = 2 * depth
-    for ref, t, at in ((up_ref, plan.count - 1, LANES - wide), (down_ref, 0, 0)):
+    edges = []
+    for t, at in ((plan.count - 1, LANES - wide), (0, 0)):
         packed = [None] * 3
         for v in range(NVAR):
             for s in range(plan.rows // SUB):
@@ -311,18 +327,23 @@
                 moved = roll(q[v, t + 1, PAD + SUB * s : PAD + SUB * (s + 1)], slot * wide - at)
                 where, old = piece // 8, packed[piece // 8]
                 packed[where] = moved if old is None else jnp.where(lane // wide == slot, moved, old)
-        for index, tile in enumerate(packed):
-            ref[plan.ring_rows + SUB * index : plan.ring_rows + SUB * (index + 1)] = tile
-    for ref, x in ((xup_ref, plan.rows - 2), (xdown_ref, 0)):
-        ref[16:24] = blank
+        edges.append(packed)
+    for k, ref in zip(plan.near, near_refs):
+        upward = plan.target(me, k) == (me + 1) % plan.size
+        for index in range(3):
+            ref[plan.ring_rows + SUB * index : plan.ring_rows + SUB * (index + 1)] = jnp.where(
+                upward, edges[0][index], edges[1][index]
+            )
+    for base, x in ((0, plan.rows - 2), (plan.edge_rows, 0)):
+        rows_ref[base + 16 : base + 24] = blank
         for v in range(NVAR):
             for t in range(plan.count):
-                at = (v * plan.count + t) * 2
-                ref[at : at + 2] = q[v, t + 1, PAD + x : PAD + x + 2]
+                at = base + (v * plan.count + t) * 2
+                rows_ref[at : at + 2] = q[v, t + 1, PAD + x : PAD + x + 2]
     for load in loads[1:]:
         load.wait()
     zero = jnp.zeros((SUB, LANES), jnp.float32)
-    for index, number in enumerate((site_ref[0, 0], lax.axis_index("gy"))):
+    for index, number in enumerate((site_ref[0, 0], me, (me + 1) % plan.size, (me + plan.size - 1) % plan.size)):
         ids_ref[SUB * index : SUB * (index + 1)] = zero + number.astype(jnp.float32)
 
 
@@ -331,15 +352,14 @@
     out_ref, pay_ref, q, q_later, lines, faces, sides = refs[others + 1 : others + 8]
     work = refs[others + 8 :]
     owner = ids_ref[0:SUB]
-    gap = ids_ref[SUB : 2 * SUB] - owner
-    turn = jnp.where(gap < 0, gap + plan.size, gap)
+    sources = [jnp.broadcast_to(ref[plan.source_at : plan.source_at + 1], (SUB, LANES)) == owner for ref in rings]
     count, depth, rows = plan.fine_count, plan.fine_depth, plan.fine_rows
     lane = lanes_of()
     ring = []
     for at in range(0, plan.ring_rows, SUB):
         chosen = rings[0][at : at + SUB]
         for k in range(1, others + 1):
-            chosen = jnp.where(turn == k, rings[k][at : at + SUB], chosen)
+            chosen = jnp.where(sources[k], rings[k][at : at + SUB], chosen)
         ring.append(chosen)
     for t in range(count):
         cells = (lane // depth + t * (LANES // depth)) // 2
@@ -459,7 +479,10 @@
     pay_ref[plan.face_at + SUB : plan.face_at + SUB + 2] = packed[-1][0:2]
 
 
-def outer_kernel(plan, live_ref, c_ref, held_ref, low_ref, high_ref, before_ref, after_ref, out_ref, fine_ref, q, sem, *work):
+def outer_kernel(plan, live_ref, ids_ref, c_ref, held_ref, before_ref, after_ref, *refs):
+    near_refs = refs[: len(plan.near)]
+    out_ref, fine_ref, q, sem = refs[len(plan.near) : len(plan.near) + 4]
+    work = refs[len(plan.near) + 4 :]
     put = pltpu.make_async_copy(held_ref, fine_ref, sem)
     put.start()
     count, depth, rows = plan.count, plan.depth, plan.rows
@@ -473,14 +496,24 @@
             q[v, t + 1, 0:PAD] = blank
             q[v, t + 1, PAD + rows : 2 * PAD + rows] = blank
             q[v, t + 1, PAD - 2 : PAD] = before_ref[at : at + 2]
-            q[v, t + 1, PAD + rows : PAD + rows + 2] = after_ref[at : at + 2]
+            q[v, t + 1, PAD + rows : PAD + rows + 2] = after_ref[plan.edge_rows + at : plan.edge_rows + at + 2]
+    columns = []
+    for side in range(2):
+        wanted = ids_ref[SUB * (3 - side) : SUB * (4 - side)]
+        chosen = [blank] * 3
+        for ref in near_refs:
+            found = jnp.broadcast_to(ref[plan.source_at : plan.source_at + 1], (SUB, LANES)) == wanted
+            for index in range(3):
+                at = plan.ring_rows + SUB * index
+                chosen[index] = jnp.where(found, ref[at : at + SUB], chosen[index])
+        columns.append(chosen)
+    for v in range(NVAR):
         for s in range(rows // SUB):
             piece = v * (rows // SUB) + s
-            at = plan.ring_rows + SUB * (piece // 8)
             slot = piece % 8
             row = PAD + SUB * s
-            q[v, 0, row : row + SUB] = roll(low_ref[at : at + SUB], LANES - wide - slot * wide)
-            q[v, count + 1, row : row + SUB] = roll(high_ref[at : at + SUB], -slot * wide)
+            q[v, 0, row : row + SUB] = roll(columns[0][piece // 8], LANES - wide - slot * wide)
+            q[v, count + 1, row : row + SUB] = roll(columns[1][piece // 8], -slot * wide)
     weight = courant * live_ref[0].astype(jnp.float32)
     level = Level(work, count, rows, depth, "full")
     slopes = level.slopes
@@ -596,12 +629,7 @@
     )
 
 
-def rotate(array, axis, step):
-    size = lax.axis_size(axis)
-    return lax.ppermute(array, axis, [(i, (i + step) % size) for i in range(size)])
-
-
-def shards(coarse_state, fine_state, slot_site, box_live):
+def step(coarse_state, fine_state, slot_site, box_live):
     size = lax.axis_size("gy")
     plan = Plan(coarse_state.shape, fine_state.shape, size)
     f32 = jnp.float32
@@ -610,27 +638,31 @@
     cells = VMEM((NVAR, plan.count + 2, plan.rows + 2 * PAD, LANES), f32)
     copying = pltpu.SemaphoreType.DMA
     sent = shape((plan.sent_rows, LANES), f32)
-    edge = shape((24, LANES), f32)
+    edge = shape((2 * plan.edge_rows, LANES), f32)
     held_shape = shape(fine_state.shape, f32)
     coarse_shape = shape(coarse_state.shape, f32)
-    up, down, mid, xup, xdown, ids, held, coarse = call(
+    near = plan.near
+    mid, edges, ids, held, coarse, *edged = call(
         partial(coarse_kernel, plan),
-        (sent, sent, shape((plan.ring_rows, LANES), f32), edge, edge, edge, held_shape, coarse_shape),
+        (shape((plan.ring_rows, LANES), f32), edge, shape((4 * SUB, LANES), f32), held_shape, coarse_shape)
+        + (sent,) * len(near),
         [cells, VMEM((NVAR, plan.count, plan.rows, LANES), f32), smem((1, 2), jnp.int32), copying((3,))]
         + Level.work(plan.count, plan.rows),
         4_000_000,
         400_000,
         [pltpu.HBM] * 3,
     )(*[pltpu.with_memory_space_constraint(x, pltpu.HBM) for x in (slot_site, coarse_state, fine_state)])
-    others = size - 1
-    rings = {0: mid}
-    for k in range(1, size):
-        rings[k] = rotate(up if k == 1 else down if k == size - 1 else mid, "gy", k)
-    before = rotate(xup, "gx", 1)
-    after = rotate(xdown, "gx", -1)
+    buffers = dict(zip(near, edged))
+    pairs = {k: [(i, plan.target(i, k)) for i in range(size)] for k in plan.exchanges}
+    rings = {k: lax.ppermute(buffers.get(k, mid), "gy", pairs[k]) for k in plan.exchanges}
+    length = lax.axis_size("gx")
+    rise = [(i, (i + 1) % length) for i in range(length)]
+    fall = [(j, i) for i, j in rise]
+    before = lax.ppermute(edges, "gx", rise)
+    after = lax.ppermute(edges, "gx", fall)
     fine_cells = VMEM((NVAR, plan.fine_count + 2, plan.fine_rows + 2 * PAD, LANES), f32)
     second, payload = call(
-        partial(fine_kernel, plan, others),
+        partial(fine_kernel, plan, size - 1),
         (held_shape, shape((plan.payload_rows, LANES), f32)),
         [
             fine_cells,
@@ -643,19 +675,19 @@
         16_000_000,
         1_000_000,
         [VMEM, VMEM] + [VMEM] * size,
-    )(ids, held, *[rings[k] for k in range(size)])
-    payloads = [payload] + [rotate(payload, "gy", k) for k in range(1, size)]
+    )(ids, held, mid, *[rings[k] for k in plan.exchanges])
+    payloads = [payload] + [lax.ppermute(payload, "gy", pairs[k]) for k in plan.exchanges]
     coarse_new, fine_out = call(
         partial(outer_kernel, plan),
         (coarse_shape, held_shape),
         [cells, copying] + Level.work(plan.count, plan.rows),
         4_000_000,
         400_000,
-        [smem] + [VMEM] * 6,
+        [smem] + [VMEM] * (5 + len(near)),
         (VMEM, pltpu.HBM),
-    )(box_live, coarse, second, rings[1], rings[size - 1], before, after)
+    )(box_live, ids, coarse, second, before, after, *[rings[k] for k in near])
     coarse_out = call(
-        partial(patch_kernel, plan, others),
+        partial(patch_kernel, plan, size - 1),
         coarse_shape,
         [VMEM((plan.payload_rows, LANES), f32)],
         400_000,
@@ -667,7 +699,7 @@
 
 def solution(mesh):
     return jax.shard_map(
-        shards,
+        step,
         mesh=mesh,
         in_specs=(
             P(None, "gx", "gy"),

time: 22.3 us -> 27.3 us (1.22)
  waiting for transfers between devices: 3.23 us -> 9.67 us
  starting transfers between devices: 11.4 us -> 9.95 us
    ppermute x8, waiting for transfers between devices: 3.23 us -> 9.67 us  [the longest x1 5 us: step(): before = lax.ppermute(edges, 'gx', rise)]
    ppermute x8, starting transfers between devices: 11.4 us -> 9.95 us  [the longest x1 4.53 us: step(): after = lax.ppermute(edges, 'gx', fall)]
  transfers between devices with their start and end apart: 8 -> 8, of which waited for: 2 -> 3; matrix products, arithmetic and copies ran while one was open for 0% -> 0% of each run, Pallas kernels for 4% -> 3%
where the time goes in v3:
time: 27.3 us; the launch traced here: 27.1 us
  starting transfers between devices  9.95 us (36%)
  waiting for transfers between devices  9.67 us (35%)
  Pallas kernels  6.17 us (23%)
  between operations  1.34 us (5%)
    ppermute x1, waiting for transfers between devices, step(): before = lax.ppermute(edges, 'gx', rise)  5 us
    ppermute x1, starting transfers between devices, step(): after = lax.ppermute(edges, 'gx', fall)  4.53 us
    ppermute x3, waiting for transfers between devices, step(): lax.ppermute(buffers.get(k, mid), 'gy', pairs[k])  3.79 us
    ppermute x3, starting transfers between devices, step(): lax.ppermute(buffers.get(k, mid), 'gy', pairs[k])  3.22 us
    pallas_call x1, Pallas kernels, step(): call(partial(fine_kernel, plan, size - 1), (held_shape, shape((plan.paylo...  2.69 us
    ppermute x3, starting transfers between devices, step(): lax.ppermute(payload, 'gy', pairs[k])  2.2 us
    pallas_call x1, Pallas kernels, step(): call(partial(coarse_kernel, plan), (shape((plan.ring_rows, LANES), f32),...  1.76 us
    pallas_call x1, Pallas kernels, step(): call(partial(outer_kernel, plan), (coarse_shape, held_shape), [cells, cop...  0.95 us
  transfers between devices with their start and end apart: 8, of which 3 were waited for; matrix products, arithmetic and copies ran while one was open for 0% of the time, Pallas kernels for 3%

profile of v3, /device:TPU:0, one launch (start us, length us, event | category | flops | bytes accessed | tf_op | source)
XLA Modules:
  0.0 27.1 jit_solution(10212184913715053332)
XLA Ops:
  0.6 1.8 %shard_map.59 = (f32[48,128]{1,0:T(8,128)S(1)}, f32[48,128]{1,0:T(8,128)S(1)}, f32[32,128]{1,0:T(8,128)S(1)}, f32[1,5,32,512]{3,2,1,0:T(8,128)S(1)}, f32[5,32,25...) custom-call(s32[1,2]{1,0:T(1,128)} %site_hbm.1, f32[5,32,256]{2,1,0:T(8,128)} %c_hbm.1, ...), custom_call_target="tpu_custom_call" | custom-call | flops 4000000 | bytes 400000 | tf_op jit(solution)/shard_map/pallas_call | solution.py:645
  2.4 2.5 %collective-permute-start.1 = (f32[72,128]{1,0:T(8,128)S(1)}, f32[72,128]{1,0:T(8,128)S(1)}, u32[]{:S(2)}, u32[]{:S(2)}) collective-permute-start(f32[72,128]{1,0:T(8,128)S(1)} %get-tuple-element.17), channel_id=1, source_target_pairs={{0,3},{1,2},{2,1},{3,0},{4,7},{5,6},{6,5},{7,4},{8,11},{9,10},{10,... | collective-permute-start | bytes 110600 | tf_op jit(solution)/shard_map/ppermute | solution.py:657
  4.9 0.7 %collective-permute-start.2 = (f32[72,128]{1,0:T(8,128)S(1)}, f32[72,128]{1,0:T(8,128)S(1)}, u32[]{:S(2)}, u32[]{:S(2)}) collective-permute-start(f32[72,128]{1,0:T(8,128)S(1)} %get-tuple-element.18), channel_id=1, source_target_pairs={{0,1},{1,0},{2,3},{3,2},{4,5},{5,4},{6,7},{7,6},{8,9},{9,8},{10,11... | collective-permute-start | bytes 110600 | tf_op jit(solution)/shard_map/ppermute | solution.py:657
  5.6 0.0 collective-permute-start
  5.6 3.8 %collective-permute-done.refs_1_ = f32[48,128]{1,0:T(8,128)S(1)} collective-permute-done((f32[48,128]{1,0:T(8,128)S(1)}, f32[48,128]{1,0:T(8,128)S(1)}, u32[]{:S(2)}, u32[]{:S(2)}) %collective-permute-start) | collective-permute-done | bytes 24608 | tf_op jit(solution)/shard_map/ppermute | solution.py:657
  9.4 0.0 collective-permute-done.1.refs_2_.refs_0_
  9.4 0.0 collective-permute-done.2.refs_3_.refs_1_
  9.4 2.7 %shard_map.60 = (f32[1,5,32,512]{3,2,1,0:T(8,128)S(1)}, f32[112,128]{1,0:T(8,128)S(1)}) custom-call(f32[32,128]{1,0:T(8,128)S(1)} %get-tuple-element.13.ids_ref, f32[1,5,32,512]{3,2,1,0:T(8,128)S(1)} %get-tuple-element.15.f_ref, f32[48,128]{1,0:T(8,128)S(1)} %get-tuple-element.16.refs_0_, f32[48,128]{1,0:T(8,128)S(1)} %collective-permute-done.refs_1_, ...), custom_call_target="tpu_custom_call" | custom-call | flops 16000000 | bytes 1000000 | tf_op jit(solution)/shard_map/pallas_call | solution.py:664
  12.1 0.1 collective-permute-start.7
  12.2 0.5 %collective-permute-start.6 = (f32[112,128]{1,0:T(8,128)S(1)}, f32[112,128]{1,0:T(8,128)S(1)}, u32[]{:S(2)}, u32[]{:S(2)}) collective-permute-start(f32[112,128]{1,0:T(8,128)S(1)} %get-tuple-element.22.refs_0_), channel_id=1, source_target_pairs={{0,3},{1,2},{2,1},{3,0},{4,7},{5,6},{6,5},{7,4},{8,11},{9,10},{10,... | collective-permute-start | bytes 172040 | tf_op jit(solution)/shard_map/ppermute | solution.py:679
  12.6 1.7 %collective-permute-start.5 = (f32[112,128]{1,0:T(8,128)S(1)}, f32[112,128]{1,0:T(8,128)S(1)}, u32[]{:S(2)}, u32[]{:S(2)}) collective-permute-start(f32[112,128]{1,0:T(8,128)S(1)} %get-tuple-element.22.refs_0_), channel_id=1, source_target_pairs={{0,2},{1,3},{2,0},{3,1},{4,6},{5,7},{6,4},{7,5},{8,10},{9,11},{10,... | collective-permute-start | bytes 172040 | tf_op jit(solution)/shard_map/ppermute | solution.py:679
  14.3 4.5 %collective-permute-start.4 = (f32[48,128]{1,0:T(8,128)S(1)}, f32[48,128]{1,0:T(8,128)S(1)}, u32[]{:S(2)}, u32[]{:S(2)}) collective-permute-start(f32[48,128]{1,0:T(8,128)S(1)} %get-tuple-element.20), channel_id=1, source_target_pairs={{4,0},{8,4},{12,8},{16,12},{20,16},{24,20},{28,24},{0,28},{5,1},{9... | collective-permute-start | bytes 73736 | tf_op jit(solution)/shard_map/ppermute | solution.py:662
  18.8 0.0 collective-permute-start.3
  19.5 0.9 %collective-permute-done.4.after_ref = f32[48,128]{1,0:T(8,128)S(1)} collective-permute-done((f32[48,128]{1,0:T(8,128)S(1)}, f32[48,128]{1,0:T(8,128)S(1)}, u32[]{:S(2)}, u32[]{:S(2)}) %collective-permute-start.4) | collective-permute-done | bytes 24608 | tf_op jit(solution)/shard_map/ppermute | solution.py:662
  20.4 5.0 %collective-permute-done.3.before_ref = f32[48,128]{1,0:T(8,128)S(1)} collective-permute-done((f32[48,128]{1,0:T(8,128)S(1)}, f32[48,128]{1,0:T(8,128)S(1)}, u32[]{:S(2)}, u32[]{:S(2)}) %collective-permute-start.3) | collective-permute-done | bytes 24608 | tf_op jit(solution)/shard_map/ppermute | solution.py:661
  25.4 0.9 %shard_map.61 = (f32[5,32,256]{2,1,0:T(8,128)S(1)}, f32[1,5,32,512]{3,2,1,0:T(8,128)}) custom-call(s32[1]{0:T(128)S(6)} %copy.6.live_ref, f32[32,128]{1,0:T(8,128)S(1)} %get-tuple-element.13.ids_ref, f32[5,32,256]{2,1,0:T(8,128)S(1)} %get-tuple-element.14.c_ref, f32[1,5,32,512]{3,2,1,0:T(8,128)S(1)} %get-tuple-element.19.held_ref, ...), custom_call_target="tpu_custom_call" | custom-call | flops 4000000 | bytes 400000 | tf_op jit(solution)/shard_map/pallas_call | solution.py:680
  26.3 0.0 collective-permute-done.7.refs_3_
  26.3 0.0 collective-permute-done.6.refs_2_
  26.3 0.0 collective-permute-done.5.refs_1_
  26.4 0.8 %shard_map.62 = f32[5,32,256]{2,1,0:T(8,128)} custom-call(s32[1]{0:T(128)S(6)} %copy.6.live_ref, f32[32,128]{1,0:T(8,128)S(1)} %get-tuple-element.13.ids_ref, f32[5,32,256]{2,1,0:T(8,128)S(1)} %get-tuple-element.21.c_ref, f32[112,128]{1,0:T(8,128)S(1)} %get-tuple-element.22.refs_0_, f32[112,128]{1,0:T(8,128)S(1)} %collective-permute-done.5.refs_1_, ...), custom_call_target="tpu_custom_call" | custom-call | flops 400000 | bytes 400000 | tf_op jit(solution)/shard_map/pallas_call | solution.py:689
Async XLA Ops:
  2.4 7.0 %collective-permute-start.1 = (f32[72,128]{1,0:T(8,128)S(1)}, f32[72,128]{1,0:T(8,128)S(1)}, u32[]{:S(2)}, u32[]{:S(2)}) collective-permute-start(f32[72,128]{1,0:T(8,128)S(1)} %get-tuple-element.17), channel_id=1, source_target_pairs={{0,3},{1,2},{2,1},{3,0},{4,7},{5,6},{6,5},{7,4},{8,11},{9,10},{10,... | collective-permute-start | bytes 110600 | tf_op jit(solution)/shard_map/ppermute | solution.py:657
  4.9 4.5 %collective-permute-start.2 = (f32[72,128]{1,0:T(8,128)S(1)}, f32[72,128]{1,0:T(8,128)S(1)}, u32[]{:S(2)}, u32[]{:S(2)}) collective-permute-start(f32[72,128]{1,0:T(8,128)S(1)} %get-tuple-element.18), channel_id=1, source_target_pairs={{0,1},{1,0},{2,3},{3,2},{4,5},{5,4},{6,7},{7,6},{8,9},{9,8},{10,11... | collective-permute-start | bytes 110600 | tf_op jit(solution)/shard_map/ppermute | solution.py:657
  5.6 3.8 %collective-permute-start = (f32[48,128]{1,0:T(8,128)S(1)}, f32[48,128]{1,0:T(8,128)S(1)}, u32[]{:S(2)}, u32[]{:S(2)}) collective-permute-start(f32[48,128]{1,0:T(8,128)S(1)} %get-tuple-element.16.refs_0_), channel_id=1, source_target_pairs={{0,2},{1,3},{2,0},{3,1},{4,6},{5,7},{6,4},{7,5},{8,10},{9,11},{10,... | collective-permute-start | bytes 73736 | tf_op jit(solution)/shard_map/ppermute | solution.py:657
  12.1 14.2 %collective-permute-start.7 = (f32[112,128]{1,0:T(8,128)S(1)}, f32[112,128]{1,0:T(8,128)S(1)}, u32[]{:S(2)}, u32[]{:S(2)}) collective-permute-start(f32[112,128]{1,0:T(8,128)S(1)} %get-tuple-element.22.refs_0_), channel_id=1, source_target_pairs={{0,1},{1,0},{2,3},{3,2},{4,5},{5,4},{6,7},{7,6},{8,9},{9,8},{10,11... | collective-permute-start | bytes 172040 | tf_op jit(solution)/shard_map/ppermute | solution.py:679
  12.2 14.1 %collective-permute-start.6 = (f32[112,128]{1,0:T(8,128)S(1)}, f32[112,128]{1,0:T(8,128)S(1)}, u32[]{:S(2)}, u32[]{:S(2)}) collective-permute-start(f32[112,128]{1,0:T(8,128)S(1)} %get-tuple-element.22.refs_0_), channel_id=1, source_target_pairs={{0,3},{1,2},{2,1},{3,0},{4,7},{5,6},{6,5},{7,4},{8,11},{9,10},{10,... | collective-permute-start | bytes 172040 | tf_op jit(solution)/shard_map/ppermute | solution.py:679
  12.6 13.7 %collective-permute-start.5 = (f32[112,128]{1,0:T(8,128)S(1)}, f32[112,128]{1,0:T(8,128)S(1)}, u32[]{:S(2)}, u32[]{:S(2)}) collective-permute-start(f32[112,128]{1,0:T(8,128)S(1)} %get-tuple-element.22.refs_0_), channel_id=1, source_target_pairs={{0,2},{1,3},{2,0},{3,1},{4,6},{5,7},{6,4},{7,5},{8,10},{9,11},{10,... | collective-permute-start | bytes 172040 | tf_op jit(solution)/shard_map/ppermute | solution.py:679
  14.3 6.0 %collective-permute-start.4 = (f32[48,128]{1,0:T(8,128)S(1)}, f32[48,128]{1,0:T(8,128)S(1)}, u32[]{:S(2)}, u32[]{:S(2)}) collective-permute-start(f32[48,128]{1,0:T(8,128)S(1)} %get-tuple-element.20), channel_id=1, source_target_pairs={{4,0},{8,4},{12,8},{16,12},{20,16},{24,20},{28,24},{0,28},{5,1},{9... | collective-permute-start | bytes 73736 | tf_op jit(solution)/shard_map/ppermute | solution.py:662
  18.8 6.5 %collective-permute-start.3 = (f32[48,128]{1,0:T(8,128)S(1)}, f32[48,128]{1,0:T(8,128)S(1)}, u32[]{:S(2)}, u32[]{:S(2)}) collective-permute-start(f32[48,128]{1,0:T(8,128)S(1)} %get-tuple-element.20), channel_id=1, source_target_pairs={{0,4},{4,8},{8,12},{12,16},{16,20},{20,24},{24,28},{28,0},{1,5},{5... | collective-permute-start | bytes 73736 | tf_op jit(solution)/shard_map/ppermute | solution.py:661

commit v4 on v3

--- a/solution.py
+++ b/solution.py
@@ -2,6 +2,7 @@
 
 import jax
 import jax.numpy as jnp
+import numpy as np
 from jax import lax
 from jax.experimental import pallas as pl
 from jax.experimental.pallas import tpu as pltpu
@@ -56,9 +57,13 @@
 
 
 class Level:
-    def __init__(self, work, count, rows, depth, ghosts):
+    def __init__(self, work, count, rows, depth, ghosts, matrix=None):
         self.slopes, self.low, self.slope, self.left, self.right = work[:5]
-        self.zlow, self.zslope, self.zleft, self.zright = work[5:]
+        self.matrix = matrix
+        if matrix is None:
+            self.zlow, self.zslope, self.zleft, self.zright = work[5:]
+        else:
+            self.parts, self.steps, self.rises = work[5:]
         self.count, self.rows, self.depth, self.ghosts = count, rows, depth, ghosts
         lane = lanes_of()
         self.first = lane < depth
@@ -68,11 +73,27 @@
         self.ahead = jnp.where(place == depth - 1, lane - depth + 1, lane + 1)
 
     @staticmethod
-    def work(count, rows):
+    def work(count, rows, matrix=False):
         f32 = jnp.float32
         wide = VMEM((NVAR, count + 2, rows, LANES), f32)
         narrow = VMEM((NVAR, count, rows, LANES), f32)
-        return [VMEM((NVAR, count, rows + SUB, LANES), f32)] + [wide] * 4 + [narrow] * 4
+        cells = NVAR * count * rows
+        along_z = [narrow] * 4
+        if matrix:
+            along_z = [VMEM((cells, 2 * LANES), jnp.bfloat16)] + [VMEM((cells, 2 * LANES), f32)] * 2
+        return [VMEM((NVAR, count, rows + SUB, LANES), f32)] + [wide] * 4 + along_z
+
+    def place(self, v, t, row):
+        return (v * self.count + t) * self.rows + row
+
+    def split(self, at, values):
+        high = values.astype(jnp.bfloat16)
+        rest = (values - high.astype(jnp.float32)).astype(jnp.bfloat16)
+        self.parts[at : at + 2 * SUB, 0:LANES] = high
+        self.parts[at : at + 2 * SUB, LANES : 2 * LANES] = rest
+
+    def differences(self):
+        return jnp.dot(self.parts[...], self.matrix[...], preferred_element_type=jnp.float32)
 
     def columns(self):
         for v in range(NVAR):
@@ -100,9 +121,16 @@
                 self.low[v, count + 1, here] = cells[count + 1] - jnp.where(self.first, moved[count], top)
             if flat:
                 self.low[v, count + 1, here] = cells[count + 1] - moved[count]
-        for v, t, here, padded in self.tiles():
-            cell = q[v, t + 1, padded]
-            self.zlow[v, t, here] = cell - take(cell, self.behind)
+        if self.matrix is None:
+            for v, t, here, padded in self.tiles():
+                cell = q[v, t + 1, padded]
+                self.zlow[v, t, here] = cell - take(cell, self.behind)
+        else:
+            for v in range(NVAR):
+                for t in range(count):
+                    for row in range(0, self.rows, 2 * SUB):
+                        self.split(self.place(v, t, row), q[v, t + 1, PAD + row : PAD + row + 2 * SUB])
+            self.steps[...] = self.differences()
         for v in range(NVAR):
             for t in range(count):
                 for b in range((self.rows + 2 + SUB - 1) // SUB):
@@ -127,15 +155,21 @@
                 high = jnp.where(self.last, moved[1], roll(low[0], -depth))
                 self.slope[v, 0, here] = 0.5 * minmod(low[0], high)
                 self.slope[v, count + 1, here] = 0.5 * minmod(low[count + 1], moved[count + 1])
-        for v, t, here, padded in self.tiles():
-            low = self.zlow[v, t, here]
-            self.zslope[v, t, here] = 0.5 * minmod(low, take(low, self.ahead))
+        if self.matrix is None:
+            for v, t, here, padded in self.tiles():
+                low = self.zlow[v, t, here]
+                self.zslope[v, t, here] = 0.5 * minmod(low, take(low, self.ahead))
+        else:
+            for at in range(0, NVAR * count * self.rows, 2 * SUB):
+                both = slice(at, at + 2 * SUB)
+                self.split(at, 0.5 * minmod(self.steps[both, 0:LANES], self.steps[both, LANES : 2 * LANES]))
+            self.rises[...] = self.differences()
 
     def finish(self, q, store):
         count, depth = self.count, self.depth
         full, flat = self.ghosts == "full", self.ghosts == "flat"
         inner = range(1, count + 1)
-        for v, t, here, padded in self.tiles():
+        for v, t, here, padded in self.tiles() if self.matrix is None else ():
             slope = self.zslope[v, t, here]
             rise = slope - take(slope, self.behind)
             low = self.zlow[v, t, here]
@@ -158,7 +192,7 @@
                 self.right[v, count + 1, here] = self.low[v, count + 1, here] - rise
             if flat:
                 self.right[v, count + 1, here] = self.low[v, count + 1, here] + moved[count]
-        for v, t, here, padded in self.tiles():
+        for v, t, here, padded in self.tiles() if self.matrix is None else ():
             self.zright[v, t, here] = take(self.zright[v, t, here], self.ahead)
         for v, here, padded in self.columns():
             moved = {t: roll(self.right[v, t, here], -depth) for t in inner}
@@ -192,8 +226,13 @@
                     right = high - (self.slopes[v, t, SUB * s + 2 : SUB * s + 2 + SUB] - slope)
                 elif direction == 1:
                     left, right = self.left[v, t + 1, here], self.right[v, t + 1, here]
+                elif self.matrix is None:
+                    left, right = self.zleft[v, t, here], self.zright[v, t, here]
                 else:
-                    left, right = self.zleft[v, t, here], self.zright[v, t, here]
+                    at = self.place(v, t, SUB * s)
+                    at = slice(at, at + SUB)
+                    left = self.steps[at, 0:LANES] + self.rises[at, 0:LANES]
+                    right = self.steps[at, LANES : 2 * LANES] - self.rises[at, LANES : 2 * LANES]
                 add(v, (courant * PLUS[direction]) * left + (courant * MINUS[direction]) * right)
                 targets = [w for w in couples if couples[w] == v]
                 if targets:
@@ -202,6 +241,15 @@
                         add(w, shared)
         for v in range(NVAR):
             store(v, t, s, cell[v] - acc[v])
+
+
+def z_matrix(depth):
+    lane = np.arange(LANES)
+    base = lane - lane % depth
+    below, above = base + (lane - 1) % depth, base + (lane + 1) % depth
+    one = np.eye(LANES, dtype=np.float32)
+    half = np.concatenate([one - one[:, below], one[:, above] - one], axis=1)
+    return jnp.asarray(np.concatenate([half, half]), jnp.bfloat16)
 
 
 class Plan:
@@ -347,7 +395,7 @@
         ids_ref[SUB * index : SUB * (index + 1)] = zero + number.astype(jnp.float32)
 
 
-def fine_kernel(plan, others, ids_ref, f_ref, *refs):
+def fine_kernel(plan, others, ids_ref, matrix_ref, f_ref, *refs):
     rings = refs[: others + 1]
     out_ref, pay_ref, q, q_later, lines, faces, sides = refs[others + 1 : others + 8]
     work = refs[others + 8 :]
@@ -391,7 +439,7 @@
     for v in range(NVAR):
         for t in range(count):
             q[v, t + 1, PAD : PAD + rows] = f_ref[0, v, :, LANES * t : LANES * (t + 1)]
-    level = Level(work, count, rows, depth, "flat")
+    level = Level(work, count, rows, depth, "flat", matrix_ref)
     slopes = level.slopes
     second = (lane >= depth) & (lane < 2 * depth)
     ghosts(q, 0)
@@ -671,11 +719,11 @@
             VMEM((plan.fine_count, 2 * SUB, LANES), f32),
             VMEM((NVAR, plan.fine_rows, LANES), f32),
         ]
-        + Level.work(plan.fine_count, plan.fine_rows),
+        + Level.work(plan.fine_count, plan.fine_rows, True),
         16_000_000,
         1_000_000,
-        [VMEM, VMEM] + [VMEM] * size,
-    )(ids, held, mid, *[rings[k] for k in plan.exchanges])
+        [VMEM, VMEM, VMEM] + [VMEM] * size,
+    )(ids, z_matrix(plan.fine_depth), held, mid, *[rings[k] for k in plan.exchanges])
     payloads = [payload] + [lax.ppermute(payload, "gy", pairs[k]) for k in plan.exchanges]
     coarse_new, fine_out = call(
         partial(outer_kernel, plan),

time: 27.3 us -> 26.7 us (0.978)
  Pallas kernels: 6.17 us -> 5.52 us
    pallas_call x1, Pallas kernels: 2.69 us -> 2.01 us  [step(): call(partial(fine_kernel, plan, size - 1), (held_shape, shape((plan.paylo...]
  transfers between devices with their start and end apart: 8 -> 8, of which waited for: 3 -> 3; matrix products, arithmetic and copies ran while one was open for 0% -> 0% of each run, Pallas kernels for 3% -> 4%
where the time goes in v4:
time: 26.7 us; the launch traced here: 26.5 us
  starting transfers between devices  9.95 us (37%)
  waiting for transfers between devices  9.67 us (36%)
  Pallas kernels  5.52 us (21%)
  between operations  1.36 us (5%)
    ppermute x1, waiting for transfers between devices, step(): before = lax.ppermute(edges, 'gx', rise)  5 us
    ppermute x1, starting transfers between devices, step(): after = lax.ppermute(edges, 'gx', fall)  4.53 us
    ppermute x3, waiting for transfers between devices, step(): lax.ppermute(buffers.get(k, mid), 'gy', pairs[k])  3.79 us
    ppermute x3, starting transfers between devices, step(): lax.ppermute(buffers.get(k, mid), 'gy', pairs[k])  3.22 us
    ppermute x3, starting transfers between devices, step(): lax.ppermute(payload, 'gy', pairs[k])  2.2 us
    pallas_call x1, Pallas kernels, step(): call(partial(fine_kernel, plan, size - 1), (held_shape, shape((plan.paylo...  2.01 us
    pallas_call x1, Pallas kernels, step(): call(partial(coarse_kernel, plan), (shape((plan.ring_rows, LANES), f32),...  1.8 us
    pallas_call x1, Pallas kernels, step(): call(partial(outer_kernel, plan), (coarse_shape, held_shape), [cells, cop...  0.95 us
  transfers between devices with their start and end apart: 8, of which 3 were waited for; matrix products, arithmetic and copies ran while one was open for 0% of the time, Pallas kernels for 4%

profile of v4, /device:TPU:0, one launch (start us, length us, event | category | flops | bytes accessed | tf_op | source)
XLA Modules:
  0.0 26.5 jit_solution(14338875291442525749)
XLA Ops:
  0.6 0.0 copy-start
  0.6 1.8 %shard_map.68 = (f32[48,128]{1,0:T(8,128)S(1)}, f32[48,128]{1,0:T(8,128)S(1)}, f32[32,128]{1,0:T(8,128)S(1)}, f32[1,5,32,512]{3,2,1,0:T(8,128)S(1)}, f32[5,32,25...) custom-call(s32[1,2]{1,0:T(1,128)} %site_hbm.1, f32[5,32,256]{2,1,0:T(8,128)} %c_hbm.1, ...), custom_call_target="tpu_custom_call" | custom-call | flops 4000000 | bytes 400000 | tf_op jit(solution)/shard_map/pallas_call | solution.py:693
  2.4 2.5 %collective-permute-start.1 = (f32[72,128]{1,0:T(8,128)S(1)}, f32[72,128]{1,0:T(8,128)S(1)}, u32[]{:S(2)}, u32[]{:S(2)}) collective-permute-start(f32[72,128]{1,0:T(8,128)S(1)} %get-tuple-element.17), channel_id=1, source_target_pairs={{0,3},{1,2},{2,1},{3,0},{4,7},{5,6},{6,5},{7,4},{8,11},{9,10},{10,... | collective-permute-start | bytes 110600 | tf_op jit(solution)/shard_map/ppermute | solution.py:705
  4.9 0.7 %collective-permute-start.2 = (f32[72,128]{1,0:T(8,128)S(1)}, f32[72,128]{1,0:T(8,128)S(1)}, u32[]{:S(2)}, u32[]{:S(2)}) collective-permute-start(f32[72,128]{1,0:T(8,128)S(1)} %get-tuple-element.18), channel_id=1, source_target_pairs={{0,1},{1,0},{2,3},{3,2},{4,5},{5,4},{6,7},{7,6},{8,9},{9,8},{10,11... | collective-permute-start | bytes 110600 | tf_op jit(solution)/shard_map/ppermute | solution.py:705
  5.6 0.0 collective-permute-start
  5.7 3.8 %collective-permute-done.refs_1_ = f32[48,128]{1,0:T(8,128)S(1)} collective-permute-done((f32[48,128]{1,0:T(8,128)S(1)}, f32[48,128]{1,0:T(8,128)S(1)}, u32[]{:S(2)}, u32[]{:S(2)}) %collective-permute-start) | collective-permute-done | bytes 24608 | tf_op jit(solution)/shard_map/ppermute | solution.py:705
  9.5 0.0 collective-permute-done.1.refs_2_.refs_0_
  9.5 0.0 collective-permute-done.2.refs_3_.refs_1_
  9.5 0.0 copy-done
  9.5 2.0 %shard_map.69 = (f32[1,5,32,512]{3,2,1,0:T(8,128)S(1)}, f32[112,128]{1,0:T(8,128)S(1)}) custom-call(f32[32,128]{1,0:T(8,128)S(1)} %get-tuple-element.13.ids_ref, bf16[256,256]{1,0:T(8,128)(2,1)S(1)} %copy-done, f32[1,5,32,512]{3,2,1,0:T(8,128)S(1)} %get-tuple-element.15.f_ref, f32[48,128]{1,0:T(8,128)S(1)} %get-tuple-element.16.refs_0_, ...), custom_call_target="tpu_custom_call" | custom-call | flops 16000000 | bytes 1000000 | tf_op jit(solution)/shard_map/pallas_call | solution.py:712
  11.5 0.1 collective-permute-start.7
  11.6 0.5 %collective-permute-start.6 = (f32[112,128]{1,0:T(8,128)S(1)}, f32[112,128]{1,0:T(8,128)S(1)}, u32[]{:S(2)}, u32[]{:S(2)}) collective-permute-start(f32[112,128]{1,0:T(8,128)S(1)} %get-tuple-element.22.refs_0_), channel_id=1, source_target_pairs={{0,3},{1,2},{2,1},{3,0},{4,7},{5,6},{6,5},{7,4},{8,11},{9,10},{10,... | collective-permute-start | bytes 172040 | tf_op jit(solution)/shard_map/ppermute | solution.py:727
  12.0 1.7 %collective-permute-start.5 = (f32[112,128]{1,0:T(8,128)S(1)}, f32[112,128]{1,0:T(8,128)S(1)}, u32[]{:S(2)}, u32[]{:S(2)}) collective-permute-start(f32[112,128]{1,0:T(8,128)S(1)} %get-tuple-element.22.refs_0_), channel_id=1, source_target_pairs={{0,2},{1,3},{2,0},{3,1},{4,6},{5,7},{6,4},{7,5},{8,10},{9,11},{10,... | collective-permute-start | bytes 172040 | tf_op jit(solution)/shard_map/ppermute | solution.py:727
  13.7 4.5 %collective-permute-start.4 = (f32[48,128]{1,0:T(8,128)S(1)}, f32[48,128]{1,0:T(8,128)S(1)}, u32[]{:S(2)}, u32[]{:S(2)}) collective-permute-start(f32[48,128]{1,0:T(8,128)S(1)} %get-tuple-element.20), channel_id=1, source_target_pairs={{4,0},{8,4},{12,8},{16,12},{20,16},{24,20},{28,24},{0,28},{5,1},{9... | collective-permute-start | bytes 73736 | tf_op jit(solution)/shard_map/ppermute | solution.py:710
  18.2 0.0 collective-permute-start.3
  18.9 0.9 %collective-permute-done.4.after_ref = f32[48,128]{1,0:T(8,128)S(1)} collective-permute-done((f32[48,128]{1,0:T(8,128)S(1)}, f32[48,128]{1,0:T(8,128)S(1)}, u32[]{:S(2)}, u32[]{:S(2)}) %collective-permute-start.4) | collective-permute-done | bytes 24608 | tf_op jit(solution)/shard_map/ppermute | solution.py:710
  19.7 5.0 %collective-permute-done.3.before_ref = f32[48,128]{1,0:T(8,128)S(1)} collective-permute-done((f32[48,128]{1,0:T(8,128)S(1)}, f32[48,128]{1,0:T(8,128)S(1)}, u32[]{:S(2)}, u32[]{:S(2)}) %collective-permute-start.3) | collective-permute-done | bytes 24608 | tf_op jit(solution)/shard_map/ppermute | solution.py:709
  24.7 0.9 %shard_map.70 = (f32[5,32,256]{2,1,0:T(8,128)S(1)}, f32[1,5,32,512]{3,2,1,0:T(8,128)}) custom-call(s32[1]{0:T(128)S(6)} %copy.7.live_ref, f32[32,128]{1,0:T(8,128)S(1)} %get-tuple-element.13.ids_ref, f32[5,32,256]{2,1,0:T(8,128)S(1)} %get-tuple-element.14.c_ref, f32[1,5,32,512]{3,2,1,0:T(8,128)S(1)} %get-tuple-element.19.held_ref, ...), custom_call_target="tpu_custom_call" | custom-call | flops 4000000 | bytes 400000 | tf_op jit(solution)/shard_map/pallas_call | solution.py:728
  25.7 0.0 collective-permute-done.7.refs_3_
  25.7 0.0 collective-permute-done.6.refs_2_
  25.7 0.0 collective-permute-done.5.refs_1_
  25.7 0.8 %shard_map.71 = f32[5,32,256]{2,1,0:T(8,128)} custom-call(s32[1]{0:T(128)S(6)} %copy.7.live_ref, f32[32,128]{1,0:T(8,128)S(1)} %get-tuple-element.13.ids_ref, f32[5,32,256]{2,1,0:T(8,128)S(1)} %get-tuple-element.21.c_ref, f32[112,128]{1,0:T(8,128)S(1)} %get-tuple-element.22.refs_0_, f32[112,128]{1,0:T(8,128)S(1)} %collective-permute-done.5.refs_1_, ...), custom_call_target="tpu_custom_call" | custom-call | flops 400000 | bytes 400000 | tf_op jit(solution)/shard_map/pallas_call | solution.py:737
Async XLA Ops:
  0.6 8.8 %copy-start = (bf16[256,256]{1,0:T(8,128)(2,1)S(1)}, bf16[256,256]{1,0:T(8,128)(2,1)}, u32[]{:S(2)}) copy-start(bf16[256,256]{1,0:T(8,128)(2,1)} %constant.2.clone.matrix_ref) | copy-start | bytes 393220
  2.4 7.0 %collective-permute-start.1 = (f32[72,128]{1,0:T(8,128)S(1)}, f32[72,128]{1,0:T(8,128)S(1)}, u32[]{:S(2)}, u32[]{:S(2)}) collective-permute-start(f32[72,128]{1,0:T(8,128)S(1)} %get-tuple-element.17), channel_id=1, source_target_pairs={{0,3},{1,2},{2,1},{3,0},{4,7},{5,6},{6,5},{7,4},{8,11},{9,10},{10,... | collective-permute-start | bytes 110600 | tf_op jit(solution)/shard_map/ppermute | solution.py:705
  4.9 4.5 %collective-permute-start.2 = (f32[72,128]{1,0:T(8,128)S(1)}, f32[72,128]{1,0:T(8,128)S(1)}, u32[]{:S(2)}, u32[]{:S(2)}) collective-permute-start(f32[72,128]{1,0:T(8,128)S(1)} %get-tuple-element.18), channel_id=1, source_target_pairs={{0,1},{1,0},{2,3},{3,2},{4,5},{5,4},{6,7},{7,6},{8,9},{9,8},{10,11... | collective-permute-start | bytes 110600 | tf_op jit(solution)/shard_map/ppermute | solution.py:705
  5.6 3.8 %collective-permute-start = (f32[48,128]{1,0:T(8,128)S(1)}, f32[48,128]{1,0:T(8,128)S(1)}, u32[]{:S(2)}, u32[]{:S(2)}) collective-permute-start(f32[48,128]{1,0:T(8,128)S(1)} %get-tuple-element.16.refs_0_), channel_id=1, source_target_pairs={{0,2},{1,3},{2,0},{3,1},{4,6},{5,7},{6,4},{7,5},{8,10},{9,11},{10,... | collective-permute-start | bytes 73736 | tf_op jit(solution)/shard_map/ppermute | solution.py:705
  11.5 14.2 %collective-permute-start.7 = (f32[112,128]{1,0:T(8,128)S(1)}, f32[112,128]{1,0:T(8,128)S(1)}, u32[]{:S(2)}, u32[]{:S(2)}) collective-permute-start(f32[112,128]{1,0:T(8,128)S(1)} %get-tuple-element.22.refs_0_), channel_id=1, source_target_pairs={{0,1},{1,0},{2,3},{3,2},{4,5},{5,4},{6,7},{7,6},{8,9},{9,8},{10,11... | collective-permute-start | bytes 172040 | tf_op jit(solution)/shard_map/ppermute | solution.py:727
  11.6 14.1 %collective-permute-start.6 = (f32[112,128]{1,0:T(8,128)S(1)}, f32[112,128]{1,0:T(8,128)S(1)}, u32[]{:S(2)}, u32[]{:S(2)}) collective-permute-start(f32[112,128]{1,0:T(8,128)S(1)} %get-tuple-element.22.refs_0_), channel_id=1, source_target_pairs={{0,3},{1,2},{2,1},{3,0},{4,7},{5,6},{6,5},{7,4},{8,11},{9,10},{10,... | collective-permute-start | bytes 172040 | tf_op jit(solution)/shard_map/ppermute | solution.py:727
  12.0 13.7 %collective-permute-start.5 = (f32[112,128]{1,0:T(8,128)S(1)}, f32[112,128]{1,0:T(8,128)S(1)}, u32[]{:S(2)}, u32[]{:S(2)}) collective-permute-start(f32[112,128]{1,0:T(8,128)S(1)} %get-tuple-element.22.refs_0_), channel_id=1, source_target_pairs={{0,2},{1,3},{2,0},{3,1},{4,6},{5,7},{6,4},{7,5},{8,10},{9,11},{10,... | collective-permute-start | bytes 172040 | tf_op jit(solution)/shard_map/ppermute | solution.py:727
  13.7 6.0 %collective-permute-start.4 = (f32[48,128]{1,0:T(8,128)S(1)}, f32[48,128]{1,0:T(8,128)S(1)}, u32[]{:S(2)}, u32[]{:S(2)}) collective-permute-start(f32[48,128]{1,0:T(8,128)S(1)} %get-tuple-element.20), channel_id=1, source_target_pairs={{4,0},{8,4},{12,8},{16,12},{20,16},{24,20},{28,24},{0,28},{5,1},{9... | collective-permute-start | bytes 73736 | tf_op jit(solution)/shard_map/ppermute | solution.py:710
  18.2 6.5 %collective-permute-start.3 = (f32[48,128]{1,0:T(8,128)S(1)}, f32[48,128]{1,0:T(8,128)S(1)}, u32[]{:S(2)}, u32[]{:S(2)}) collective-permute-start(f32[48,128]{1,0:T(8,128)S(1)} %get-tuple-element.20), channel_id=1, source_target_pairs={{0,4},{4,8},{8,12},{12,16},{16,20},{20,24},{24,28},{28,0},{1,5},{5... | collective-permute-start | bytes 73736 | tf_op jit(solution)/shard_map/ppermute | solution.py:709

commit v5 on v4

--- a/solution.py
+++ b/solution.py
@@ -18,6 +18,7 @@
 signal = (1.5, 1.3, 1.2)
 PLUS = tuple(0.5 * (a + s) for a, s in zip(drift, signal))
 MINUS = tuple(0.5 * (a - s) for a, s in zip(drift, signal))
+assert all(abs(m + 0.5) < 1e-12 for m in MINUS)
 
 NVAR = 5
 VMEM = pltpu.VMEM
@@ -58,12 +59,12 @@
 
 class Level:
     def __init__(self, work, count, rows, depth, ghosts, matrix=None):
-        self.slopes, self.low, self.slope, self.left, self.right = work[:5]
+        self.jumps, self.slopes, self.low, self.slope, self.left, self.right = work[:6]
         self.matrix = matrix
         if matrix is None:
-            self.zlow, self.zslope, self.zleft, self.zright = work[5:]
+            self.zlow, self.zslope, self.zleft, self.zright = work[6:]
         else:
-            self.parts, self.steps, self.rises = work[5:]
+            self.parts, self.steps, self.rises = work[6:]
         self.count, self.rows, self.depth, self.ghosts = count, rows, depth, ghosts
         lane = lanes_of()
         self.first = lane < depth
@@ -81,7 +82,8 @@
         along_z = [narrow] * 4
         if matrix:
             along_z = [VMEM((cells, 2 * LANES), jnp.bfloat16)] + [VMEM((cells, 2 * LANES), f32)] * 2
-        return [VMEM((NVAR, count, rows + SUB, LANES), f32)] + [wide] * 4 + along_z
+        jumps = VMEM((NVAR, count, rows + 2 * SUB, LANES), f32)
+        return [jumps, VMEM((NVAR, count, rows + SUB, LANES), f32)] + [wide] * 4 + along_z
 
     def place(self, v, t, row):
         return (v * self.count + t) * self.rows + row
@@ -92,8 +94,8 @@
         self.parts[at : at + 2 * SUB, 0:LANES] = high
         self.parts[at : at + 2 * SUB, LANES : 2 * LANES] = rest
 
-    def differences(self):
-        return jnp.dot(self.parts[...], self.matrix[...], preferred_element_type=jnp.float32)
+    def differences(self, index):
+        return jnp.dot(self.parts[...], self.matrix[index], preferred_element_type=jnp.float32)
 
     def columns(self):
         for v in range(NVAR):
@@ -130,15 +132,19 @@
                 for t in range(count):
                     for row in range(0, self.rows, 2 * SUB):
                         self.split(self.place(v, t, row), q[v, t + 1, PAD + row : PAD + row + 2 * SUB])
-            self.steps[...] = self.differences()
+            self.steps[...] = self.differences(0)
         for v in range(NVAR):
             for t in range(count):
-                for b in range((self.rows + 2 + SUB - 1) // SUB):
-                    row = PAD - 1 + SUB * b
-                    cell = q[v, t + 1, row : row + SUB]
-                    low = cell - q[v, t + 1, row - 1 : row - 1 + SUB]
-                    high = q[v, t + 1, row + 1 : row + 1 + SUB] - cell
-                    self.slopes[v, t, SUB * b : SUB * (b + 1)] = 0.5 * minmod(low, high)
+                for at in range(0, self.rows + 3, SUB):
+                    row = PAD - 2 + at
+                    self.jumps[v, t, at : at + SUB] = (
+                        q[v, t + 1, row + 1 : row + 1 + SUB] - q[v, t + 1, row : row + SUB]
+                    )
+        for v in range(NVAR):
+            for t in range(count):
+                for at in range(0, self.rows + 2, SUB):
+                    low, high = self.jumps[v, t, at : at + SUB], self.jumps[v, t, at + 1 : at + 1 + SUB]
+                    self.slopes[v, t, at : at + SUB] = 0.5 * minmod(low, high)
         for v, here, padded in self.columns():
             low = {t: self.low[v, t, here] for t in inner}
             moved = {t: roll(low[t], -depth) for t in inner}
@@ -162,8 +168,8 @@
         else:
             for at in range(0, NVAR * count * self.rows, 2 * SUB):
                 both = slice(at, at + 2 * SUB)
-                self.split(at, 0.5 * minmod(self.steps[both, 0:LANES], self.steps[both, LANES : 2 * LANES]))
-            self.rises[...] = self.differences()
+                self.split(at, minmod(self.steps[both, 0:LANES], self.steps[both, LANES : 2 * LANES]))
+            self.rises[...] = self.differences(1)
 
     def finish(self, q, store):
         count, depth = self.count, self.depth
@@ -210,20 +216,20 @@
         here = slice(SUB * s, SUB * (s + 1))
         row = PAD + SUB * s
         cell = [q[v, t + 1, row : row + SUB] for v in range(NVAR)]
-        acc = [None] * NVAR
-
-        def add(v, term):
+        lefts, rights = [None] * NVAR, [None] * NVAR
+
+        def add(acc, v, term):
             acc[v] = term if acc[v] is None else acc[v] + term
 
         for direction in range(3):
             couples = coupled(direction)
             for v in range(NVAR):
                 if direction == 0:
-                    low = cell[v] - q[v, t + 1, row - 1 : row - 1 + SUB]
-                    high = q[v, t + 1, row + 1 : row + 1 + SUB] - cell[v]
                     slope = self.slopes[v, t, SUB * s + 1 : SUB * s + 1 + SUB]
-                    left = low + (slope - self.slopes[v, t, SUB * s : SUB * s + SUB])
-                    right = high - (self.slopes[v, t, SUB * s + 2 : SUB * s + 2 + SUB] - slope)
+                    rise = slope - self.slopes[v, t, SUB * s : SUB * s + SUB]
+                    fall = self.slopes[v, t, SUB * s + 2 : SUB * s + 2 + SUB] - slope
+                    left = self.jumps[v, t, SUB * s + 1 : SUB * s + 1 + SUB] + rise
+                    right = self.jumps[v, t, SUB * s + 2 : SUB * s + 2 + SUB] - fall
                 elif direction == 1:
                     left, right = self.left[v, t + 1, here], self.right[v, t + 1, here]
                 elif self.matrix is None:
@@ -233,14 +239,15 @@
                     at = slice(at, at + SUB)
                     left = self.steps[at, 0:LANES] + self.rises[at, 0:LANES]
                     right = self.steps[at, LANES : 2 * LANES] - self.rises[at, LANES : 2 * LANES]
-                add(v, (courant * PLUS[direction]) * left + (courant * MINUS[direction]) * right)
+                add(lefts, v, 2.0 * PLUS[direction] * left)
+                add(rights, v, right)
                 targets = [w for w in couples if couples[w] == v]
                 if targets:
-                    shared = (0.5 * courant) * (left + right)
+                    shared = left + right
                     for w in targets:
-                        add(w, shared)
+                        add(lefts, w, shared)
         for v in range(NVAR):
-            store(v, t, s, cell[v] - acc[v])
+            store(v, t, s, cell[v] - (0.5 * courant) * (lefts[v] - rights[v]))
 
 
 def z_matrix(depth):
@@ -249,7 +256,8 @@
     below, above = base + (lane - 1) % depth, base + (lane + 1) % depth
     one = np.eye(LANES, dtype=np.float32)
     half = np.concatenate([one - one[:, below], one[:, above] - one], axis=1)
-    return jnp.asarray(np.concatenate([half, half]), jnp.bfloat16)
+    whole = np.concatenate([half, half])
+    return jnp.asarray(np.stack([whole, 0.5 * whole]), jnp.bfloat16)
 
 
 class Plan:
@@ -296,16 +304,16 @@
 
 
 def coarse_kernel(
-    plan, site_hbm, c_hbm, f_hbm, mid_ref, rows_ref, ids_ref, held_ref, c_ref, *refs
+    plan, site_hbm, c_hbm, f_hbm, matrix_hbm, mid_ref, rows_ref, ids_ref, held_ref, c_ref, *refs
 ):
     near_refs = refs[: len(plan.near)]
-    q, fresh, site_ref, sems = refs[len(plan.near) : len(plan.near) + 4]
-    work = refs[len(plan.near) + 4 :]
+    q, fresh, site_ref, matrix_ref, sems = refs[len(plan.near) : len(plan.near) + 5]
+    work = refs[len(plan.near) + 5 :]
     me = lax.axis_index("gy")
     loads = [
         pltpu.make_async_copy(source, target, sems.at[index])
         for index, (source, target) in enumerate(
-            ((c_hbm, c_ref), (f_hbm, held_ref), (site_hbm, site_ref))
+            ((c_hbm, c_ref), (matrix_hbm, matrix_ref), (f_hbm, held_ref), (site_hbm, site_ref))
         )
     ]
     for load in loads:
@@ -318,7 +326,8 @@
                 q[v, t + 1, edge : edge + PAD] = jnp.zeros((PAD, LANES), jnp.float32)
         for t in (0, plan.count + 1):
             q[v, t, PAD : PAD + plan.rows] = jnp.zeros((plan.rows, LANES), jnp.float32)
-    level = Level(work, plan.count, plan.rows, plan.depth, "none")
+    level = Level(work, plan.count, plan.rows, plan.depth, "none", matrix_ref)
+    loads[1].wait()
     level.prepare(q)
 
     def store(v, t, s, tile):
@@ -388,7 +397,7 @@
             for t in range(plan.count):
                 at = base + (v * plan.count + t) * 2
                 rows_ref[at : at + 2] = q[v, t + 1, PAD + x : PAD + x + 2]
-    for load in loads[1:]:
+    for load in loads[2:]:
         load.wait()
     zero = jnp.zeros((SUB, LANES), jnp.float32)
     for index, number in enumerate((site_ref[0, 0], me, (me + 1) % plan.size, (me + plan.size - 1) % plan.size)):
@@ -690,16 +699,18 @@
     held_shape = shape(fine_state.shape, f32)
     coarse_shape = shape(coarse_state.shape, f32)
     near = plan.near
+    matrix = z_matrix(plan.depth)
     mid, edges, ids, held, coarse, *edged = call(
         partial(coarse_kernel, plan),
         (shape((plan.ring_rows, LANES), f32), edge, shape((4 * SUB, LANES), f32), held_shape, coarse_shape)
         + (sent,) * len(near),
-        [cells, VMEM((NVAR, plan.count, plan.rows, LANES), f32), smem((1, 2), jnp.int32), copying((3,))]
-        + Level.work(plan.count, plan.rows),
+        [cells, VMEM((NVAR, plan.count, plan.rows, LANES), f32), smem((1, 2), jnp.int32)]
+        + [VMEM(matrix.shape, matrix.dtype), copying((4,))]
+        + Level.work(plan.count, plan.rows, True),
         4_000_000,
         400_000,
-        [pltpu.HBM] * 3,
-    )(*[pltpu.with_memory_space_constraint(x, pltpu.HBM) for x in (slot_site, coarse_state, fine_state)])
+        [pltpu.HBM] * 4,
+    )(*[pltpu.with_memory_space_constraint(x, pltpu.HBM) for x in (slot_site, coarse_state, fine_state, matrix)])
     buffers = dict(zip(near, edged))
     pairs = {k: [(i, plan.target(i, k)) for i in range(size)] for k in plan.exchanges}
     rings = {k: lax.ppermute(buffers.get(k, mid), "gy", pairs[k]) for k in plan.exchanges}

time: 26.7 us -> 26.4 us (0.989)
  transfers between devices with their start and end apart: 8 -> 8, of which waited for: 3 -> 3; matrix products, arithmetic and copies ran while one was open for 0% -> 0% of each run, Pallas kernels for 4% -> 3%
where the time goes in v5:
time: 26.4 us; the launch traced here: 26.3 us
  starting transfers between devices  9.95 us (38%)
  waiting for transfers between devices  9.67 us (37%)
  Pallas kernels  5.31 us (20%)
  between operations  1.35 us (5%)
    ppermute x1, waiting for transfers between devices, step(): before = lax.ppermute(edges, 'gx', rise)  5 us
    ppermute x1, starting transfers between devices, step(): after = lax.ppermute(edges, 'gx', fall)  4.53 us
    ppermute x3, waiting for transfers between devices, step(): lax.ppermute(buffers.get(k, mid), 'gy', pairs[k])  3.79 us
    ppermute x3, starting transfers between devices, step(): lax.ppermute(buffers.get(k, mid), 'gy', pairs[k])  3.22 us
    ppermute x3, starting transfers between devices, step(): lax.ppermute(payload, 'gy', pairs[k])  2.2 us
    pallas_call x1, Pallas kernels, step(): call(partial(fine_kernel, plan, size - 1), (held_shape, shape((plan.paylo...  1.94 us
    pallas_call x1, Pallas kernels, step(): call(partial(coarse_kernel, plan), (shape((plan.ring_rows, LANES), f32),...  1.68 us
    pallas_call x1, Pallas kernels, step(): call(partial(outer_kernel, plan), (coarse_shape, held_shape), [cells, cop...  0.91 us
  transfers between devices with their start and end apart: 8, of which 3 were waited for; matrix products, arithmetic and copies ran while one was open for 0% of the time, Pallas kernels for 3%

profile of v5, /device:TPU:0, one launch (start us, length us, event | category | flops | bytes accessed | tf_op | source)
XLA Modules:
  0.0 26.3 jit_solution(13211800196953806527)
XLA Ops:
  0.6 0.0 copy-start
  0.6 1.7 %shard_map.77 = (f32[48,128]{1,0:T(8,128)S(1)}, f32[48,128]{1,0:T(8,128)S(1)}, f32[32,128]{1,0:T(8,128)S(1)}, f32[1,5,32,512]{3,2,1,0:T(8,128)S(1)}, f32[5,32,25...) custom-call(s32[1,2]{1,0:T(1,128)} %site_hbm.1, f32[5,32,256]{2,1,0:T(8,128)} %c_hbm.1, ...), custom_call_target="tpu_custom_call" | custom-call | flops 4000000 | bytes 400000 | tf_op jit(solution)/shard_map/pallas_call | solution.py:703
  2.3 2.5 %collective-permute-start.1 = (f32[72,128]{1,0:T(8,128)S(1)}, f32[72,128]{1,0:T(8,128)S(1)}, u32[]{:S(2)}, u32[]{:S(2)}) collective-permute-start(f32[72,128]{1,0:T(8,128)S(1)} %get-tuple-element.17), channel_id=1, source_target_pairs={{0,3},{1,2},{2,1},{3,0},{4,7},{5,6},{6,5},{7,4},{8,11},{9,10},{10,... | collective-permute-start | bytes 110600 | tf_op jit(solution)/shard_map/ppermute | solution.py:716
  4.8 0.7 %collective-permute-start.2 = (f32[72,128]{1,0:T(8,128)S(1)}, f32[72,128]{1,0:T(8,128)S(1)}, u32[]{:S(2)}, u32[]{:S(2)}) collective-permute-start(f32[72,128]{1,0:T(8,128)S(1)} %get-tuple-element.18), channel_id=1, source_target_pairs={{0,1},{1,0},{2,3},{3,2},{4,5},{5,4},{6,7},{7,6},{8,9},{9,8},{10,11... | collective-permute-start | bytes 110600 | tf_op jit(solution)/shard_map/ppermute | solution.py:716
  5.5 0.0 collective-permute-start
  5.5 3.8 %collective-permute-done.refs_1_ = f32[48,128]{1,0:T(8,128)S(1)} collective-permute-done((f32[48,128]{1,0:T(8,128)S(1)}, f32[48,128]{1,0:T(8,128)S(1)}, u32[]{:S(2)}, u32[]{:S(2)}) %collective-permute-start) | collective-permute-done | bytes 24608 | tf_op jit(solution)/shard_map/ppermute | solution.py:716
  9.3 0.0 collective-permute-done.1.refs_2_.refs_0_
  9.3 0.0 collective-permute-done.2.refs_3_.refs_1_
  9.3 0.0 copy-done
  9.3 1.9 %shard_map.78 = (f32[1,5,32,512]{3,2,1,0:T(8,128)S(1)}, f32[112,128]{1,0:T(8,128)S(1)}) custom-call(f32[32,128]{1,0:T(8,128)S(1)} %get-tuple-element.13.ids_ref, bf16[2,256,256]{2,1,0:T(8,128)(2,1)S(1)} %copy-done, f32[1,5,32,512]{3,2,1,0:T(8,128)S(1)} %get-tuple-element.15.f_ref, f32[48,128]{1,0:T(8,128)S(1)} %get-tuple-element.16.refs_0_, ...), custom_call_target="tpu_custom_call" | custom-call | flops 16000000 | bytes 1000000 | tf_op jit(solution)/shard_map/pallas_call | solution.py:723
  11.3 0.1 collective-permute-start.7
  11.4 0.5 %collective-permute-start.6 = (f32[112,128]{1,0:T(8,128)S(1)}, f32[112,128]{1,0:T(8,128)S(1)}, u32[]{:S(2)}, u32[]{:S(2)}) collective-permute-start(f32[112,128]{1,0:T(8,128)S(1)} %get-tuple-element.22.refs_0_), channel_id=1, source_target_pairs={{0,3},{1,2},{2,1},{3,0},{4,7},{5,6},{6,5},{7,4},{8,11},{9,10},{10,... | collective-permute-start | bytes 172040 | tf_op jit(solution)/shard_map/ppermute | solution.py:738
  11.8 1.7 %collective-permute-start.5 = (f32[112,128]{1,0:T(8,128)S(1)}, f32[112,128]{1,0:T(8,128)S(1)}, u32[]{:S(2)}, u32[]{:S(2)}) collective-permute-start(f32[112,128]{1,0:T(8,128)S(1)} %get-tuple-element.22.refs_0_), channel_id=1, source_target_pairs={{0,2},{1,3},{2,0},{3,1},{4,6},{5,7},{6,4},{7,5},{8,10},{9,11},{10,... | collective-permute-start | bytes 172040 | tf_op jit(solution)/shard_map/ppermute | solution.py:738
  13.5 4.5 %collective-permute-start.4 = (f32[48,128]{1,0:T(8,128)S(1)}, f32[48,128]{1,0:T(8,128)S(1)}, u32[]{:S(2)}, u32[]{:S(2)}) collective-permute-start(f32[48,128]{1,0:T(8,128)S(1)} %get-tuple-element.20), channel_id=1, source_target_pairs={{4,0},{8,4},{12,8},{16,12},{20,16},{24,20},{28,24},{0,28},{5,1},{9... | collective-permute-start | bytes 73736 | tf_op jit(solution)/shard_map/ppermute | solution.py:721
  18.0 0.0 collective-permute-start.3
  18.7 0.9 %collective-permute-done.4.after_ref = f32[48,128]{1,0:T(8,128)S(1)} collective-permute-done((f32[48,128]{1,0:T(8,128)S(1)}, f32[48,128]{1,0:T(8,128)S(1)}, u32[]{:S(2)}, u32[]{:S(2)}) %collective-permute-start.4) | collective-permute-done | bytes 24608 | tf_op jit(solution)/shard_map/ppermute | solution.py:721
  19.5 5.0 %collective-permute-done.3.before_ref = f32[48,128]{1,0:T(8,128)S(1)} collective-permute-done((f32[48,128]{1,0:T(8,128)S(1)}, f32[48,128]{1,0:T(8,128)S(1)}, u32[]{:S(2)}, u32[]{:S(2)}) %collective-permute-start.3) | collective-permute-done | bytes 24608 | tf_op jit(solution)/shard_map/ppermute | solution.py:720
  24.5 0.9 %shard_map.79 = (f32[5,32,256]{2,1,0:T(8,128)S(1)}, f32[1,5,32,512]{3,2,1,0:T(8,128)}) custom-call(s32[1]{0:T(128)S(6)} %copy.8.live_ref, f32[32,128]{1,0:T(8,128)S(1)} %get-tuple-element.13.ids_ref, f32[5,32,256]{2,1,0:T(8,128)S(1)} %get-tuple-element.14.c_ref, f32[1,5,32,512]{3,2,1,0:T(8,128)S(1)} %get-tuple-element.19.held_ref, ...), custom_call_target="tpu_custom_call" | custom-call | flops 4000000 | bytes 400000 | tf_op jit(solution)/shard_map/pallas_call | solution.py:739
  25.5 0.0 collective-permute-done.7.refs_3_
  25.5 0.0 collective-permute-done.6.refs_2_
  25.5 0.0 collective-permute-done.5.refs_1_
  25.5 0.8 %shard_map.80 = f32[5,32,256]{2,1,0:T(8,128)} custom-call(s32[1]{0:T(128)S(6)} %copy.8.live_ref, f32[32,128]{1,0:T(8,128)S(1)} %get-tuple-element.13.ids_ref, f32[5,32,256]{2,1,0:T(8,128)S(1)} %get-tuple-element.21.c_ref, f32[112,128]{1,0:T(8,128)S(1)} %get-tuple-element.22.refs_0_, f32[112,128]{1,0:T(8,128)S(1)} %collective-permute-done.5.refs_1_, ...), custom_call_target="tpu_custom_call" | custom-call | flops 400000 | bytes 400000 | tf_op jit(solution)/shard_map/pallas_call | solution.py:748
Async XLA Ops:
  0.6 8.7 %copy-start = (bf16[2,256,256]{2,1,0:T(8,128)(2,1)S(1)}, bf16[2,256,256]{2,1,0:T(8,128)(2,1)}, u32[]{:S(2)}) copy-start(bf16[2,256,256]{2,1,0:T(8,128)(2,1)} %constant.5.clone.matrix_ref) | copy-start | bytes 786436
  2.3 7.0 %collective-permute-start.1 = (f32[72,128]{1,0:T(8,128)S(1)}, f32[72,128]{1,0:T(8,128)S(1)}, u32[]{:S(2)}, u32[]{:S(2)}) collective-permute-start(f32[72,128]{1,0:T(8,128)S(1)} %get-tuple-element.17), channel_id=1, source_target_pairs={{0,3},{1,2},{2,1},{3,0},{4,7},{5,6},{6,5},{7,4},{8,11},{9,10},{10,... | collective-permute-start | bytes 110600 | tf_op jit(solution)/shard_map/ppermute | solution.py:716
  4.8 4.5 %collective-permute-start.2 = (f32[72,128]{1,0:T(8,128)S(1)}, f32[72,128]{1,0:T(8,128)S(1)}, u32[]{:S(2)}, u32[]{:S(2)}) collective-permute-start(f32[72,128]{1,0:T(8,128)S(1)} %get-tuple-element.18), channel_id=1, source_target_pairs={{0,1},{1,0},{2,3},{3,2},{4,5},{5,4},{6,7},{7,6},{8,9},{9,8},{10,11... | collective-permute-start | bytes 110600 | tf_op jit(solution)/shard_map/ppermute | solution.py:716
  5.5 3.8 %collective-permute-start = (f32[48,128]{1,0:T(8,128)S(1)}, f32[48,128]{1,0:T(8,128)S(1)}, u32[]{:S(2)}, u32[]{:S(2)}) collective-permute-start(f32[48,128]{1,0:T(8,128)S(1)} %get-tuple-element.16.refs_0_), channel_id=1, source_target_pairs={{0,2},{1,3},{2,0},{3,1},{4,6},{5,7},{6,4},{7,5},{8,10},{9,11},{10,... | collective-permute-start | bytes 73736 | tf_op jit(solution)/shard_map/ppermute | solution.py:716
  11.3 14.2 %collective-permute-start.7 = (f32[112,128]{1,0:T(8,128)S(1)}, f32[112,128]{1,0:T(8,128)S(1)}, u32[]{:S(2)}, u32[]{:S(2)}) collective-permute-start(f32[112,128]{1,0:T(8,128)S(1)} %get-tuple-element.22.refs_0_), channel_id=1, source_target_pairs={{0,1},{1,0},{2,3},{3,2},{4,5},{5,4},{6,7},{7,6},{8,9},{9,8},{10,11... | collective-permute-start | bytes 172040 | tf_op jit(solution)/shard_map/ppermute | solution.py:738
  11.4 14.1 %collective-permute-start.6 = (f32[112,128]{1,0:T(8,128)S(1)}, f32[112,128]{1,0:T(8,128)S(1)}, u32[]{:S(2)}, u32[]{:S(2)}) collective-permute-start(f32[112,128]{1,0:T(8,128)S(1)} %get-tuple-element.22.refs_0_), channel_id=1, source_target_pairs={{0,3},{1,2},{2,1},{3,0},{4,7},{5,6},{6,5},{7,4},{8,11},{9,10},{10,... | collective-permute-start | bytes 172040 | tf_op jit(solution)/shard_map/ppermute | solution.py:738
  11.8 13.7 %collective-permute-start.5 = (f32[112,128]{1,0:T(8,128)S(1)}, f32[112,128]{1,0:T(8,128)S(1)}, u32[]{:S(2)}, u32[]{:S(2)}) collective-permute-start(f32[112,128]{1,0:T(8,128)S(1)} %get-tuple-element.22.refs_0_), channel_id=1, source_target_pairs={{0,2},{1,3},{2,0},{3,1},{4,6},{5,7},{6,4},{7,5},{8,10},{9,11},{10,... | collective-permute-start | bytes 172040 | tf_op jit(solution)/shard_map/ppermute | solution.py:738
  13.5 6.0 %collective-permute-start.4 = (f32[48,128]{1,0:T(8,128)S(1)}, f32[48,128]{1,0:T(8,128)S(1)}, u32[]{:S(2)}, u32[]{:S(2)}) collective-permute-start(f32[48,128]{1,0:T(8,128)S(1)} %get-tuple-element.20), channel_id=1, source_target_pairs={{4,0},{8,4},{12,8},{16,12},{20,16},{24,20},{28,24},{0,28},{5,1},{9... | collective-permute-start | bytes 73736 | tf_op jit(solution)/shard_map/ppermute | solution.py:721
  18.0 6.5 %collective-permute-start.3 = (f32[48,128]{1,0:T(8,128)S(1)}, f32[48,128]{1,0:T(8,128)S(1)}, u32[]{:S(2)}, u32[]{:S(2)}) collective-permute-start(f32[48,128]{1,0:T(8,128)S(1)} %get-tuple-element.20), channel_id=1, source_target_pairs={{0,4},{4,8},{8,12},{12,16},{16,20},{20,24},{24,28},{28,0},{1,5},{5... | collective-permute-start | bytes 73736 | tf_op jit(solution)/shard_map/ppermute | solution.py:720

commit v6 on v5

--- a/solution.py
+++ b/solution.py
@@ -89,8 +89,7 @@
         return (v * self.count + t) * self.rows + row
 
     def split(self, at, values):
-        high = values.astype(jnp.bfloat16)
-        rest = (values - high.astype(jnp.float32)).astype(jnp.bfloat16)
+        high, rest = parts_of(values)
         self.parts[at : at + 2 * SUB, 0:LANES] = high
         self.parts[at : at + 2 * SUB, LANES : 2 * LANES] = rest
 
@@ -258,6 +257,20 @@
     half = np.concatenate([one - one[:, below], one[:, above] - one], axis=1)
     whole = np.concatenate([half, half])
     return jnp.asarray(np.stack([whole, 0.5 * whole]), jnp.bfloat16)
+
+
+def mean_matrix(depth, count):
+    lane = np.arange(LANES)
+    place = (lane // depth // 2) * (depth // 2) + lane % depth // 2
+    out = np.zeros((count, 2, LANES, LANES), np.float32)
+    for t in range(count):
+        out[t, :, lane, LANES // 4 * t + place] = 0.125
+    return jnp.asarray(out.reshape(-1, LANES), jnp.bfloat16)
+
+
+def parts_of(values):
+    high = values.astype(jnp.bfloat16)
+    return high, (values - high.astype(jnp.float32)).astype(jnp.bfloat16)
 
 
 class Plan:
@@ -404,10 +417,10 @@
         ids_ref[SUB * index : SUB * (index + 1)] = zero + number.astype(jnp.float32)
 
 
-def fine_kernel(plan, others, ids_ref, matrix_ref, f_ref, *refs):
+def fine_kernel(plan, others, ids_ref, matrix_ref, mean_ref, f_ref, *refs):
     rings = refs[: others + 1]
-    out_ref, pay_ref, q, q_later, lines, faces, sides = refs[others + 1 : others + 8]
-    work = refs[others + 8 :]
+    out_ref, pay_ref, q, q_later, lines, faces, sides, sums = refs[others + 1 : others + 9]
+    work = refs[others + 9 :]
     owner = ids_ref[0:SUB]
     sources = [jnp.broadcast_to(ref[plan.source_at : plan.source_at + 1], (SUB, LANES)) == owner for ref in rings]
     count, depth, rows = plan.fine_count, plan.fine_depth, plan.fine_rows
@@ -453,6 +466,31 @@
     second = (lane >= depth) & (lane < 2 * depth)
     ghosts(q, 0)
     ghosts(q_later, 1)
+
+    def put_sums(rows_of, t, values):
+        for part, piece in enumerate(parts_of(values)):
+            at = (2 * t + part) * LANES
+            sums[rows_of, at : at + LANES] = piece
+
+    def pack_registers():
+        pair = ((lane // plan.depth) % 2) * depth + (lane % plan.depth) * 2
+        halves = plan.patch // SUB
+        beside = []
+        for v in range(NVAR):
+            for half in range(halves):
+                row = 2 * SUB * half
+                beside.append(sides[v, pl.ds(row, SUB, stride=2)] + sides[v, pl.ds(row + 1, SUB, stride=2)])
+        beside = [tile + roll(tile, -1) for tile in beside]
+        beside = [take(tile, pair) for tile in beside]
+        for half in range(halves):
+            out = beside[half]
+            for v in range(1, NVAR):
+                out = jnp.where(lane // depth == v, beside[v * halves + half], out)
+            at = plan.side_at + SUB * half
+            pay_ref[at : at + SUB] = 0.125 * out
+        for t in range(count):
+            put_sums(slice(plan.average_rows, plan.average_rows + 2 * SUB), t, faces[t])
+
     for step, (now, later) in enumerate(((q, q_later), (q_later, q))):
 
         def add(ref, index, value, step=step):
@@ -489,51 +527,19 @@
             if step == 1:
                 out_ref[0, v, SUB * s : SUB * (s + 1), LANES * t : LANES * (t + 1)] = tile
 
+        if step == 1:
+            pack_registers()
         level.finish(now, store)
 
-    within = ((lane % 32) // plan.depth) * (2 * depth) + (lane % plan.depth) * 2
-
-    groups = []
     for v in range(NVAR):
-        for half in range(plan.patch // SUB):
-            row = PAD + 2 * SUB * half
-            groups.append(
-                [
-                    q[v, t + 1, pl.ds(row, SUB, stride=2)] + q[v, t + 1, pl.ds(row + 1, SUB, stride=2)]
-                    for t in range(count)
-                ]
-            )
-    for part in range(2):
-        groups.append([faces[t, SUB * part : SUB * (part + 1)] for t in range(count)])
-    beside = []
-    for v in range(NVAR):
-        for half in range(plan.patch // SUB):
-            row = 2 * SUB * half
-            beside.append(sides[v, pl.ds(row, SUB, stride=2)] + sides[v, pl.ds(row + 1, SUB, stride=2)])
-    groups = [[tile + roll(tile, -1) for tile in tiles] for tiles in groups]
-    beside = [tile + roll(tile, -1) for tile in beside]
-    groups = [[tile + roll(tile, -depth) for tile in tiles] for tiles in groups]
-    pair = ((lane // plan.depth) % 2) * depth + (lane % plan.depth) * 2
-    beside = [take(tile, pair) for tile in beside]
-    groups = [[take(tile, within) for tile in tiles] for tiles in groups]
-    packed = []
-    for tiles in groups:
-        out = tiles[0]
-        for t in range(1, count):
-            out = jnp.where(lane // 32 == t, tiles[t], out)
-        packed.append(0.125 * out)
-    halves = plan.patch // SUB
-    for at in range(NVAR * halves):
-        pay_ref[SUB * at : SUB * (at + 1)] = packed[at]
-    for half in range(halves):
-        out = beside[half]
-        for v in range(1, NVAR):
-            out = jnp.where(lane // depth == v, beside[v * halves + half], out)
-        at = plan.side_at + SUB * half
-        pay_ref[at : at + SUB] = 0.125 * out
+        rows_of = slice(v * plan.patch, (v + 1) * plan.patch)
+        for t in range(count):
+            pairs = q[v, t + 1, pl.ds(PAD, plan.patch, stride=2)] + q[v, t + 1, pl.ds(PAD + 1, plan.patch, stride=2)]
+            put_sums(rows_of, t, pairs)
+    means = jnp.dot(sums[...], mean_ref[...], preferred_element_type=jnp.float32)
+    pay_ref[0 : plan.average_rows] = means[0 : plan.average_rows]
     pay_ref[plan.payload_rows - SUB : plan.payload_rows] = owner
-    pay_ref[plan.face_at : plan.face_at + SUB] = packed[-2]
-    pay_ref[plan.face_at + SUB : plan.face_at + SUB + 2] = packed[-1][0:2]
+    pay_ref[plan.face_at : plan.face_at + 2 * NVAR] = means[plan.average_rows : plan.average_rows + 2 * NVAR]
 
 
 def outer_kernel(plan, live_ref, ids_ref, c_ref, held_ref, before_ref, after_ref, *refs):
@@ -729,12 +735,13 @@
             VMEM((plan.fine_count, plan.line_rows, LANES), f32),
             VMEM((plan.fine_count, 2 * SUB, LANES), f32),
             VMEM((NVAR, plan.fine_rows, LANES), f32),
+            VMEM((plan.average_rows + 2 * SUB, 2 * plan.fine_count * LANES), jnp.bfloat16),
         ]
         + Level.work(plan.fine_count, plan.fine_rows, True),
         16_000_000,
         1_000_000,
-        [VMEM, VMEM, VMEM] + [VMEM] * size,
-    )(ids, z_matrix(plan.fine_depth), held, mid, *[rings[k] for k in plan.exchanges])
+        [VMEM, VMEM, VMEM, VMEM] + [VMEM] * size,
+    )(ids, z_matrix(plan.fine_depth), mean_matrix(plan.fine_depth, plan.fine_count), held, mid, *[rings[k] for k in plan.exchanges])
     payloads = [payload] + [lax.ppermute(payload, "gy", pairs[k]) for k in plan.exchanges]
     coarse_new, fine_out = call(
         partial(outer_kernel, plan),

time: 26.4 us -> 26.4 us (level)
  no operation moved by 1% of the time
where the time goes in v6:
time: 26.4 us; the launch traced here: 26.3 us
  starting transfers between devices  9.95 us (38%)
  waiting for transfers between devices  9.67 us (37%)
  Pallas kernels  5.28 us (20%)
  between operations  1.37 us (5%)
    ppermute x1, waiting for transfers between devices, step(): before = lax.ppermute(edges, 'gx', rise)  5 us
    ppermute x1, starting transfers between devices, step(): after = lax.ppermute(edges, 'gx', fall)  4.53 us
    ppermute x3, waiting for transfers between devices, step(): lax.ppermute(buffers.get(k, mid), 'gy', pairs[k])  3.79 us
    ppermute x3, starting transfers between devices, step(): lax.ppermute(buffers.get(k, mid), 'gy', pairs[k])  3.22 us
    ppermute x3, starting transfers between devices, step(): lax.ppermute(payload, 'gy', pairs[k])  2.2 us
    pallas_call x1, Pallas kernels, step(): call(partial(fine_kernel, plan, size - 1), (held_shape, shape((plan.paylo...  1.91 us
    pallas_call x1, Pallas kernels, step(): call(partial(coarse_kernel, plan), (shape((plan.ring_rows, LANES), f32),...  1.69 us
    pallas_call x1, Pallas kernels, step(): call(partial(outer_kernel, plan), (coarse_shape, held_shape), [cells, cop...  0.91 us
  transfers between devices with their start and end apart: 8, of which 3 were waited for; matrix products, arithmetic and copies ran while one was open for 0% of the time, Pallas kernels for 3%

profile of v6, /device:TPU:0, one launch (start us, length us, event | category | flops | bytes accessed | tf_op | source)
XLA Modules:
  0.0 26.3 jit_solution(4130449733323914924)
XLA Ops:
  0.6 0.0 copy-start
  0.6 0.0 copy-start.1
  0.7 1.7 %shard_map.86 = (f32[48,128]{1,0:T(8,128)S(1)}, f32[48,128]{1,0:T(8,128)S(1)}, f32[32,128]{1,0:T(8,128)S(1)}, f32[1,5,32,512]{3,2,1,0:T(8,128)S(1)}, f32[5,32,25...) custom-call(s32[1,2]{1,0:T(1,128)} %site_hbm.1, f32[5,32,256]{2,1,0:T(8,128)} %c_hbm.1, ...), custom_call_target="tpu_custom_call" | custom-call | flops 4000000 | bytes 400000 | tf_op jit(solution)/shard_map/pallas_call | solution.py:709
  2.4 2.5 %collective-permute-start.1 = (f32[72,128]{1,0:T(8,128)S(1)}, f32[72,128]{1,0:T(8,128)S(1)}, u32[]{:S(2)}, u32[]{:S(2)}) collective-permute-start(f32[72,128]{1,0:T(8,128)S(1)} %get-tuple-element.17), channel_id=1, source_target_pairs={{0,3},{1,2},{2,1},{3,0},{4,7},{5,6},{6,5},{7,4},{8,11},{9,10},{10,... | collective-permute-start | bytes 110600 | tf_op jit(solution)/shard_map/ppermute | solution.py:722
  4.9 0.7 %collective-permute-start.2 = (f32[72,128]{1,0:T(8,128)S(1)}, f32[72,128]{1,0:T(8,128)S(1)}, u32[]{:S(2)}, u32[]{:S(2)}) collective-permute-start(f32[72,128]{1,0:T(8,128)S(1)} %get-tuple-element.18), channel_id=1, source_target_pairs={{0,1},{1,0},{2,3},{3,2},{4,5},{5,4},{6,7},{7,6},{8,9},{9,8},{10,11... | collective-permute-start | bytes 110600 | tf_op jit(solution)/shard_map/ppermute | solution.py:722
  5.5 0.0 collective-permute-start
  5.6 3.8 %collective-permute-done.refs_1_ = f32[48,128]{1,0:T(8,128)S(1)} collective-permute-done((f32[48,128]{1,0:T(8,128)S(1)}, f32[48,128]{1,0:T(8,128)S(1)}, u32[]{:S(2)}, u32[]{:S(2)}) %collective-permute-start) | collective-permute-done | bytes 24608 | tf_op jit(solution)/shard_map/ppermute | solution.py:722
  9.4 0.0 collective-permute-done.1.refs_2_.refs_0_
  9.4 0.0 collective-permute-done.2.refs_3_.refs_1_
  9.4 0.0 copy-done
  9.4 0.0 copy-done.1
  9.4 1.9 %shard_map.87 = (f32[1,5,32,512]{3,2,1,0:T(8,128)S(1)}, f32[112,128]{1,0:T(8,128)S(1)}) custom-call(f32[32,128]{1,0:T(8,128)S(1)} %get-tuple-element.13.ids_ref, bf16[2,256,256]{2,1,0:T(8,128)(2,1)S(1)} %copy-done.1, bf16[1024,128]{1,0:T(8,128)(2,1)S(1)} %copy-done, f32[1,5,32,512]{3,2,1,0:T(8,128)S(1)} %get-tuple-element.15.f_ref, ...), custom_call_target="tpu_custom_call" | custom-call | flops 16000000 | bytes 1000000 | tf_op jit(solution)/shard_map/pallas_call | solution.py:729
  11.3 0.1 collective-permute-start.7
  11.4 0.5 %collective-permute-start.6 = (f32[112,128]{1,0:T(8,128)S(1)}, f32[112,128]{1,0:T(8,128)S(1)}, u32[]{:S(2)}, u32[]{:S(2)}) collective-permute-start(f32[112,128]{1,0:T(8,128)S(1)} %get-tuple-element.22.refs_0_), channel_id=1, source_target_pairs={{0,3},{1,2},{2,1},{3,0},{4,7},{5,6},{6,5},{7,4},{8,11},{9,10},{10,... | collective-permute-start | bytes 172040 | tf_op jit(solution)/shard_map/ppermute | solution.py:745
  11.8 1.7 %collective-permute-start.5 = (f32[112,128]{1,0:T(8,128)S(1)}, f32[112,128]{1,0:T(8,128)S(1)}, u32[]{:S(2)}, u32[]{:S(2)}) collective-permute-start(f32[112,128]{1,0:T(8,128)S(1)} %get-tuple-element.22.refs_0_), channel_id=1, source_target_pairs={{0,2},{1,3},{2,0},{3,1},{4,6},{5,7},{6,4},{7,5},{8,10},{9,11},{10,... | collective-permute-start | bytes 172040 | tf_op jit(solution)/shard_map/ppermute | solution.py:745
  13.5 4.5 %collective-permute-start.4 = (f32[48,128]{1,0:T(8,128)S(1)}, f32[48,128]{1,0:T(8,128)S(1)}, u32[]{:S(2)}, u32[]{:S(2)}) collective-permute-start(f32[48,128]{1,0:T(8,128)S(1)} %get-tuple-element.20), channel_id=1, source_target_pairs={{4,0},{8,4},{12,8},{16,12},{20,16},{24,20},{28,24},{0,28},{5,1},{9... | collective-permute-start | bytes 73736 | tf_op jit(solution)/shard_map/ppermute | solution.py:727
  18.0 0.0 collective-permute-start.3
  18.7 0.9 %collective-permute-done.4.after_ref = f32[48,128]{1,0:T(8,128)S(1)} collective-permute-done((f32[48,128]{1,0:T(8,128)S(1)}, f32[48,128]{1,0:T(8,128)S(1)}, u32[]{:S(2)}, u32[]{:S(2)}) %collective-permute-start.4) | collective-permute-done | bytes 24608 | tf_op jit(solution)/shard_map/ppermute | solution.py:727
  19.6 5.0 %collective-permute-done.3.before_ref = f32[48,128]{1,0:T(8,128)S(1)} collective-permute-done((f32[48,128]{1,0:T(8,128)S(1)}, f32[48,128]{1,0:T(8,128)S(1)}, u32[]{:S(2)}, u32[]{:S(2)}) %collective-permute-start.3) | collective-permute-done | bytes 24608 | tf_op jit(solution)/shard_map/ppermute | solution.py:726
  24.6 0.9 %shard_map.88 = (f32[5,32,256]{2,1,0:T(8,128)S(1)}, f32[1,5,32,512]{3,2,1,0:T(8,128)}) custom-call(s32[1]{0:T(128)S(6)} %copy.9.live_ref, f32[32,128]{1,0:T(8,128)S(1)} %get-tuple-element.13.ids_ref, f32[5,32,256]{2,1,0:T(8,128)S(1)} %get-tuple-element.14.c_ref, f32[1,5,32,512]{3,2,1,0:T(8,128)S(1)} %get-tuple-element.19.held_ref, ...), custom_call_target="tpu_custom_call" | custom-call | flops 4000000 | bytes 400000 | tf_op jit(solution)/shard_map/pallas_call | solution.py:746
  25.5 0.0 collective-permute-done.7.refs_3_
  25.5 0.0 collective-permute-done.6.refs_2_
  25.5 0.0 collective-permute-done.5.refs_1_
  25.5 0.8 %shard_map.89 = f32[5,32,256]{2,1,0:T(8,128)} custom-call(s32[1]{0:T(128)S(6)} %copy.9.live_ref, f32[32,128]{1,0:T(8,128)S(1)} %get-tuple-element.13.ids_ref, f32[5,32,256]{2,1,0:T(8,128)S(1)} %get-tuple-element.21.c_ref, f32[112,128]{1,0:T(8,128)S(1)} %get-tuple-element.22.refs_0_, f32[112,128]{1,0:T(8,128)S(1)} %collective-permute-done.5.refs_1_, ...), custom_call_target="tpu_custom_call" | custom-call | flops 400000 | bytes 400000 | tf_op jit(solution)/shard_map/pallas_call | solution.py:755
Async XLA Ops:
  0.6 8.7 %copy-start = (bf16[1024,128]{1,0:T(8,128)(2,1)S(1)}, bf16[1024,128]{1,0:T(8,128)(2,1)}, u32[]{:S(2)}) copy-start(bf16[1024,128]{1,0:T(8,128)(2,1)} %constant.8.clone.mean_ref) | copy-start | bytes 786436
  0.6 8.7 %copy-start.1 = (bf16[2,256,256]{2,1,0:T(8,128)(2,1)S(1)}, bf16[2,256,256]{2,1,0:T(8,128)(2,1)}, u32[]{:S(2)}) copy-start(bf16[2,256,256]{2,1,0:T(8,128)(2,1)} %constant.7.clone.matrix_ref) | copy-start | bytes 786436
  2.4 7.0 %collective-permute-start.1 = (f32[72,128]{1,0:T(8,128)S(1)}, f32[72,128]{1,0:T(8,128)S(1)}, u32[]{:S(2)}, u32[]{:S(2)}) collective-permute-start(f32[72,128]{1,0:T(8,128)S(1)} %get-tuple-element.17), channel_id=1, source_target_pairs={{0,3},{1,2},{2,1},{3,0},{4,7},{5,6},{6,5},{7,4},{8,11},{9,10},{10,... | collective-permute-start | bytes 110600 | tf_op jit(solution)/shard_map/ppermute | solution.py:722
  4.9 4.5 %collective-permute-start.2 = (f32[72,128]{1,0:T(8,128)S(1)}, f32[72,128]{1,0:T(8,128)S(1)}, u32[]{:S(2)}, u32[]{:S(2)}) collective-permute-start(f32[72,128]{1,0:T(8,128)S(1)} %get-tuple-element.18), channel_id=1, source_target_pairs={{0,1},{1,0},{2,3},{3,2},{4,5},{5,4},{6,7},{7,6},{8,9},{9,8},{10,11... | collective-permute-start | bytes 110600 | tf_op jit(solution)/shard_map/ppermute | solution.py:722
  5.5 3.8 %collective-permute-start = (f32[48,128]{1,0:T(8,128)S(1)}, f32[48,128]{1,0:T(8,128)S(1)}, u32[]{:S(2)}, u32[]{:S(2)}) collective-permute-start(f32[48,128]{1,0:T(8,128)S(1)} %get-tuple-element.16.refs_0_), channel_id=1, source_target_pairs={{0,2},{1,3},{2,0},{3,1},{4,6},{5,7},{6,4},{7,5},{8,10},{9,11},{10,... | collective-permute-start | bytes 73736 | tf_op jit(solution)/shard_map/ppermute | solution.py:722
  11.3 14.2 %collective-permute-start.7 = (f32[112,128]{1,0:T(8,128)S(1)}, f32[112,128]{1,0:T(8,128)S(1)}, u32[]{:S(2)}, u32[]{:S(2)}) collective-permute-start(f32[112,128]{1,0:T(8,128)S(1)} %get-tuple-element.22.refs_0_), channel_id=1, source_target_pairs={{0,1},{1,0},{2,3},{3,2},{4,5},{5,4},{6,7},{7,6},{8,9},{9,8},{10,11... | collective-permute-start | bytes 172040 | tf_op jit(solution)/shard_map/ppermute | solution.py:745
  11.4 14.1 %collective-permute-start.6 = (f32[112,128]{1,0:T(8,128)S(1)}, f32[112,128]{1,0:T(8,128)S(1)}, u32[]{:S(2)}, u32[]{:S(2)}) collective-permute-start(f32[112,128]{1,0:T(8,128)S(1)} %get-tuple-element.22.refs_0_), channel_id=1, source_target_pairs={{0,3},{1,2},{2,1},{3,0},{4,7},{5,6},{6,5},{7,4},{8,11},{9,10},{10,... | collective-permute-start | bytes 172040 | tf_op jit(solution)/shard_map/ppermute | solution.py:745
  11.8 13.7 %collective-permute-start.5 = (f32[112,128]{1,0:T(8,128)S(1)}, f32[112,128]{1,0:T(8,128)S(1)}, u32[]{:S(2)}, u32[]{:S(2)}) collective-permute-start(f32[112,128]{1,0:T(8,128)S(1)} %get-tuple-element.22.refs_0_), channel_id=1, source_target_pairs={{0,2},{1,3},{2,0},{3,1},{4,6},{5,7},{6,4},{7,5},{8,10},{9,11},{10,... | collective-permute-start | bytes 172040 | tf_op jit(solution)/shard_map/ppermute | solution.py:745
  13.5 6.0 %collective-permute-start.4 = (f32[48,128]{1,0:T(8,128)S(1)}, f32[48,128]{1,0:T(8,128)S(1)}, u32[]{:S(2)}, u32[]{:S(2)}) collective-permute-start(f32[48,128]{1,0:T(8,128)S(1)} %get-tuple-element.20), channel_id=1, source_target_pairs={{4,0},{8,4},{12,8},{16,12},{20,16},{24,20},{28,24},{0,28},{5,1},{9... | collective-permute-start | bytes 73736 | tf_op jit(solution)/shard_map/ppermute | solution.py:727
  18.0 6.5 %collective-permute-start.3 = (f32[48,128]{1,0:T(8,128)S(1)}, f32[48,128]{1,0:T(8,128)S(1)}, u32[]{:S(2)}, u32[]{:S(2)}) collective-permute-start(f32[48,128]{1,0:T(8,128)S(1)} %get-tuple-element.20), channel_id=1, source_target_pairs={{0,4},{4,8},{8,12},{12,16},{16,20},{20,24},{24,28},{28,0},{1,5},{5... | collective-permute-start | bytes 73736 | tf_op jit(solution)/shard_map/ppermute | solution.py:726

commit v7 on v6

--- a/solution.py
+++ b/solution.py
@@ -287,6 +287,8 @@
         self.size = size
         self.paired = size & (size - 1) == 0
         self.exchanges = list(range(size // 2, size)) + list(range(1, size // 2))
+        self.passed = size == 2 * 2
+        self.direct = [k for k in self.exchanges if not (self.passed and k == size - 1)]
         near = {1, size - 1}
         self.near = [k for k in self.exchanges if any((self.target(i, k) - i) % size in near for i in range(size))]
         self.line_rows = 24
@@ -742,7 +744,9 @@
         1_000_000,
         [VMEM, VMEM, VMEM, VMEM] + [VMEM] * size,
     )(ids, z_matrix(plan.fine_depth), mean_matrix(plan.fine_depth, plan.fine_count), held, mid, *[rings[k] for k in plan.exchanges])
-    payloads = [payload] + [lax.ppermute(payload, "gy", pairs[k]) for k in plan.exchanges]
+    payloads = [payload] + [lax.ppermute(payload, "gy", pairs[k]) for k in plan.direct]
+    if plan.passed:
+        payloads.append(lax.ppermute(payloads[1], "gy", pairs[1]))
     coarse_new, fine_out = call(
         partial(outer_kernel, plan),
         (coarse_shape, held_shape),

time: 26.4 us -> 28.5 us (1.080)
  waiting for transfers between devices: 9.67 us -> 13.5 us
  starting transfers between devices: 9.95 us -> 8.18 us
    ppermute x3 -> x2, waiting for transfers between devices: 0.01 us -> 3.81 us  [step(): lax.ppermute(payload, 'gy', pairs[k])]
    ppermute x3 -> x2, starting transfers between devices: 2.2 us -> 0.43 us  [step(): lax.ppermute(payload, 'gy', pairs[k])]
  transfers between devices with their start and end apart: 8 -> 8, of which waited for: 3 -> 4; matrix products, arithmetic and copies ran while one was open for 0% -> 0% of each run, Pallas kernels for 3% -> 3%
where the time goes in v7:
time: 28.5 us; the launch traced here: 28.3 us
  waiting for transfers between devices  13.5 us (47%)
  starting transfers between devices  8.18 us (29%)
  Pallas kernels  5.28 us (19%)
  between operations  1.36 us (5%)
    ppermute x1, waiting for transfers between devices, step(): before = lax.ppermute(edges, 'gx', rise)  5 us
    ppermute x1, starting transfers between devices, step(): after = lax.ppermute(edges, 'gx', fall)  4.53 us
    ppermute x2, waiting for transfers between devices, step(): lax.ppermute(payload, 'gy', pairs[k])  3.81 us
    ppermute x3, waiting for transfers between devices, step(): lax.ppermute(buffers.get(k, mid), 'gy', pairs[k])  3.79 us
    ppermute x3, starting transfers between devices, step(): lax.ppermute(buffers.get(k, mid), 'gy', pairs[k])  3.22 us
    pallas_call x1, Pallas kernels, step(): call(partial(fine_kernel, plan, size - 1), (held_shape, shape((plan.paylo...  1.91 us
    pallas_call x1, Pallas kernels, step(): call(partial(coarse_kernel, plan), (shape((plan.ring_rows, LANES), f32),...  1.69 us
    pallas_call x1, Pallas kernels, step(): call(partial(outer_kernel, plan), (coarse_shape, held_shape), [cells, cop...  0.91 us
  transfers between devices with their start and end apart: 8, of which 4 were waited for; matrix products, arithmetic and copies ran while one was open for 0% of the time, Pallas kernels for 3%

profile of v7, /device:TPU:0, one launch (start us, length us, event | category | flops | bytes accessed | tf_op | source)
XLA Modules:
  0.0 28.3 jit_solution(292351000068903703)
XLA Ops:
  0.6 0.0 copy-start
  0.6 0.0 copy-start.1
  0.7 1.7 %shard_map.86 = (f32[48,128]{1,0:T(8,128)S(1)}, f32[48,128]{1,0:T(8,128)S(1)}, f32[32,128]{1,0:T(8,128)S(1)}, f32[1,5,32,512]{3,2,1,0:T(8,128)S(1)}, f32[5,32,25...) custom-call(s32[1,2]{1,0:T(1,128)} %site_hbm.1, f32[5,32,256]{2,1,0:T(8,128)} %c_hbm.1, ...), custom_call_target="tpu_custom_call" | custom-call | flops 4000000 | bytes 400000 | tf_op jit(solution)/shard_map/pallas_call | solution.py:711
  2.4 2.5 %collective-permute-start.1 = (f32[72,128]{1,0:T(8,128)S(1)}, f32[72,128]{1,0:T(8,128)S(1)}, u32[]{:S(2)}, u32[]{:S(2)}) collective-permute-start(f32[72,128]{1,0:T(8,128)S(1)} %get-tuple-element.17), channel_id=1, source_target_pairs={{0,3},{1,2},{2,1},{3,0},{4,7},{5,6},{6,5},{7,4},{8,11},{9,10},{10,... | collective-permute-start | bytes 110600 | tf_op jit(solution)/shard_map/ppermute | solution.py:724
  4.9 0.7 %collective-permute-start.2 = (f32[72,128]{1,0:T(8,128)S(1)}, f32[72,128]{1,0:T(8,128)S(1)}, u32[]{:S(2)}, u32[]{:S(2)}) collective-permute-start(f32[72,128]{1,0:T(8,128)S(1)} %get-tuple-element.18), channel_id=1, source_target_pairs={{0,1},{1,0},{2,3},{3,2},{4,5},{5,4},{6,7},{7,6},{8,9},{9,8},{10,11... | collective-permute-start | bytes 110600 | tf_op jit(solution)/shard_map/ppermute | solution.py:724
  5.5 0.0 collective-permute-start
  5.6 3.8 %collective-permute-done.refs_1_ = f32[48,128]{1,0:T(8,128)S(1)} collective-permute-done((f32[48,128]{1,0:T(8,128)S(1)}, f32[48,128]{1,0:T(8,128)S(1)}, u32[]{:S(2)}, u32[]{:S(2)}) %collective-permute-start) | collective-permute-done | bytes 24608 | tf_op jit(solution)/shard_map/ppermute | solution.py:724
  9.4 0.0 collective-permute-done.1.refs_2_.refs_0_
  9.4 0.0 collective-permute-done.2.refs_3_.refs_1_
  9.4 0.0 copy-done
  9.4 0.0 copy-done.1
  9.4 1.9 %shard_map.87 = (f32[1,5,32,512]{3,2,1,0:T(8,128)S(1)}, f32[112,128]{1,0:T(8,128)S(1)}) custom-call(f32[32,128]{1,0:T(8,128)S(1)} %get-tuple-element.13.ids_ref, bf16[2,256,256]{2,1,0:T(8,128)(2,1)S(1)} %copy-done.1, bf16[1024,128]{1,0:T(8,128)(2,1)S(1)} %copy-done, f32[1,5,32,512]{3,2,1,0:T(8,128)S(1)} %get-tuple-element.15.f_ref, ...), custom_call_target="tpu_custom_call" | custom-call | flops 16000000 | bytes 1000000 | tf_op jit(solution)/shard_map/pallas_call | solution.py:731
  11.3 0.4 %collective-permute-start.5 = (f32[112,128]{1,0:T(8,128)S(1)}, f32[112,128]{1,0:T(8,128)S(1)}, u32[]{:S(2)}, u32[]{:S(2)}) collective-permute-start(f32[112,128]{1,0:T(8,128)S(1)} %get-tuple-element.22.refs_0_), channel_id=1, source_target_pairs={{0,2},{1,3},{2,0},{3,1},{4,6},{5,7},{6,4},{7,5},{8,10},{9,11},{10,... | collective-permute-start | bytes 172040 | tf_op jit(solution)/shard_map/ppermute | solution.py:747
  11.7 0.0 collective-permute-start.6
  11.7 3.8 %collective-permute-done.5.refs_1_ = f32[112,128]{1,0:T(8,128)S(1)} collective-permute-done((f32[112,128]{1,0:T(8,128)S(1)}, f32[112,128]{1,0:T(8,128)S(1)}, u32[]{:S(2)}, u32[]{:S(2)}) %collective-permute-start.5) | collective-permute-done | bytes 57376 | tf_op jit(solution)/shard_map/ppermute | solution.py:747
  15.5 0.0 collective-permute-start.7
  15.5 4.5 %collective-permute-start.4 = (f32[48,128]{1,0:T(8,128)S(1)}, f32[48,128]{1,0:T(8,128)S(1)}, u32[]{:S(2)}, u32[]{:S(2)}) collective-permute-start(f32[48,128]{1,0:T(8,128)S(1)} %get-tuple-element.20), channel_id=1, source_target_pairs={{4,0},{8,4},{12,8},{16,12},{20,16},{24,20},{28,24},{0,28},{5,1},{9... | collective-permute-start | bytes 73736 | tf_op jit(solution)/shard_map/ppermute | solution.py:729
  20.1 0.0 collective-permute-start.3
  20.7 0.9 %collective-permute-done.4.after_ref = f32[48,128]{1,0:T(8,128)S(1)} collective-permute-done((f32[48,128]{1,0:T(8,128)S(1)}, f32[48,128]{1,0:T(8,128)S(1)}, u32[]{:S(2)}, u32[]{:S(2)}) %collective-permute-start.4) | collective-permute-done | bytes 24608 | tf_op jit(solution)/shard_map/ppermute | solution.py:729
  21.6 5.0 %collective-permute-done.3.before_ref = f32[48,128]{1,0:T(8,128)S(1)} collective-permute-done((f32[48,128]{1,0:T(8,128)S(1)}, f32[48,128]{1,0:T(8,128)S(1)}, u32[]{:S(2)}, u32[]{:S(2)}) %collective-permute-start.3) | collective-permute-done | bytes 24608 | tf_op jit(solution)/shard_map/ppermute | solution.py:728
  26.6 0.9 %shard_map.88 = (f32[5,32,256]{2,1,0:T(8,128)S(1)}, f32[1,5,32,512]{3,2,1,0:T(8,128)}) custom-call(s32[1]{0:T(128)S(6)} %copy.9.live_ref, f32[32,128]{1,0:T(8,128)S(1)} %get-tuple-element.13.ids_ref, f32[5,32,256]{2,1,0:T(8,128)S(1)} %get-tuple-element.14.c_ref, f32[1,5,32,512]{3,2,1,0:T(8,128)S(1)} %get-tuple-element.19.held_ref, ...), custom_call_target="tpu_custom_call" | custom-call | flops 4000000 | bytes 400000 | tf_op jit(solution)/shard_map/pallas_call | solution.py:750
  27.5 0.0 collective-permute-done.6.refs_2_
  27.5 0.0 collective-permute-done.7.refs_3_
  27.5 0.8 %shard_map.89 = f32[5,32,256]{2,1,0:T(8,128)} custom-call(s32[1]{0:T(128)S(6)} %copy.9.live_ref, f32[32,128]{1,0:T(8,128)S(1)} %get-tuple-element.13.ids_ref, f32[5,32,256]{2,1,0:T(8,128)S(1)} %get-tuple-element.21.c_ref, f32[112,128]{1,0:T(8,128)S(1)} %get-tuple-element.22.refs_0_, f32[112,128]{1,0:T(8,128)S(1)} %collective-permute-done.5.refs_1_, ...), custom_call_target="tpu_custom_call" | custom-call | flops 400000 | bytes 400000 | tf_op jit(solution)/shard_map/pallas_call | solution.py:759
Async XLA Ops:
  0.6 8.7 %copy-start = (bf16[1024,128]{1,0:T(8,128)(2,1)S(1)}, bf16[1024,128]{1,0:T(8,128)(2,1)}, u32[]{:S(2)}) copy-start(bf16[1024,128]{1,0:T(8,128)(2,1)} %constant.8.clone.mean_ref) | copy-start | bytes 786436
  0.6 8.7 %copy-start.1 = (bf16[2,256,256]{2,1,0:T(8,128)(2,1)S(1)}, bf16[2,256,256]{2,1,0:T(8,128)(2,1)}, u32[]{:S(2)}) copy-start(bf16[2,256,256]{2,1,0:T(8,128)(2,1)} %constant.7.clone.matrix_ref) | copy-start | bytes 786436
  2.4 7.0 %collective-permute-start.1 = (f32[72,128]{1,0:T(8,128)S(1)}, f32[72,128]{1,0:T(8,128)S(1)}, u32[]{:S(2)}, u32[]{:S(2)}) collective-permute-start(f32[72,128]{1,0:T(8,128)S(1)} %get-tuple-element.17), channel_id=1, source_target_pairs={{0,3},{1,2},{2,1},{3,0},{4,7},{5,6},{6,5},{7,4},{8,11},{9,10},{10,... | collective-permute-start | bytes 110600 | tf_op jit(solution)/shard_map/ppermute | solution.py:724
  4.9 4.5 %collective-permute-start.2 = (f32[72,128]{1,0:T(8,128)S(1)}, f32[72,128]{1,0:T(8,128)S(1)}, u32[]{:S(2)}, u32[]{:S(2)}) collective-permute-start(f32[72,128]{1,0:T(8,128)S(1)} %get-tuple-element.18), channel_id=1, source_target_pairs={{0,1},{1,0},{2,3},{3,2},{4,5},{5,4},{6,7},{7,6},{8,9},{9,8},{10,11... | collective-permute-start | bytes 110600 | tf_op jit(solution)/shard_map/ppermute | solution.py:724
  5.5 3.8 %collective-permute-start = (f32[48,128]{1,0:T(8,128)S(1)}, f32[48,128]{1,0:T(8,128)S(1)}, u32[]{:S(2)}, u32[]{:S(2)}) collective-permute-start(f32[48,128]{1,0:T(8,128)S(1)} %get-tuple-element.16.refs_0_), channel_id=1, source_target_pairs={{0,2},{1,3},{2,0},{3,1},{4,6},{5,7},{6,4},{7,5},{8,10},{9,11},{10,... | collective-permute-start | bytes 73736 | tf_op jit(solution)/shard_map/ppermute | solution.py:724
  11.3 4.2 %collective-permute-start.5 = (f32[112,128]{1,0:T(8,128)S(1)}, f32[112,128]{1,0:T(8,128)S(1)}, u32[]{:S(2)}, u32[]{:S(2)}) collective-permute-start(f32[112,128]{1,0:T(8,128)S(1)} %get-tuple-element.22.refs_0_), channel_id=1, source_target_pairs={{0,2},{1,3},{2,0},{3,1},{4,6},{5,7},{6,4},{7,5},{8,10},{9,11},{10,... | collective-permute-start | bytes 172040 | tf_op jit(solution)/shard_map/ppermute | solution.py:747
  11.7 15.8 %collective-permute-start.6 = (f32[112,128]{1,0:T(8,128)S(1)}, f32[112,128]{1,0:T(8,128)S(1)}, u32[]{:S(2)}, u32[]{:S(2)}) collective-permute-start(f32[112,128]{1,0:T(8,128)S(1)} %get-tuple-element.22.refs_0_), channel_id=1, source_target_pairs={{0,1},{1,0},{2,3},{3,2},{4,5},{5,4},{6,7},{7,6},{8,9},{9,8},{10,11... | collective-permute-start | bytes 172040 | tf_op jit(solution)/shard_map/ppermute | solution.py:747
  15.5 12.0 %collective-permute-start.7 = (f32[112,128]{1,0:T(8,128)S(1)}, f32[112,128]{1,0:T(8,128)S(1)}, u32[]{:S(2)}, u32[]{:S(2)}) collective-permute-start(f32[112,128]{1,0:T(8,128)S(1)} %collective-permute-done.5.refs_1_), channel_id=1, source_target_pairs={{0,1},{1,0},{2,3},{3,2},{4,5},{5,4},{6,7},{7,6},{8,9},{9,8},{10,11... | collective-permute-start | bytes 172040 | tf_op jit(solution)/shard_map/ppermute | solution.py:749
  15.5 6.1 %collective-permute-start.4 = (f32[48,128]{1,0:T(8,128)S(1)}, f32[48,128]{1,0:T(8,128)S(1)}, u32[]{:S(2)}, u32[]{:S(2)}) collective-permute-start(f32[48,128]{1,0:T(8,128)S(1)} %get-tuple-element.20), channel_id=1, source_target_pairs={{4,0},{8,4},{12,8},{16,12},{20,16},{24,20},{28,24},{0,28},{5,1},{9... | collective-permute-start | bytes 73736 | tf_op jit(solution)/shard_map/ppermute | solution.py:729
  20.1 6.5 %collective-permute-start.3 = (f32[48,128]{1,0:T(8,128)S(1)}, f32[48,128]{1,0:T(8,128)S(1)}, u32[]{:S(2)}, u32[]{:S(2)}) collective-permute-start(f32[48,128]{1,0:T(8,128)S(1)} %get-tuple-element.20), channel_id=1, source_target_pairs={{0,4},{4,8},{8,12},{12,16},{16,20},{20,24},{24,28},{28,0},{1,5},{5... | collective-permute-start | bytes 73736 | tf_op jit(solution)/shard_map/ppermute | solution.py:728
